TPU v7x, 32 devices: a whole 2x2x4 slice. The times are simulated.
32 devices in a mesh: strike: 8 (over z, core), cross: 4 (over y, x).
Axes of the slice: x: 2, y: 2, z: 4, core: 2. Of those that a mesh axis runs over, the one named last changes fastest.
Arguments:
- velocity: float32 [3, 128, 64, 256], P(None, 'strike', 'cross'), may hold values from -4 to 4
- stress: float32 [6, 128, 64, 256], P(None, 'strike', 'cross'), may hold values from -1.6 to 1.6
- buoyancy: float32 [128, 64, 256], P('strike', 'cross'), may hold values from 0.5 to 1
- lame: float32 [128, 64, 256], P('strike', 'cross'), may hold values from 0.5 to 1.2
- shear: float32 [128, 64, 256], P('strike', 'cross'), may hold values from 0.5 to 1
- fault_tile: int32 [8], replicated, may hold values from 1 to 3
- prestress: float32 [128, 256], P('strike', 'cross'), may hold values from 1.2 to 2.4
- normal_stress: float32 [128, 256], P('strike', 'cross'), may hold values from 2 to 4
- rate_a: float32 [128, 256], P('strike', 'cross'), may hold values from 0.02 to 0.04
- state: float32 [128, 256], P('strike', 'cross'), may hold values from 0.45 to 0.6
Outputs:
- velocity_out: float32 [3, 128, 64, 256], P(None, 'strike', 'cross')
- stress_out: float32 [6, 128, 64, 256], P(None, 'strike', 'cross')
- slip_rate: float32 [128, 256], P('strike', 'cross')
- state_out: float32 [128, 256], P('strike', 'cross')
Inputs may be any that keep to these rules, and one draw needn't show every extreme that they name: `fault_tile`: each strike index has its fault plane in the first row of one cross tile other than the first.
All inputs are finite; a program needn't handle non-finite values.
Results may differ from a plain program's by a relative error of at most 0.0003.
Values sent between devices are 32-bit elements; how exact they have to be, the bound alone decides.
No kernel may reach another device: no remote copies, remote signals or barrier semaphores. Data moves between devices by JAX's collectives and lax.ppermute only.
A program may use at most 64 MiB of HBM per device.

v0:
```python
import jax
import jax.numpy as jnp
from jax import lax
from jax.experimental import pallas as pl
from jax.experimental.pallas import tpu as pltpu
from jax.sharding import PartitionSpec as P

STEPS = 4
NEWTON = 8

step_ratio = 0.25
ref_rate = 0.001
evolve_rate = 1e-05
base_friction = 0.6
evolve_b = 0.03
near_weight = 27.0
unit = step_ratio / 24.0

VMEM = pl.BlockSpec(memory_space=pltpu.VMEM)
SMEM = pl.BlockSpec(memory_space=pltpu.SMEM)
PARAMS = pltpu.CompilerParams(vmem_limit_bytes=16 * 1024 * 1024)

STRESS_FACE = (((3, "b"), (4, "b"), (0, "f")), ((3, "b"), (5, "b"), (1, "f")))
VELOCITY_FACE = (((0, "b"), (1, "f"), (2, "f")), ((1, "b"), (0, "f"), (2, "f")))


def layers(kind):
    return (2, 1) if kind == "b" else (1, 2)


def combine(hi, lo, far_hi, far_lo):
    def sub(a, b):
        if a is None:
            return None if b is None else -b
        return a if b is None else a - b

    near, far = sub(hi, lo), sub(far_hi, far_lo)
    if near is None:
        return -far
    near = near_weight * near
    return near if far is None else near - far


def difference(kind, get):
    if kind == "b":
        return combine(get(0), get(-1), get(1), get(-2))
    return combine(get(1), get(0), get(2), get(-1))


def plane_shift(field, axis):
    length = field.shape[axis]
    place = lax.broadcasted_iota(jnp.int32, field.shape, axis)

    def get(k):
        if k == 0:
            return field
        rolled = pltpu.roll(field, (-k) % length, axis)
        keep = place < length - k if k > 0 else place >= -k
        return jnp.where(keep, rolled, 0.0)

    return get


def strike_shift(ref, comp, i, count):
    def get(k):
        return ref[comp, i + k] if 0 <= i + k < count else None

    return get


def add(*terms):
    return sum(terms[1:], terms[0])


def velocity_body(v_ref, s_ref, b_ref, out_ref):
    count = v_ref.shape[1]
    for i in range(count):
        gain = b_ref[i] * unit
        sxx, syy, szz, sxy, sxz, syz = (s_ref[c, i] for c in range(6))
        sxy_y, sxz_z = plane_shift(sxy, 0), plane_shift(sxz, 1)
        force = add(
            difference("f", strike_shift(s_ref, 0, i, count)),
            difference("b", sxy_y),
            difference("b", sxz_z),
        )
        out_ref[0, i] = v_ref[0, i] + gain * force
        force = add(
            difference("b", strike_shift(s_ref, 3, i, count)),
            difference("f", plane_shift(syy, 0)),
            difference("b", plane_shift(syz, 1)),
        )
        out_ref[1, i] = v_ref[1, i] + gain * force
        force = add(
            difference("b", strike_shift(s_ref, 4, i, count)),
            difference("b", plane_shift(syz, 0)),
            difference("f", plane_shift(szz, 1)),
        )
        out_ref[2, i] = v_ref[2, i] + gain * force


def stress_body(s_ref, v_ref, lame_ref, shear_ref, out_ref):
    count = s_ref.shape[1]
    for i in range(count):
        lam, mu = lame_ref[i] * unit, shear_ref[i] * unit
        vx, vy, vz = (v_ref[c, i] for c in range(3))
        ex = difference("b", strike_shift(v_ref, 0, i, count))
        ey = difference("b", plane_shift(vy, 0))
        ez = difference("b", plane_shift(vz, 1))
        spread = lam * (ex + ey + ez)
        twice = 2.0 * mu
        out_ref[0, i] = s_ref[0, i] + (spread + twice * ex)
        out_ref[1, i] = s_ref[1, i] + (spread + twice * ey)
        out_ref[2, i] = s_ref[2, i] + (spread + twice * ez)
        out_ref[3, i] = s_ref[3, i] + mu * (
            difference("f", plane_shift(vx, 0)) + difference("f", strike_shift(v_ref, 1, i, count))
        )
        out_ref[4, i] = s_ref[4, i] + mu * (
            difference("f", plane_shift(vx, 1)) + difference("f", strike_shift(v_ref, 2, i, count))
        )
        out_ref[5, i] = s_ref[5, i] + mu * (
            difference("f", plane_shift(vy, 1)) + difference("f", plane_shift(vz, 0))
        )


def row(axis, comp, i):
    return (comp, i) if axis == 0 else (comp, slice(None), i)


def mat(axis, i):
    return (i,) if axis == 0 else (slice(None), i)


def side(axis):
    name = ("strike", "cross")[axis]
    pos, size = lax.axis_index(name), lax.axis_size(name)
    return lax.rem(pos, 2) == 0, pos > 0, pos < size - 1


def pack(ref, axis, spec, a_ref, b_ref):
    even, _, _ = side(axis)
    count = ref.shape[1 + axis]
    up, down = [], []
    for comp, kind in spec:
        before, after = layers(kind)
        up += [row(axis, comp, count - before + k) for k in range(before)]
        down += [row(axis, comp, k) for k in range(after)]
    for k in range(a_ref.shape[0]):
        high = ref[up[min(k, len(up) - 1)]]
        low = ref[down[min(k, len(down) - 1)]]
        a_ref[k] = lax.select(even, high, low)
        b_ref[k] = lax.select(even, low, high)


def halo_terms(axis, spec, count, a_ref, b_ref):
    even, has_before, has_after = side(axis)
    terms = []
    at_before, at_after = 0, 0
    for comp, kind in spec:
        before, after = layers(kind)
        head, tail = [], []
        for k in range(before):
            j = at_before + k
            value = lax.select(even, b_ref[j], a_ref[j])
            head.append(lax.select(has_before, value, jnp.zeros_like(value)))
        for k in range(after):
            j = at_after + k
            value = lax.select(even, a_ref[j], b_ref[j])
            tail.append(lax.select(has_after, value, jnp.zeros_like(value)))
        at_before, at_after = at_before + before, at_after + after
        if kind == "b":
            update = {0: head[0] - near_weight * head[1], 1: head[1], count - 1: -tail[0]}
        else:
            update = {0: head[0], count - 2: -tail[0], count - 1: near_weight * tail[0] - tail[1]}
        terms.append(update)
    return terms


def velocity_edge_body(v_ref, b_ref, xa, xb, ya, yb, out_ref, *packs):
    for axis, a_ref, b_ref2 in ((0, xa, xb), (1, ya, yb)):
        count = v_ref.shape[1 + axis]
        terms = halo_terms(axis, STRESS_FACE[axis], count, a_ref, b_ref2)
        targets = (1, 2, 0) if axis == 0 else (0, 2, 1)
        for target, update in zip(targets, terms):
            for i, value in update.items():
                at = row(axis, target, i)
                out_ref[at] = out_ref[at] + (b_ref[mat(axis, i)] * unit) * value
    if packs:
        for axis in (0, 1):
            pack(out_ref, axis, VELOCITY_FACE[axis], *packs[2 * axis : 2 * axis + 2])


def inverse_sinh(value):
    magnitude = jnp.abs(value)
    grown = jnp.log(magnitude + jnp.sqrt(magnitude * magnitude + 1.0))
    return jnp.where(value < 0.0, -grown, grown)


def friction(trial, damping, prestress, normal_stress, rate_a, state):
    total = trial + prestress
    width = 2.0 * ref_rate * jnp.exp(-state / rate_a)
    strength = rate_a * normal_stress
    drag = damping * width
    scaled = inverse_sinh(total / drag)
    for iteration in range(NEWTON):
        grow, decay = 0.5 * jnp.exp(scaled), 0.5 * jnp.exp(-scaled)
        residual = strength * scaled + drag * (grow - decay) - total
        slope = strength + drag * (grow + decay)
        scaled = scaled - residual / slope
    slip = width * (0.5 * jnp.exp(scaled) - 0.5 * jnp.exp(-scaled))
    traction = total - damping * slip
    evolved = state + evolve_rate * (
        jnp.exp((base_friction - state) / evolve_b) - jnp.abs(slip) / ref_rate
    )
    return (traction - prestress, slip, evolved)


def stress_edge_body(
    tile_ref, s_ref, lame_ref, shear_ref, b_ref, fault_ref, state_ref, xa, xb, ya, yb,
    out_ref, slip_ref, evolved_ref, *packs
):
    for axis, a_ref, b_ref2 in ((0, xa, xb), (1, ya, yb)):
        count = s_ref.shape[1 + axis]
        terms = halo_terms(axis, VELOCITY_FACE[axis], count, a_ref, b_ref2)
        for i, value in terms[0].items():
            lam, mu = lame_ref[mat(axis, i)] * unit, shear_ref[mat(axis, i)] * unit
            spread = lam * value
            for comp in range(3):
                at = row(axis, comp, i)
                more = spread + 2.0 * mu * value if comp == axis else spread
                out_ref[at] = out_ref[at] + more
        targets = (3, 4) if axis == 0 else (3, 5)
        for target, update in zip(targets, terms[1:]):
            for i, value in update.items():
                at = row(axis, target, i)
                out_ref[at] = out_ref[at] + (shear_ref[mat(axis, i)] * unit) * value
    is_owner = tile_ref[lax.axis_index("strike")] == lax.axis_index("cross")
    first = row(1, 3, 0)
    trial = out_ref[first]
    damping = 0.5 * jnp.sqrt(shear_ref[:, 0] / b_ref[:, 0])
    change, slip, evolved = friction(
        trial, damping, fault_ref[0], fault_ref[1], fault_ref[2], state_ref[...]
    )
    out_ref[first] = lax.select(is_owner, change, trial)
    slip_ref[...] = slip
    evolved_ref[...] = evolved
    if packs:
        for axis in (0, 1):
            pack(out_ref, axis, STRESS_FACE[axis], *packs[2 * axis : 2 * axis + 2])


def pack_body(s_ref, *packs):
    for axis in (0, 1):
        pack(s_ref, axis, STRESS_FACE[axis], *packs[2 * axis : 2 * axis + 2])


def swaps(pairs):
    return [p for i, j in pairs for p in ((i, j), (j, i))]


def exchange_pairs(n_strike, n_cross):
    def at(s, c):
        return s * n_cross + c

    strike_a = [(at(s, c), at(s + 1, c)) for s in range(0, n_strike - 1, 2) for c in range(n_cross)]
    strike_b = [(at(s, c), at(s + 1, c)) for s in range(1, n_strike - 1, 2) for c in range(n_cross)]
    cross_a = [(at(s, c), at(s, c + 1)) for s in range(n_strike) for c in range(0, n_cross - 1, 2)]
    cross_b = [(at(s, c), at(s, c + 1)) for s in range(n_strike) for c in range(1, n_cross - 1, 2)]
    half = n_cross // 2
    for s in (0, n_strike - 1):
        strike_b += [(at(s, c), at(s, c + half)) for c in range(half)]
    for c in (0, n_cross - 1):
        cross_b += [(at(s, c), at(s + 1, c)) for s in range(0, n_strike - 1, 2)]
    return tuple(swaps(p) for p in (strike_a, strike_b, cross_a, cross_b))


def local(
    velocity, stress, buoyancy, lame, shear, fault_tile, prestress, normal_stress, rate_a, state
):
    n_strike, n_cross = lax.axis_size("strike"), lax.axis_size("cross")
    axes = ("strike", "cross")
    strike_pos, cross_pos = lax.axis_index("strike"), lax.axis_index("cross")
    strike_a, strike_b, cross_a, cross_b = exchange_pairs(n_strike, n_cross)
    _, nx, ny, nz = velocity.shape
    bz = prestress.shape[1]
    f32 = jnp.float32
    thick = 5
    vec = lambda *shape: jax.ShapeDtypeStruct(shape, f32)
    faces = (vec(thick, ny, nz), vec(thick, ny, nz), vec(thick, nx, nz), vec(thick, nx, nz))
    like_v, like_s = vec(*velocity.shape), vec(*stress.shape)
    plane = vec(nx, nz)

    def call(body, ins, outs, alias=None, smem=0, name=None):
        return pl.pallas_call(
            body,
            in_specs=[SMEM] * smem + [VMEM] * (len(ins) - smem),
            out_specs=[VMEM] * len(outs),
            out_shape=list(outs),
            input_output_aliases={} if alias is None else {alias: 0},
            compiler_params=PARAMS,
            name=name,
        )(*ins)

    def exchange(packs):
        xa, xb, ya, yb = packs
        yb = lax.ppermute(yb, axes, cross_b)
        ya = lax.ppermute(ya, axes, cross_a)
        xb = lax.ppermute(xb, axes, strike_b)
        xa = lax.ppermute(xa, axes, strike_a)
        return xa, xb, ya, yb

    def partner(block, r):
        pairs = [(s * n_cross + c, s * n_cross + (c ^ r)) for s in range(n_strike) for c in range(n_cross)]
        return lax.ppermute(block, axes, pairs)

    packs = call(pack_body, (stress,), faces, name="pack")
    own = jnp.concatenate([prestress, normal_stress, rate_a, state], axis=1)
    blocks = jnp.stack([own] + [partner(own, r) for r in range(1, n_cross)])
    blocks = jnp.take(blocks, jnp.arange(n_cross) ^ cross_pos, axis=0)
    fault = blocks.reshape(n_cross, nx, 4, bz).transpose(2, 1, 0, 3).reshape(4, nx, nz)
    fault_state = fault[3]

    for iteration in range(STEPS):
        halos = exchange(packs)
        (velocity,) = call(velocity_body, (velocity, stress, buoyancy), (like_v,), 0, name="velocity")
        velocity, *packs = call(
            velocity_edge_body, (velocity, buoyancy, *halos), (like_v, *faces), 0, name="velocity_edge"
        )
        halos = exchange(packs)
        (stress,) = call(stress_body, (stress, velocity, lame, shear), (like_s,), 0, name="stress")
        outs = (like_s, plane, plane) + (faces if iteration < STEPS - 1 else ())
        stress, slip, fault_state, *packs = call(
            stress_edge_body,
            (fault_tile, stress, lame, shear, buoyancy, fault, fault_state, *halos),
            outs, 1, smem=1, name="stress_edge",
        )

    both = jnp.stack([slip, fault_state])
    owner = fault_tile[strike_pos]
    result = jnp.zeros((2, nx, bz), f32)
    for r in range(n_cross):
        target = cross_pos ^ r
        part = lax.dynamic_slice_in_dim(both, target * bz, bz, axis=2)
        got = part if r == 0 else partner(part, r)
        result = jnp.where(owner == target, got, result)
    return (velocity, stress, result[0], result[1])


def solution(mesh):
    in_specs = (
        P(None, "strike", "cross", None),
        P(None, "strike", "cross", None),
        P("strike", "cross", None),
        P("strike", "cross", None),
        P("strike", "cross", None),
        P(),
        P("strike", "cross"),
        P("strike", "cross"),
        P("strike", "cross"),
        P("strike", "cross"),
    )
    out_specs = (
        P(None, "strike", "cross", None),
        P(None, "strike", "cross", None),
        P("strike", "cross"),
        P("strike", "cross"),
    )
    return jax.shard_map(local, mesh=mesh, in_specs=in_specs, out_specs=out_specs, check_vma=False)
```

profile of v0, /device:TPU:0, one launch (start us, length us, event | category | flops | bytes accessed | tf_op | source)
XLA Modules:
  0.0 106.2 jit_solution(7173477220871622608)
XLA Ops:
  0.7 1.5 %copy.53.s_ref = f32[6,16,16,256]{3,2,1,0:T(8,128)S(1)} copy(f32[6,16,16,256]{3,2,1,0:T(8,128)} %param.11) | data formatting | bytes 3145728
  3.2 3.0 %collective-permute-start.4 = (f32[16,256]{1,0:T(8,128)S(1)}, f32[16,256]{1,0:T(8,128)S(1)}, u32[]{:S(2)}, u32[]{:S(2)}) collective-permute-start(f32[16,256]{1,0:T(8,128)S(1)} %pad_maximum_fusion.1), channel_id=1, source_target_pairs={{0,1},{1,0},{2,3},{3,2},{4,5},{5,4},{6,7},{7,6},{8,9},{9,8},{10,11... | collective-permute-start | bytes 49160 | tf_op jit(solution)/shard_map/ppermute | solution.py:313
  6.2 1.5 %collective-permute-start.5 = (f32[16,256]{1,0:T(8,128)S(1)}, f32[16,256]{1,0:T(8,128)S(1)}, u32[]{:S(2)}, u32[]{:S(2)}) collective-permute-start(f32[16,256]{1,0:T(8,128)S(1)} %pad_maximum_fusion.1), channel_id=1, source_target_pairs={{0,2},{1,3},{2,0},{3,1},{4,6},{5,7},{6,4},{7,5},{8,10},{9,11},{10,... | collective-permute-start | bytes 49160 | tf_op jit(solution)/shard_map/ppermute | solution.py:313
  7.9 2.0 %collective-permute-start.1 = (f32[5,16,256]{2,1,0:T(8,128)S(1)}, f32[5,16,256]{2,1,0:T(8,128)S(1)}, u32[]{:S(2)}, u32[]{:S(2)}) collective-permute-start(f32[5,16,256]{2,1,0:T(8,128)S(1)} %get-tuple-element.50), channel_id=1, source_target_pairs={{4,8},{8,4},{5,9},{9,5},{6,10},{10,6},{7,11},{11,7},{12,16},{16,12... | collective-permute-start | bytes 245768 | tf_op jit(solution)/shard_map/ppermute | solution.py:307
  10.0 2.8 %velocity.4.v_ref = f32[3,16,16,256]{3,2,1,0:T(8,128)} custom-call(f32[3,16,16,256]{3,2,1,0:T(8,128)} %copy.52.v_ref, f32[6,16,16,256]{3,2,1,0:T(8,128)S(1)} %copy.53.s_ref, f32[16,16,256]{2,1,0:T(8,128)S(1)} %copy-done.8), custom_call_target="tpu_custom_call", output_to_operand_aliasing={{}: (0, {})} | custom-call | tf_op jit(solution)/shard_map/velocity/pallas_call | solution.py:293
  12.8 1.6 %collective-permute-start.2 = (f32[5,16,256]{2,1,0:T(8,128)S(1)}, f32[5,16,256]{2,1,0:T(8,128)S(1)}, u32[]{:S(2)}, u32[]{:S(2)}) collective-permute-start(f32[5,16,256]{2,1,0:T(8,128)S(1)} %get-tuple-element.51), channel_id=1, source_target_pairs={{0,1},{1,0},{2,3},{3,2},{4,5},{5,4},{6,7},{7,6},{8,9},{9,8},{10,11... | collective-permute-start | bytes 245768 | tf_op jit(solution)/shard_map/ppermute | solution.py:306
  15.1 2.3 %collective-permute-done.2.ya = f32[5,16,256]{2,1,0:T(8,128)S(1)} collective-permute-done((f32[5,16,256]{2,1,0:T(8,128)S(1)}, f32[5,16,256]{2,1,0:T(8,128)S(1)}, u32[]{:S(2)}, u32[]{:S(2)}) %collective-permute-start.2) | collective-permute-done | bytes 81952 | tf_op jit(solution)/shard_map/ppermute | solution.py:306
  17.4 2.3 %velocity_edge.4 = (f32[3,16,16,256]{3,2,1,0:T(8,128)}, f32[5,16,256]{2,1,0:T(8,128)S(1)}, f32[5,16,256]{2,1,0:T(8,128)S(1)}, f32[5,16,256]{2,1,0:T(8,128)S(1)}, f32[5,16,256]{2,1,0:T(8,128)S(1)}) custom-call(f32[3,16,16,256]{3,2,1,0:T(8,128)} %velocity.4.v_ref, f32[16,16,256]{2,1,0:T(8,128)S(1)} %copy-done.8, ...), custom_call_target="tpu_custom_call", output_to_operand_aliasing={{0}: (0, {})} | custom-call | tf_op jit(solution)/shard_map/velocity_edge/pallas_call | solution.py:293
  20.2 4.7 %collective-permute-start.8 = (f32[5,16,256]{2,1,0:T(8,128)S(1)}, f32[5,16,256]{2,1,0:T(8,128)S(1)}, u32[]{:S(2)}, u32[]{:S(2)}) collective-permute-start(f32[5,16,256]{2,1,0:T(8,128)S(1)} %get-tuple-element.55), channel_id=1, source_target_pairs={{4,8},{8,4},{5,9},{9,5},{6,10},{10,6},{7,11},{11,7},{12,16},{16,12... | collective-permute-start | bytes 245768 | tf_op jit(solution)/shard_map/ppermute | solution.py:307
  26.4 3.5 %stress.4.s_ref = f32[6,16,16,256]{3,2,1,0:T(8,128)} custom-call(f32[6,16,16,256]{3,2,1,0:T(8,128)} %copy-done, f32[3,16,16,256]{3,2,1,0:T(8,128)S(1)} %copy-done.4, f32[16,16,256]{2,1,0:T(8,128)S(1)} %copy-done.9, f32[16,16,256]{2,1,0:T(8,128)S(1)} %copy-done.10), custom_call_target="tpu_custom_call", output_to_operand_aliasing={{}: (0, {})} | custom-call | tf_op jit(solution)/shard_map/stress/pallas_call | solution.py:293
  29.9 3.2 %stress_edge.4 = (f32[6,16,16,256]{3,2,1,0:T(8,128)}, f32[16,256]{1,0:T(8,128)}, f32[16,256]{1,0:T(8,128)S(1)}, f32[5,16,256]{2,1,0:T(8,128)S(1)}, f32[5,16,256]...) custom-call(s32[8]{0:T(128)S(1)} %copy-done.11, ...), custom_call_target="tpu_custom_call", output_to_operand_aliasing={{0}: (1, {})} | custom-call | tf_op jit(solution)/shard_map/stress_edge/pallas_call | solution.py:293
  35.0 1.5 %collective-permute-start.13 = (f32[5,16,256]{2,1,0:T(8,128)S(1)}, f32[5,16,256]{2,1,0:T(8,128)S(1)}, u32[]{:S(2)}, u32[]{:S(2)}) collective-permute-start(f32[5,16,256]{2,1,0:T(8,128)S(1)} %get-tuple-element.61), channel_id=1, source_target_pairs={{0,1},{1,0},{2,3},{3,2},{4,5},{5,4},{6,7},{7,6},{8,9},{9,8},{10,11... | collective-permute-start | bytes 245768 | tf_op jit(solution)/shard_map/ppermute | solution.py:306
  36.5 1.4 %copy-done.1 = f32[6,16,16,256]{3,2,1,0:T(8,128)S(1)} copy-done((f32[6,16,16,256]{3,2,1,0:T(8,128)S(1)}, f32[6,16,16,256]{3,2,1,0:T(8,128)}, u32[]{:S(2)}) %copy-start.1) | copy-done | bytes 1572888
  37.9 2.8 %velocity.5.v_ref = f32[3,16,16,256]{3,2,1,0:T(8,128)} custom-call(f32[3,16,16,256]{3,2,1,0:T(8,128)} %get-tuple-element.53.v_ref, f32[6,16,16,256]{3,2,1,0:T(8,128)S(1)} %copy-done.1, f32[16,16,256]{2,1,0:T(8,128)S(1)} %copy-done.8), custom_call_target="tpu_custom_call", output_to_operand_aliasing={{}: (0, {})} | custom-call | tf_op jit(solution)/shard_map/velocity/pallas_call | solution.py:293
  40.8 2.3 %velocity_edge.5 = (f32[3,16,16,256]{3,2,1,0:T(8,128)}, f32[5,16,256]{2,1,0:T(8,128)S(1)}, f32[5,16,256]{2,1,0:T(8,128)S(1)}, f32[5,16,256]{2,1,0:T(8,128)S(1)}, f32[5,16,256]{2,1,0:T(8,128)S(1)}) custom-call(f32[3,16,16,256]{3,2,1,0:T(8,128)} %velocity.5.v_ref, f32[16,16,256]{2,1,0:T(8,128)S(1)} %copy-done.8, ...), custom_call_target="tpu_custom_call", output_to_operand_aliasing={{0}: (0, {})} | custom-call | tf_op jit(solution)/shard_map/velocity_edge/pallas_call | solution.py:293
  43.5 2.3 %collective-permute-start.16 = (f32[5,16,256]{2,1,0:T(8,128)S(1)}, f32[5,16,256]{2,1,0:T(8,128)S(1)}, u32[]{:S(2)}, u32[]{:S(2)}) collective-permute-start(f32[5,16,256]{2,1,0:T(8,128)S(1)} %get-tuple-element.66), channel_id=1, source_target_pairs={{4,8},{8,4},{5,9},{9,5},{6,10},{10,6},{7,11},{11,7},{12,16},{16,12... | collective-permute-start | bytes 245768 | tf_op jit(solution)/shard_map/ppermute | solution.py:307
  47.9 3.5 %stress.5.s_ref = f32[6,16,16,256]{3,2,1,0:T(8,128)} custom-call(f32[6,16,16,256]{3,2,1,0:T(8,128)} %get-tuple-element.58.s_ref, f32[3,16,16,256]{3,2,1,0:T(8,128)S(1)} %copy-done.5, f32[16,16,256]{2,1,0:T(8,128)S(1)} %copy-done.9, f32[16,16,256]{2,1,0:T(8,128)S(1)} %copy-done.10), custom_call_target="tpu_custom_call", output_to_operand_aliasing={{}: (0, {})} | custom-call | tf_op jit(solution)/shard_map/stress/pallas_call | solution.py:293
  51.4 3.2 %stress_edge.5 = (f32[6,16,16,256]{3,2,1,0:T(8,128)}, f32[16,256]{1,0:T(8,128)}, f32[16,256]{1,0:T(8,128)S(1)}, f32[5,16,256]{2,1,0:T(8,128)S(1)}, f32[5,16,256]...) custom-call(s32[8]{0:T(128)S(1)} %copy-done.11, ...), custom_call_target="tpu_custom_call", output_to_operand_aliasing={{0}: (1, {})} | custom-call | tf_op jit(solution)/shard_map/stress_edge/pallas_call | solution.py:293
  54.6 2.5 %collective-permute-start.20 = (f32[5,16,256]{2,1,0:T(8,128)S(1)}, f32[5,16,256]{2,1,0:T(8,128)S(1)}, u32[]{:S(2)}, u32[]{:S(2)}) collective-permute-start(f32[5,16,256]{2,1,0:T(8,128)S(1)} %get-tuple-element.71), channel_id=1, source_target_pairs={{4,8},{8,4},{5,9},{9,5},{6,10},{10,6},{7,11},{11,7},{12,16},{16,12... | collective-permute-start | bytes 245768 | tf_op jit(solution)/shard_map/ppermute | solution.py:307
  58.9 2.8 %velocity.6.v_ref = f32[3,16,16,256]{3,2,1,0:T(8,128)} custom-call(f32[3,16,16,256]{3,2,1,0:T(8,128)} %get-tuple-element.63.v_ref, f32[6,16,16,256]{3,2,1,0:T(8,128)S(1)} %copy-done.2, f32[16,16,256]{2,1,0:T(8,128)S(1)} %copy-done.8), custom_call_target="tpu_custom_call", output_to_operand_aliasing={{}: (0, {})} | custom-call | tf_op jit(solution)/shard_map/velocity/pallas_call | solution.py:293
  61.8 2.3 %velocity_edge.6 = (f32[3,16,16,256]{3,2,1,0:T(8,128)}, f32[5,16,256]{2,1,0:T(8,128)S(1)}, f32[5,16,256]{2,1,0:T(8,128)S(1)}, f32[5,16,256]{2,1,0:T(8,128)S(1)}, f32[5,16,256]{2,1,0:T(8,128)S(1)}) custom-call(f32[3,16,16,256]{3,2,1,0:T(8,128)} %velocity.6.v_ref, f32[16,16,256]{2,1,0:T(8,128)S(1)} %copy-done.8, ...), custom_call_target="tpu_custom_call", output_to_operand_aliasing={{0}: (0, {})} | custom-call | tf_op jit(solution)/shard_map/velocity_edge/pallas_call | solution.py:293
  64.4 2.7 %collective-permute-start.24 = (f32[5,16,256]{2,1,0:T(8,128)S(1)}, f32[5,16,256]{2,1,0:T(8,128)S(1)}, u32[]{:S(2)}, u32[]{:S(2)}) collective-permute-start(f32[5,16,256]{2,1,0:T(8,128)S(1)} %get-tuple-element.77), channel_id=1, source_target_pairs={{4,8},{8,4},{5,9},{9,5},{6,10},{10,6},{7,11},{11,7},{12,16},{16,12... | collective-permute-start | bytes 245768 | tf_op jit(solution)/shard_map/ppermute | solution.py:307
  68.7 3.5 %stress.6.s_ref = f32[6,16,16,256]{3,2,1,0:T(8,128)} custom-call(f32[6,16,16,256]{3,2,1,0:T(8,128)} %get-tuple-element.69.s_ref, f32[3,16,16,256]{3,2,1,0:T(8,128)S(1)} %copy-done.6, f32[16,16,256]{2,1,0:T(8,128)S(1)} %copy-done.9, f32[16,16,256]{2,1,0:T(8,128)S(1)} %copy-done.10), custom_call_target="tpu_custom_call", output_to_operand_aliasing={{}: (0, {})} | custom-call | tf_op jit(solution)/shard_map/stress/pallas_call | solution.py:293
  72.2 3.2 %stress_edge.6 = (f32[6,16,16,256]{3,2,1,0:T(8,128)}, f32[16,256]{1,0:T(8,128)}, f32[16,256]{1,0:T(8,128)S(1)}, f32[5,16,256]{2,1,0:T(8,128)S(1)}, f32[5,16,256]...) custom-call(s32[8]{0:T(128)S(1)} %copy-done.11, ...), custom_call_target="tpu_custom_call", output_to_operand_aliasing={{0}: (1, {})} | custom-call | tf_op jit(solution)/shard_map/stress_edge/pallas_call | solution.py:293
  75.7 2.8 %collective-permute-start.28 = (f32[5,16,256]{2,1,0:T(8,128)S(1)}, f32[5,16,256]{2,1,0:T(8,128)S(1)}, u32[]{:S(2)}, u32[]{:S(2)}) collective-permute-start(f32[5,16,256]{2,1,0:T(8,128)S(1)} %get-tuple-element.82), channel_id=1, source_target_pairs={{4,8},{8,4},{5,9},{9,5},{6,10},{10,6},{7,11},{11,7},{12,16},{16,12... | collective-permute-start | bytes 245768 | tf_op jit(solution)/shard_map/ppermute | solution.py:307
  80.3 3.0 %velocity.7.v_ref = f32[3,16,16,256]{3,2,1,0:T(8,128)} custom-call(f32[3,16,16,256]{3,2,1,0:T(8,128)} %get-tuple-element.74.v_ref, f32[6,16,16,256]{3,2,1,0:T(8,128)S(1)} %copy-done.3, f32[16,16,256]{2,1,0:T(8,128)S(1)} %copy-done.8), custom_call_target="tpu_custom_call", output_to_operand_aliasing={{}: (0, {})} | custom-call | tf_op jit(solution)/shard_map/velocity/pallas_call | solution.py:293
  83.3 2.3 %velocity_edge.7 = (f32[3,16,16,256]{3,2,1,0:T(8,128)}, f32[5,16,256]{2,1,0:T(8,128)S(1)}, f32[5,16,256]{2,1,0:T(8,128)S(1)}, f32[5,16,256]{2,1,0:T(8,128)S(1)}, f32[5,16,256]{2,1,0:T(8,128)S(1)}) custom-call(f32[3,16,16,256]{3,2,1,0:T(8,128)} %velocity.7.v_ref, f32[16,16,256]{2,1,0:T(8,128)S(1)} %copy-done.8, ...), custom_call_target="tpu_custom_call", output_to_operand_aliasing={{0}: (0, {})} | custom-call | tf_op jit(solution)/shard_map/velocity_edge/pallas_call | solution.py:293
  85.9 2.7 %collective-permute-start.32 = (f32[5,16,256]{2,1,0:T(8,128)S(1)}, f32[5,16,256]{2,1,0:T(8,128)S(1)}, u32[]{:S(2)}, u32[]{:S(2)}) collective-permute-start(f32[5,16,256]{2,1,0:T(8,128)S(1)} %get-tuple-element.88), channel_id=1, source_target_pairs={{4,8},{8,4},{5,9},{9,5},{6,10},{10,6},{7,11},{11,7},{12,16},{16,12... | collective-permute-start | bytes 245768 | tf_op jit(solution)/shard_map/ppermute | solution.py:307
  90.2 3.5 %stress.7.s_ref = f32[6,16,16,256]{3,2,1,0:T(8,128)} custom-call(f32[6,16,16,256]{3,2,1,0:T(8,128)} %get-tuple-element.80.s_ref, f32[3,16,16,256]{3,2,1,0:T(8,128)S(1)} %copy-done.7, f32[16,16,256]{2,1,0:T(8,128)S(1)} %copy-done.9, f32[16,16,256]{2,1,0:T(8,128)S(1)} %copy-done.10), custom_call_target="tpu_custom_call", output_to_operand_aliasing={{}: (0, {})} | custom-call | tf_op jit(solution)/shard_map/stress/pallas_call | solution.py:293
  93.7 3.2 %stress_edge.7 = (f32[6,16,16,256]{3,2,1,0:T(8,128)}, f32[16,256]{1,0:T(8,128)S(1)}, f32[16,256]{1,0:T(8,128)S(1)}) custom-call(s32[8]{0:T(128)S(1)} %copy-done.11, f32[6,16,16,256]{3,2,1,0:T(8,128)} %stress.7.s_ref, f32[16,16,256]{2,1,0:T(8,128)S(1)} %copy-done.9, f32[16,16,256]{2,1,0:T(8,128)S(1)} %copy-done.10, ...), custom_call_target="tpu_custom_call", output_to_operand_aliasing={{0}: (1, {})} | custom-call | tf_op jit(solution)/shard_map/stress_edge/pallas_call | solution.py:293
  97.0 1.5 %collective-permute-start.35 = (f32[2,16,64]{2,1,0:T(8,128)S(1)}, f32[2,16,64]{2,1,0:T(8,128)S(1)}, u32[]{:S(2)}, u32[]{:S(2)}) collective-permute-start(f32[2,16,64]{2,1,0:T(8,128)S(1)} %get-tuple-element.95), channel_id=1, source_target_pairs={{0,3},{1,2},{2,1},{3,0},{4,7},{5,6},{6,5},{7,4},{8,11},{9,10},{10,... | collective-permute-start | bytes 24584 | tf_op jit(solution)/shard_map/ppermute | solution.py:313
  98.4 3.3 %collective-permute-start.36 = (f32[2,16,64]{2,1,0:T(8,128)S(1)}, f32[2,16,64]{2,1,0:T(8,128)S(1)}, u32[]{:S(2)}, u32[]{:S(2)}) collective-permute-start(f32[2,16,64]{2,1,0:T(8,128)S(1)} %get-tuple-element.96), channel_id=1, source_target_pairs={{0,2},{1,3},{2,0},{3,1},{4,6},{5,7},{6,4},{7,5},{8,10},{9,11},{10,... | collective-permute-start | bytes 24584 | tf_op jit(solution)/shard_map/ppermute | solution.py:313
  (112 shorter events, 18.1 us)
Async XLA Ops:
  3.2 9.6 %collective-permute-start.4 = (f32[16,256]{1,0:T(8,128)S(1)}, f32[16,256]{1,0:T(8,128)S(1)}, u32[]{:S(2)}, u32[]{:S(2)}) collective-permute-start(f32[16,256]{1,0:T(8,128)S(1)} %pad_maximum_fusion.1), channel_id=1, source_target_pairs={{0,1},{1,0},{2,3},{3,2},{4,5},{5,4},{6,7},{7,6},{8,9},{9,8},{10,11... | collective-permute-start | bytes 49160 | tf_op jit(solution)/shard_map/ppermute | solution.py:313
  6.2 8.2 %collective-permute-start.5 = (f32[16,256]{1,0:T(8,128)S(1)}, f32[16,256]{1,0:T(8,128)S(1)}, u32[]{:S(2)}, u32[]{:S(2)}) collective-permute-start(f32[16,256]{1,0:T(8,128)S(1)} %pad_maximum_fusion.1), channel_id=1, source_target_pairs={{0,2},{1,3},{2,0},{3,1},{4,6},{5,7},{6,4},{7,5},{8,10},{9,11},{10,... | collective-permute-start | bytes 49160 | tf_op jit(solution)/shard_map/ppermute | solution.py:313
  7.7 6.7 %collective-permute-start.6 = (f32[16,256]{1,0:T(8,128)S(1)}, f32[16,256]{1,0:T(8,128)S(1)}, u32[]{:S(2)}, u32[]{:S(2)}) collective-permute-start(f32[16,256]{1,0:T(8,128)S(1)} %pad_maximum_fusion.1), channel_id=1, source_target_pairs={{0,3},{1,2},{2,1},{3,0},{4,7},{5,6},{6,5},{7,4},{8,11},{9,10},{10,... | collective-permute-start | bytes 49160 | tf_op jit(solution)/shard_map/ppermute | solution.py:313
  7.8 7.2 %collective-permute-start = (f32[5,16,256]{2,1,0:T(8,128)S(1)}, f32[5,16,256]{2,1,0:T(8,128)S(1)}, u32[]{:S(2)}, u32[]{:S(2)}) collective-permute-start(f32[5,16,256]{2,1,0:T(8,128)S(1)} %get-tuple-element.49), channel_id=1, source_target_pairs={{0,4},{4,0},{1,5},{5,1},{2,6},{6,2},{3,7},{7,3},{8,12},{12,8},{9,1... | collective-permute-start | bytes 245768 | tf_op jit(solution)/shard_map/ppermute | solution.py:308
  7.9 7.2 %collective-permute-start.1 = (f32[5,16,256]{2,1,0:T(8,128)S(1)}, f32[5,16,256]{2,1,0:T(8,128)S(1)}, u32[]{:S(2)}, u32[]{:S(2)}) collective-permute-start(f32[5,16,256]{2,1,0:T(8,128)S(1)} %get-tuple-element.50), channel_id=1, source_target_pairs={{4,8},{8,4},{5,9},{9,5},{6,10},{10,6},{7,11},{11,7},{12,16},{16,12... | collective-permute-start | bytes 245768 | tf_op jit(solution)/shard_map/ppermute | solution.py:307
  19.7 10.2 %collective-permute-start.10 = (f32[5,16,256]{2,1,0:T(8,128)S(1)}, f32[5,16,256]{2,1,0:T(8,128)S(1)}, u32[]{:S(2)}, u32[]{:S(2)}) collective-permute-start(f32[5,16,256]{2,1,0:T(8,128)S(1)} %get-tuple-element.57), channel_id=1, source_target_pairs={{1,2},{2,1},{5,6},{6,5},{9,10},{10,9},{13,14},{14,13},{17,18},{18,... | collective-permute-start | bytes 245768 | tf_op jit(solution)/shard_map/ppermute | solution.py:305
  19.7 10.2 %collective-permute-start.7 = (f32[5,16,256]{2,1,0:T(8,128)S(1)}, f32[5,16,256]{2,1,0:T(8,128)S(1)}, u32[]{:S(2)}, u32[]{:S(2)}) collective-permute-start(f32[5,16,256]{2,1,0:T(8,128)S(1)} %get-tuple-element.54), channel_id=1, source_target_pairs={{0,4},{4,0},{1,5},{5,1},{2,6},{6,2},{3,7},{7,3},{8,12},{12,8},{9,1... | collective-permute-start | bytes 245768 | tf_op jit(solution)/shard_map/ppermute | solution.py:308
  20.2 9.7 %collective-permute-start.8 = (f32[5,16,256]{2,1,0:T(8,128)S(1)}, f32[5,16,256]{2,1,0:T(8,128)S(1)}, u32[]{:S(2)}, u32[]{:S(2)}) collective-permute-start(f32[5,16,256]{2,1,0:T(8,128)S(1)} %get-tuple-element.55), channel_id=1, source_target_pairs={{4,8},{8,4},{5,9},{9,5},{6,10},{10,6},{7,11},{11,7},{12,16},{16,12... | collective-permute-start | bytes 245768 | tf_op jit(solution)/shard_map/ppermute | solution.py:307
  24.9 5.0 %collective-permute-start.9 = (f32[5,16,256]{2,1,0:T(8,128)S(1)}, f32[5,16,256]{2,1,0:T(8,128)S(1)}, u32[]{:S(2)}, u32[]{:S(2)}) collective-permute-start(f32[5,16,256]{2,1,0:T(8,128)S(1)} %get-tuple-element.56), channel_id=1, source_target_pairs={{0,1},{1,0},{2,3},{3,2},{4,5},{5,4},{6,7},{7,6},{8,9},{9,8},{10,11... | collective-permute-start | bytes 245768 | tf_op jit(solution)/shard_map/ppermute | solution.py:306
  33.1 7.6 %collective-permute-start.11 = (f32[5,16,256]{2,1,0:T(8,128)S(1)}, f32[5,16,256]{2,1,0:T(8,128)S(1)}, u32[]{:S(2)}, u32[]{:S(2)}) collective-permute-start(f32[5,16,256]{2,1,0:T(8,128)S(1)} %get-tuple-element.59), channel_id=1, source_target_pairs={{0,4},{4,0},{1,5},{5,1},{2,6},{6,2},{3,7},{7,3},{8,12},{12,8},{9,1... | collective-permute-start | bytes 245768 | tf_op jit(solution)/shard_map/ppermute | solution.py:308
  34.4 6.4 %collective-permute-start.12 = (f32[5,16,256]{2,1,0:T(8,128)S(1)}, f32[5,16,256]{2,1,0:T(8,128)S(1)}, u32[]{:S(2)}, u32[]{:S(2)}) collective-permute-start(f32[5,16,256]{2,1,0:T(8,128)S(1)} %get-tuple-element.60), channel_id=1, source_target_pairs={{4,8},{8,4},{5,9},{9,5},{6,10},{10,6},{7,11},{11,7},{12,16},{16,12... | collective-permute-start | bytes 245768 | tf_op jit(solution)/shard_map/ppermute | solution.py:307
  35.0 5.7 %collective-permute-start.13 = (f32[5,16,256]{2,1,0:T(8,128)S(1)}, f32[5,16,256]{2,1,0:T(8,128)S(1)}, u32[]{:S(2)}, u32[]{:S(2)}) collective-permute-start(f32[5,16,256]{2,1,0:T(8,128)S(1)} %get-tuple-element.61), channel_id=1, source_target_pairs={{0,1},{1,0},{2,3},{3,2},{4,5},{5,4},{6,7},{7,6},{8,9},{9,8},{10,11... | collective-permute-start | bytes 245768 | tf_op jit(solution)/shard_map/ppermute | solution.py:306
  43.0 8.4 %collective-permute-start.15 = (f32[5,16,256]{2,1,0:T(8,128)S(1)}, f32[5,16,256]{2,1,0:T(8,128)S(1)}, u32[]{:S(2)}, u32[]{:S(2)}) collective-permute-start(f32[5,16,256]{2,1,0:T(8,128)S(1)} %get-tuple-element.65), channel_id=1, source_target_pairs={{0,4},{4,0},{1,5},{5,1},{2,6},{6,2},{3,7},{7,3},{8,12},{12,8},{9,1... | collective-permute-start | bytes 245768 | tf_op jit(solution)/shard_map/ppermute | solution.py:308
  43.5 7.9 %collective-permute-start.16 = (f32[5,16,256]{2,1,0:T(8,128)S(1)}, f32[5,16,256]{2,1,0:T(8,128)S(1)}, u32[]{:S(2)}, u32[]{:S(2)}) collective-permute-start(f32[5,16,256]{2,1,0:T(8,128)S(1)} %get-tuple-element.66), channel_id=1, source_target_pairs={{4,8},{8,4},{5,9},{9,5},{6,10},{10,6},{7,11},{11,7},{12,16},{16,12... | collective-permute-start | bytes 245768 | tf_op jit(solution)/shard_map/ppermute | solution.py:307
  45.8 5.6 %collective-permute-start.17 = (f32[5,16,256]{2,1,0:T(8,128)S(1)}, f32[5,16,256]{2,1,0:T(8,128)S(1)}, u32[]{:S(2)}, u32[]{:S(2)}) collective-permute-start(f32[5,16,256]{2,1,0:T(8,128)S(1)} %get-tuple-element.67), channel_id=1, source_target_pairs={{0,1},{1,0},{2,3},{3,2},{4,5},{5,4},{6,7},{7,6},{8,9},{9,8},{10,11... | collective-permute-start | bytes 245768 | tf_op jit(solution)/shard_map/ppermute | solution.py:306
  46.0 5.4 %collective-permute-start.18 = (f32[5,16,256]{2,1,0:T(8,128)S(1)}, f32[5,16,256]{2,1,0:T(8,128)S(1)}, u32[]{:S(2)}, u32[]{:S(2)}) collective-permute-start(f32[5,16,256]{2,1,0:T(8,128)S(1)} %get-tuple-element.68), channel_id=1, source_target_pairs={{1,2},{2,1},{5,6},{6,5},{9,10},{10,9},{13,14},{14,13},{17,18},{18,... | collective-permute-start | bytes 245768 | tf_op jit(solution)/shard_map/ppermute | solution.py:305
  54.6 7.2 %collective-permute-start.19 = (f32[5,16,256]{2,1,0:T(8,128)S(1)}, f32[5,16,256]{2,1,0:T(8,128)S(1)}, u32[]{:S(2)}, u32[]{:S(2)}) collective-permute-start(f32[5,16,256]{2,1,0:T(8,128)S(1)} %get-tuple-element.70), channel_id=1, source_target_pairs={{0,4},{4,0},{1,5},{5,1},{2,6},{6,2},{3,7},{7,3},{8,12},{12,8},{9,1... | collective-permute-start | bytes 245768 | tf_op jit(solution)/shard_map/ppermute | solution.py:308
  54.6 7.2 %collective-permute-start.20 = (f32[5,16,256]{2,1,0:T(8,128)S(1)}, f32[5,16,256]{2,1,0:T(8,128)S(1)}, u32[]{:S(2)}, u32[]{:S(2)}) collective-permute-start(f32[5,16,256]{2,1,0:T(8,128)S(1)} %get-tuple-element.71), channel_id=1, source_target_pairs={{4,8},{8,4},{5,9},{9,5},{6,10},{10,6},{7,11},{11,7},{12,16},{16,12... | collective-permute-start | bytes 245768 | tf_op jit(solution)/shard_map/ppermute | solution.py:307
  57.1 4.7 %collective-permute-start.21 = (f32[5,16,256]{2,1,0:T(8,128)S(1)}, f32[5,16,256]{2,1,0:T(8,128)S(1)}, u32[]{:S(2)}, u32[]{:S(2)}) collective-permute-start(f32[5,16,256]{2,1,0:T(8,128)S(1)} %get-tuple-element.72), channel_id=1, source_target_pairs={{0,1},{1,0},{2,3},{3,2},{4,5},{5,4},{6,7},{7,6},{8,9},{9,8},{10,11... | collective-permute-start | bytes 245768 | tf_op jit(solution)/shard_map/ppermute | solution.py:306
  64.1 8.1 %collective-permute-start.23 = (f32[5,16,256]{2,1,0:T(8,128)S(1)}, f32[5,16,256]{2,1,0:T(8,128)S(1)}, u32[]{:S(2)}, u32[]{:S(2)}) collective-permute-start(f32[5,16,256]{2,1,0:T(8,128)S(1)} %get-tuple-element.76), channel_id=1, source_target_pairs={{0,4},{4,0},{1,5},{5,1},{2,6},{6,2},{3,7},{7,3},{8,12},{12,8},{9,1... | collective-permute-start | bytes 245768 | tf_op jit(solution)/shard_map/ppermute | solution.py:308
  64.4 7.8 %collective-permute-start.24 = (f32[5,16,256]{2,1,0:T(8,128)S(1)}, f32[5,16,256]{2,1,0:T(8,128)S(1)}, u32[]{:S(2)}, u32[]{:S(2)}) collective-permute-start(f32[5,16,256]{2,1,0:T(8,128)S(1)} %get-tuple-element.77), channel_id=1, source_target_pairs={{4,8},{8,4},{5,9},{9,5},{6,10},{10,6},{7,11},{11,7},{12,16},{16,12... | collective-permute-start | bytes 245768 | tf_op jit(solution)/shard_map/ppermute | solution.py:307
  67.1 5.0 %collective-permute-start.25 = (f32[5,16,256]{2,1,0:T(8,128)S(1)}, f32[5,16,256]{2,1,0:T(8,128)S(1)}, u32[]{:S(2)}, u32[]{:S(2)}) collective-permute-start(f32[5,16,256]{2,1,0:T(8,128)S(1)} %get-tuple-element.78), channel_id=1, source_target_pairs={{0,1},{1,0},{2,3},{3,2},{4,5},{5,4},{6,7},{7,6},{8,9},{9,8},{10,11... | collective-permute-start | bytes 245768 | tf_op jit(solution)/shard_map/ppermute | solution.py:306
  67.3 4.9 %collective-permute-start.26 = (f32[5,16,256]{2,1,0:T(8,128)S(1)}, f32[5,16,256]{2,1,0:T(8,128)S(1)}, u32[]{:S(2)}, u32[]{:S(2)}) collective-permute-start(f32[5,16,256]{2,1,0:T(8,128)S(1)} %get-tuple-element.79), channel_id=1, source_target_pairs={{1,2},{2,1},{5,6},{6,5},{9,10},{10,9},{13,14},{14,13},{17,18},{18,... | collective-permute-start | bytes 245768 | tf_op jit(solution)/shard_map/ppermute | solution.py:305
  75.4 7.9 %collective-permute-start.27 = (f32[5,16,256]{2,1,0:T(8,128)S(1)}, f32[5,16,256]{2,1,0:T(8,128)S(1)}, u32[]{:S(2)}, u32[]{:S(2)}) collective-permute-start(f32[5,16,256]{2,1,0:T(8,128)S(1)} %get-tuple-element.81), channel_id=1, source_target_pairs={{0,4},{4,0},{1,5},{5,1},{2,6},{6,2},{3,7},{7,3},{8,12},{12,8},{9,1... | collective-permute-start | bytes 245768 | tf_op jit(solution)/shard_map/ppermute | solution.py:308
  75.7 7.6 %collective-permute-start.28 = (f32[5,16,256]{2,1,0:T(8,128)S(1)}, f32[5,16,256]{2,1,0:T(8,128)S(1)}, u32[]{:S(2)}, u32[]{:S(2)}) collective-permute-start(f32[5,16,256]{2,1,0:T(8,128)S(1)} %get-tuple-element.82), channel_id=1, source_target_pairs={{4,8},{8,4},{5,9},{9,5},{6,10},{10,6},{7,11},{11,7},{12,16},{16,12... | collective-permute-start | bytes 245768 | tf_op jit(solution)/shard_map/ppermute | solution.py:307
  78.5 4.8 %collective-permute-start.29 = (f32[5,16,256]{2,1,0:T(8,128)S(1)}, f32[5,16,256]{2,1,0:T(8,128)S(1)}, u32[]{:S(2)}, u32[]{:S(2)}) collective-permute-start(f32[5,16,256]{2,1,0:T(8,128)S(1)} %get-tuple-element.83), channel_id=1, source_target_pairs={{0,1},{1,0},{2,3},{3,2},{4,5},{5,4},{6,7},{7,6},{8,9},{9,8},{10,11... | collective-permute-start | bytes 245768 | tf_op jit(solution)/shard_map/ppermute | solution.py:306
  85.5 8.1 %collective-permute-start.31 = (f32[5,16,256]{2,1,0:T(8,128)S(1)}, f32[5,16,256]{2,1,0:T(8,128)S(1)}, u32[]{:S(2)}, u32[]{:S(2)}) collective-permute-start(f32[5,16,256]{2,1,0:T(8,128)S(1)} %get-tuple-element.87), channel_id=1, source_target_pairs={{0,4},{4,0},{1,5},{5,1},{2,6},{6,2},{3,7},{7,3},{8,12},{12,8},{9,1... | collective-permute-start | bytes 245768 | tf_op jit(solution)/shard_map/ppermute | solution.py:308
  85.9 7.8 %collective-permute-start.32 = (f32[5,16,256]{2,1,0:T(8,128)S(1)}, f32[5,16,256]{2,1,0:T(8,128)S(1)}, u32[]{:S(2)}, u32[]{:S(2)}) collective-permute-start(f32[5,16,256]{2,1,0:T(8,128)S(1)} %get-tuple-element.88), channel_id=1, source_target_pairs={{4,8},{8,4},{5,9},{9,5},{6,10},{10,6},{7,11},{11,7},{12,16},{16,12... | collective-permute-start | bytes 245768 | tf_op jit(solution)/shard_map/ppermute | solution.py:307
  88.6 5.0 %collective-permute-start.33 = (f32[5,16,256]{2,1,0:T(8,128)S(1)}, f32[5,16,256]{2,1,0:T(8,128)S(1)}, u32[]{:S(2)}, u32[]{:S(2)}) collective-permute-start(f32[5,16,256]{2,1,0:T(8,128)S(1)} %get-tuple-element.89), channel_id=1, source_target_pairs={{0,1},{1,0},{2,3},{3,2},{4,5},{5,4},{6,7},{7,6},{8,9},{9,8},{10,11... | collective-permute-start | bytes 245768 | tf_op jit(solution)/shard_map/ppermute | solution.py:306
  88.8 4.9 %collective-permute-start.34 = (f32[5,16,256]{2,1,0:T(8,128)S(1)}, f32[5,16,256]{2,1,0:T(8,128)S(1)}, u32[]{:S(2)}, u32[]{:S(2)}) collective-permute-start(f32[5,16,256]{2,1,0:T(8,128)S(1)} %get-tuple-element.90), channel_id=1, source_target_pairs={{1,2},{2,1},{5,6},{6,5},{9,10},{10,9},{13,14},{14,13},{17,18},{18,... | collective-permute-start | bytes 245768 | tf_op jit(solution)/shard_map/ppermute | solution.py:305
  97.0 8.0 %collective-permute-start.35 = (f32[2,16,64]{2,1,0:T(8,128)S(1)}, f32[2,16,64]{2,1,0:T(8,128)S(1)}, u32[]{:S(2)}, u32[]{:S(2)}) collective-permute-start(f32[2,16,64]{2,1,0:T(8,128)S(1)} %get-tuple-element.95), channel_id=1, source_target_pairs={{0,3},{1,2},{2,1},{3,0},{4,7},{5,6},{6,5},{7,4},{8,11},{9,10},{10,... | collective-permute-start | bytes 24584 | tf_op jit(solution)/shard_map/ppermute | solution.py:313
  98.4 6.5 %collective-permute-start.36 = (f32[2,16,64]{2,1,0:T(8,128)S(1)}, f32[2,16,64]{2,1,0:T(8,128)S(1)}, u32[]{:S(2)}, u32[]{:S(2)}) collective-permute-start(f32[2,16,64]{2,1,0:T(8,128)S(1)} %get-tuple-element.96), channel_id=1, source_target_pairs={{0,2},{1,3},{2,0},{3,1},{4,6},{5,7},{6,4},{7,5},{8,10},{9,11},{10,... | collective-permute-start | bytes 24584 | tf_op jit(solution)/shard_map/ppermute | solution.py:313
  (23 other events, 88.7 us)
where the time goes:
time: 107 us; the launch traced here: 106 us
  Pallas kernels  47.3 us (44%)
  starting transfers between devices  38.7 us (36%)
  local copies, waits for them, and re-layouts  13.3 us (12%)
  between operations  3.5 us (3%)
  waiting for transfers between devices  3 us (3%)
    pallas_call x17, Pallas kernels, call(): pl.pallas_call(body, in_specs=[SMEM] * smem + [VMEM] * (len(ins) - smem),...  47.3 us
    ppermute x8, starting transfers between devices, exchange(): xb = lax.ppermute(xb, axes, strike_b)  20.5 us
    unnamed x36, local copies, waits for them, and re-layouts  11.2 us
    ppermute x6, starting transfers between devices, partner(): return lax.ppermute(block, axes, pairs)  9.3 us
    ppermute x8, starting transfers between devices, exchange(): ya = lax.ppermute(ya, axes, cross_a)  4.05 us
    ppermute x8, starting transfers between devices, exchange(): xa = lax.ppermute(xa, axes, strike_a)  3.3 us
    ppermute x8, waiting for transfers between devices, exchange(): ya = lax.ppermute(ya, axes, cross_a)  2.39 us
  transfers between devices with their start and end apart: 38, of which 3 were waited for; matrix products, arithmetic and copies ran while one was open for 2% of the time, Pallas kernels for 24%

commit v1 on v0

--- a/solution.py
+++ b/solution.py
@@ -4,6 +4,7 @@
 from jax.experimental import pallas as pl
 from jax.experimental.pallas import tpu as pltpu
 from jax.sharding import PartitionSpec as P
+
 
 STEPS = 4
 NEWTON = 8
@@ -18,6 +19,7 @@
 
 VMEM = pl.BlockSpec(memory_space=pltpu.VMEM)
 SMEM = pl.BlockSpec(memory_space=pltpu.SMEM)
+HBM = pl.BlockSpec(memory_space=pltpu.HBM)
 PARAMS = pltpu.CompilerParams(vmem_limit_bytes=16 * 1024 * 1024)
 
 STRESS_FACE = (((3, "b"), (4, "b"), (0, "f")), ((3, "b"), (5, "b"), (1, "f")))
@@ -76,7 +78,7 @@
     count = v_ref.shape[1]
     for i in range(count):
         gain = b_ref[i] * unit
-        sxx, syy, szz, sxy, sxz, syz = (s_ref[c, i] for c in range(6))
+        _, syy, szz, sxy, sxz, syz = (s_ref[c, i] for c in range(6))
         sxy_y, sxz_z = plane_shift(sxy, 0), plane_shift(sxz, 1)
         force = add(
             difference("f", strike_shift(s_ref, 0, i, count)),
@@ -96,6 +98,13 @@
             difference("f", plane_shift(szz, 1)),
         )
         out_ref[2, i] = v_ref[2, i] + gain * force
+
+
+def stress_store_body(s_ref, v_ref, lame_ref, shear_ref, out_ref, store_ref, sem):
+    copy = pltpu.make_async_copy(v_ref, store_ref, sem)
+    copy.start()
+    stress_body(s_ref, v_ref, lame_ref, shear_ref, out_ref)
+    copy.wait()
 
 
 def stress_body(s_ref, v_ref, lame_ref, shear_ref, out_ref):
@@ -201,7 +210,7 @@
     strength = rate_a * normal_stress
     drag = damping * width
     scaled = inverse_sinh(total / drag)
-    for iteration in range(NEWTON):
+    for _ in range(NEWTON):
         grow, decay = 0.5 * jnp.exp(scaled), 0.5 * jnp.exp(-scaled)
         residual = strength * scaled + drag * (grow - decay) - total
         slope = strength + drag * (grow + decay)
@@ -215,8 +224,8 @@
 
 
 def stress_edge_body(
-    tile_ref, s_ref, lame_ref, shear_ref, b_ref, fault_ref, state_ref, xa, xb, ya, yb,
-    out_ref, slip_ref, evolved_ref, *packs
+    tile_ref, s_ref, lame_ref, shear_ref, b_ref, load_ref, normal_ref, rate_ref, state_ref, xa, xb, ya, yb,
+    out_ref, *rest
 ):
     for axis, a_ref, b_ref2 in ((0, xa, xb), (1, ya, yb)):
         count = s_ref.shape[1 + axis]
@@ -238,14 +247,72 @@
     trial = out_ref[first]
     damping = 0.5 * jnp.sqrt(shear_ref[:, 0] / b_ref[:, 0])
     change, slip, evolved = friction(
-        trial, damping, fault_ref[0], fault_ref[1], fault_ref[2], state_ref[...]
+        trial, damping, load_ref[...], normal_ref[...], rate_ref[...], state_ref[...]
     )
     out_ref[first] = lax.select(is_owner, change, trial)
-    slip_ref[...] = slip
-    evolved_ref[...] = evolved
-    if packs:
+    if len(rest[-1].shape) == 3:
+        evolved_ref, *packs = rest
+        evolved_ref[...] = evolved
         for axis in (0, 1):
             pack(out_ref, axis, STRESS_FACE[axis], *packs[2 * axis : 2 * axis + 2])
+    else:
+        spread_out(slip, evolved, rest)
+
+
+def spread_out(slip, evolved, sends):
+    lanes = sends[0].shape[1]
+    width, rows = slip.shape[1], lanes // 2
+    place = lax.broadcasted_iota(jnp.int32, slip.shape, 1)
+    me = lax.axis_index("cross")
+    for r, send_ref in enumerate(sends):
+        offset = (me ^ r) * rows
+        head = pltpu.roll(slip, lax.rem(width - offset, width), 1)
+        tail = pltpu.roll(evolved, lax.rem(width + rows - offset, width), 1)
+        send_ref[...] = jnp.where(place < rows, head, tail)[:, :lanes]
+
+
+def finish_body(tile_ref, send_ref, *refs):
+    *got, slip_ref, state_ref = refs
+    owner = tile_ref[lax.axis_index("strike")]
+    me = lax.axis_index("cross")
+    value = send_ref[...]
+    for r, ref in enumerate(got, 1):
+        value = lax.select(owner == (me ^ r), ref[...], value)
+    rows = slip_ref.shape[1]
+    slip_ref[...] = value[:, :rows]
+    state_ref[...] = pltpu.roll(value, rows, 1)[:, :rows]
+
+
+def own_body(*refs):
+    *parts, out_ref = refs
+    pieces = [ref[...] for ref in parts]
+    rest = out_ref.shape[1] - sum(p.shape[1] for p in pieces)
+    if rest:
+        pieces.append(jnp.zeros((out_ref.shape[0], rest), out_ref.dtype))
+    out_ref[...] = jnp.concatenate(pieces, axis=1)
+
+
+def fault_body(*refs):
+    arrays = 4
+    blocks, outs = refs[:-arrays], refs[-arrays:]
+    count, width = len(blocks), blocks[0].shape[1]
+    depth = outs[0].shape[1]
+    rows = depth // count
+    me = lax.axis_index("cross")
+    held = [ref[...] for ref in blocks]
+    place = lax.broadcasted_iota(jnp.int32, held[0].shape, 1)
+    whole = [jnp.zeros_like(held[0])] * arrays
+    for q in range(count):
+        value = held[0]
+        for r in range(1, count):
+            value = lax.select((me ^ r) == q, held[r], value)
+        mine = (place >= q * rows) & (place < (q + 1) * rows)
+        for k in range(arrays):
+            shift = ((q - k) * rows) % width
+            moved = pltpu.roll(value, shift, 1) if shift else value
+            whole[k] = jnp.where(mine, moved, whole[k])
+    for out_ref, value in zip(outs, whole):
+        out_ref[...] = value[:, :depth]
 
 
 def pack_body(s_ref, *packs):
@@ -278,7 +345,6 @@
 ):
     n_strike, n_cross = lax.axis_size("strike"), lax.axis_size("cross")
     axes = ("strike", "cross")
-    strike_pos, cross_pos = lax.axis_index("strike"), lax.axis_index("cross")
     strike_a, strike_b, cross_a, cross_b = exchange_pairs(n_strike, n_cross)
     _, nx, ny, nz = velocity.shape
     bz = prestress.shape[1]
@@ -286,63 +352,77 @@
     thick = 5
     vec = lambda *shape: jax.ShapeDtypeStruct(shape, f32)
     faces = (vec(thick, ny, nz), vec(thick, ny, nz), vec(thick, nx, nz), vec(thick, nx, nz))
-    like_v, like_s = vec(*velocity.shape), vec(*stress.shape)
+    like_v, like_s = pltpu.VMEM(velocity.shape, f32), pltpu.VMEM(stress.shape, f32)
     plane = vec(nx, nz)
 
-    def call(body, ins, outs, alias=None, smem=0, name=None):
+    def call(body, ins, outs, specs=None, alias=None, scratch=()):
         return pl.pallas_call(
             body,
-            in_specs=[SMEM] * smem + [VMEM] * (len(ins) - smem),
-            out_specs=[VMEM] * len(outs),
-            out_shape=list(outs),
+            in_specs=[VMEM] * len(ins) if specs is None else specs,
+            out_specs=[HBM if getattr(o, "hbm", False) else VMEM for o in outs],
+            out_shape=[o.shape if getattr(o, "hbm", False) else o for o in outs],
             input_output_aliases={} if alias is None else {alias: 0},
             compiler_params=PARAMS,
-            name=name,
+            scratch_shapes=scratch,
         )(*ins)
 
     def exchange(packs):
-        xa, xb, ya, yb = packs
-        yb = lax.ppermute(yb, axes, cross_b)
-        ya = lax.ppermute(ya, axes, cross_a)
-        xb = lax.ppermute(xb, axes, strike_b)
-        xa = lax.ppermute(xa, axes, strike_a)
-        return xa, xb, ya, yb
+        perms = dict(xa=strike_a, xb=strike_b, ya=cross_a, yb=cross_b)
+        halos = {}
+        for name, block in reversed(tuple(zip(perms, packs))):
+            halos[name] = lax.ppermute(block, axes, perms[name])
+        return [halos[name] for name in perms]
 
     def partner(block, r):
         pairs = [(s * n_cross + c, s * n_cross + (c ^ r)) for s in range(n_strike) for c in range(n_cross)]
         return lax.ppermute(block, axes, pairs)
 
-    packs = call(pack_body, (stress,), faces, name="pack")
-    own = jnp.concatenate([prestress, normal_stress, rate_a, state], axis=1)
-    blocks = jnp.stack([own] + [partner(own, r) for r in range(1, n_cross)])
-    blocks = jnp.take(blocks, jnp.arange(n_cross) ^ cross_pos, axis=0)
-    fault = blocks.reshape(n_cross, nx, 4, bz).transpose(2, 1, 0, 3).reshape(4, nx, nz)
-    fault_state = fault[3]
-
+    width = max(nz, 4 * bz)
+    (own,) = call(own_body, (prestress, normal_stress, rate_a, state), (vec(nx, width),))
+    packs = call(pack_body, (stress,), faces)
     for iteration in range(STEPS):
+        first, last = iteration == 0, iteration == STEPS - 1
         halos = exchange(packs)
-        (velocity,) = call(velocity_body, (velocity, stress, buoyancy), (like_v,), 0, name="velocity")
+        if first:
+            blocks = [own] + [partner(own, r) for r in range(1, n_cross)]
+            *fault, fault_state = call(fault_body, blocks, (plane,) * 4)
+        (velocity,) = call(
+            velocity_body, (velocity, stress, buoyancy), (like_v,),
+            alias=None if first else 0,
+        )
         velocity, *packs = call(
-            velocity_edge_body, (velocity, buoyancy, *halos), (like_v, *faces), 0, name="velocity_edge"
+            velocity_edge_body, (velocity, buoyancy, *halos), (like_v, *faces), alias=0,
         )
         halos = exchange(packs)
-        (stress,) = call(stress_body, (stress, velocity, lame, shear), (like_s,), 0, name="stress")
-        outs = (like_s, plane, plane) + (faces if iteration < STEPS - 1 else ())
-        stress, slip, fault_state, *packs = call(
+        body, outs, scratch = stress_body, (like_s,), ()
+        if last:
+            body, outs = stress_store_body, (like_s, Stored(vec(*velocity.shape)))
+            scratch = [pltpu.SemaphoreType.DMA]
+        stress, *stored = call(
+            body, (stress, velocity, lame, shear), outs,
+            alias=None if first else 0, scratch=scratch,
+        )
+        outs = (like_s,) + (vec(nx, 2 * bz),) * n_cross if last else (like_s, plane, *faces)
+        stress, fault_state, *packs = call(
             stress_edge_body,
-            (fault_tile, stress, lame, shear, buoyancy, fault, fault_state, *halos),
-            outs, 1, smem=1, name="stress_edge",
-        )
-
-    both = jnp.stack([slip, fault_state])
-    owner = fault_tile[strike_pos]
-    result = jnp.zeros((2, nx, bz), f32)
-    for r in range(n_cross):
-        target = cross_pos ^ r
-        part = lax.dynamic_slice_in_dim(both, target * bz, bz, axis=2)
-        got = part if r == 0 else partner(part, r)
-        result = jnp.where(owner == target, got, result)
-    return (velocity, stress, result[0], result[1])
+            (fault_tile, stress, lame, shear, buoyancy, *fault, fault_state, *halos),
+            outs, [SMEM] + [VMEM] * 12, alias=1,
+        )
+
+    sends = [fault_state, *packs]
+    got = [partner(sends[r], r) for r in range(1, n_cross)]
+    slip_out, state_out = call(
+        finish_body, (fault_tile, sends[0], *got), (vec(nx, bz), vec(nx, bz)),
+        [SMEM] + [VMEM] * n_cross,
+    )
+    return (stored[0], stress, slip_out, state_out)
+
+
+class Stored:
+    hbm = True
+
+    def __init__(self, shape):
+        self.shape = shape
 
 
 def solution(mesh):

time: 107 us -> 88 us (0.82)
  Pallas kernels: 47.3 us -> 14.8 us
  waiting for transfers between devices: 3 us -> 29.8 us
  local copies, waits for them, and re-layouts: 13.3 us -> 4.04 us
  between operations: 3.5 us -> 1.04 us
    pallas_call x17 -> x20, Pallas kernels: 47.3 us -> 14.8 us  [call(): pl.pallas_call(body, in_specs=[VMEM] * len(ins) if specs is None else spe...]
    ppermute x32, waiting for transfers between devices: 2.45 us -> 21 us  [exchange(): halos[name] = lax.ppermute(block, axes, perms[name])]
    ppermute x6, waiting for transfers between devices: 0.55 us -> 8.85 us  [partner(): return lax.ppermute(block, axes, pairs)]
    unnamed x36 -> x25, local copies, waits for them, and re-layouts: 11.2 us -> 4.04 us
    ppermute x32, starting transfers between devices: 29.4 us -> 28.2 us  [exchange(): halos[name] = lax.ppermute(block, axes, perms[name])]
  transfers between devices with their start and end apart: 38 -> 38, of which waited for: 3 -> 18; matrix products, arithmetic and copies ran while one was open for 2% -> 1% of each run, Pallas kernels for 24% -> 8%
where the time goes in v1:
time: 88 us; the launch traced here: 87.9 us
  starting transfers between devices  38.2 us (43%)
  waiting for transfers between devices  29.8 us (34%)
  Pallas kernels  14.8 us (17%)
  local copies, waits for them, and re-layouts  4.04 us (5%)
  between operations  1.04 us (1%)
    ppermute x32, starting transfers between devices, exchange(): halos[name] = lax.ppermute(block, axes, perms[name])  28.2 us
    ppermute x32, waiting for transfers between devices, exchange(): halos[name] = lax.ppermute(block, axes, perms[name])  21 us
    pallas_call x20, Pallas kernels, call(): pl.pallas_call(body, in_specs=[VMEM] * len(ins) if specs is None else spe...  14.8 us
    ppermute x6, starting transfers between devices, partner(): return lax.ppermute(block, axes, pairs)  9.92 us
    ppermute x6, waiting for transfers between devices, partner(): return lax.ppermute(block, axes, pairs)  8.85 us
    unnamed x25, local copies, waits for them, and re-layouts  4.04 us
  transfers between devices with their start and end apart: 38, of which 18 were waited for; matrix products, arithmetic and copies ran while one was open for 1% of the time, Pallas kernels for 8%

profile of v1, /device:TPU:0, one launch (start us, length us, event | category | flops | bytes accessed | tf_op | source)
XLA Modules:
  0.0 87.9 jit_solution(8992106423914834939)
XLA Ops:
  0.7 1.4 %copy-done.3 = f32[6,16,16,256]{3,2,1,0:T(8,128)S(1)} copy-done((f32[6,16,16,256]{3,2,1,0:T(8,128)S(1)}, f32[6,16,16,256]{3,2,1,0:T(8,128)}, u32[]{:S(2)}) %copy-start.3) | copy-done | bytes 1572888
  2.8 2.6 %collective-permute-start.1 = (f32[5,16,256]{2,1,0:T(8,128)S(1)}, f32[5,16,256]{2,1,0:T(8,128)S(1)}, u32[]{:S(2)}, u32[]{:S(2)}) collective-permute-start(f32[5,16,256]{2,1,0:T(8,128)S(1)} %get-tuple-element.60), channel_id=1, source_target_pairs={{4,8},{8,4},{5,9},{9,5},{6,10},{10,6},{7,11},{11,7},{12,16},{16,12... | collective-permute-start | bytes 245768 | tf_op jit(solution)/shard_map/ppermute | solution.py:373
  5.3 1.5 %collective-permute-start.2 = (f32[5,16,256]{2,1,0:T(8,128)S(1)}, f32[5,16,256]{2,1,0:T(8,128)S(1)}, u32[]{:S(2)}, u32[]{:S(2)}) collective-permute-start(f32[5,16,256]{2,1,0:T(8,128)S(1)} %get-tuple-element.61), channel_id=1, source_target_pairs={{0,1},{1,0},{2,3},{3,2},{4,5},{5,4},{6,7},{7,6},{8,9},{9,8},{10,11... | collective-permute-start | bytes 245768 | tf_op jit(solution)/shard_map/ppermute | solution.py:373
  6.8 1.4 %copy-done.4 = f32[6,16,16,256]{3,2,1,0:T(8,128)S(1)} copy-done((f32[6,16,16,256]{3,2,1,0:T(8,128)S(1)}, f32[6,16,16,256]{3,2,1,0:T(8,128)}, u32[]{:S(2)}) %copy-start.4) | copy-done | bytes 1572888
  10.3 3.7 %collective-permute-start.8 = (f32[5,16,256]{2,1,0:T(8,128)S(1)}, f32[5,16,256]{2,1,0:T(8,128)S(1)}, u32[]{:S(2)}, u32[]{:S(2)}) collective-permute-start(f32[5,16,256]{2,1,0:T(8,128)S(1)} %get-tuple-element.69), channel_id=1, source_target_pairs={{4,8},{8,4},{5,9},{9,5},{6,10},{10,6},{7,11},{11,7},{12,16},{16,12... | collective-permute-start | bytes 245768 | tf_op jit(solution)/shard_map/ppermute | solution.py:373
  14.2 1.3 %collective-permute-start.10 = (f32[5,16,256]{2,1,0:T(8,128)S(1)}, f32[5,16,256]{2,1,0:T(8,128)S(1)}, u32[]{:S(2)}, u32[]{:S(2)}) collective-permute-start(f32[5,16,256]{2,1,0:T(8,128)S(1)} %get-tuple-element.71), channel_id=1, source_target_pairs={{1,2},{2,1},{5,6},{6,5},{9,10},{10,9},{13,14},{14,13},{17,18},{18,... | collective-permute-start | bytes 245768 | tf_op jit(solution)/shard_map/ppermute | solution.py:373
  15.6 1.3 %collective-permute-start.6 = (f32[16,256]{1,0:T(8,128)S(1)}, f32[16,256]{1,0:T(8,128)S(1)}, u32[]{:S(2)}, u32[]{:S(2)}) collective-permute-start(f32[16,256]{1,0:T(8,128)S(1)} %shard_map.133.refs_0_), channel_id=1, source_target_pairs={{0,3},{1,2},{2,1},{3,0},{4,7},{5,6},{6,5},{7,4},{8,11},{9,10},{10,... | collective-permute-start | bytes 49160 | tf_op jit(solution)/shard_map/ppermute | solution.py:378
  16.9 3.3 %collective-permute-done.6.refs_3_ = f32[16,256]{1,0:T(8,128)S(1)} collective-permute-done((f32[16,256]{1,0:T(8,128)S(1)}, f32[16,256]{1,0:T(8,128)S(1)}, u32[]{:S(2)}, u32[]{:S(2)}) %collective-permute-start.6) | collective-permute-done | bytes 16416 | tf_op jit(solution)/shard_map/ppermute | solution.py:378
  20.2 1.9 %collective-permute-start.5 = (f32[16,256]{1,0:T(8,128)S(1)}, f32[16,256]{1,0:T(8,128)S(1)}, u32[]{:S(2)}, u32[]{:S(2)}) collective-permute-start(f32[16,256]{1,0:T(8,128)S(1)} %shard_map.133.refs_0_), channel_id=1, source_target_pairs={{0,2},{1,3},{2,0},{3,1},{4,6},{5,7},{6,4},{7,5},{8,10},{9,11},{10,... | collective-permute-start | bytes 49160 | tf_op jit(solution)/shard_map/ppermute | solution.py:378
  22.2 1.8 %collective-permute-done.5.refs_2_ = f32[16,256]{1,0:T(8,128)S(1)} collective-permute-done((f32[16,256]{1,0:T(8,128)S(1)}, f32[16,256]{1,0:T(8,128)S(1)}, u32[]{:S(2)}, u32[]{:S(2)}) %collective-permute-start.5) | collective-permute-done | bytes 16416 | tf_op jit(solution)/shard_map/ppermute | solution.py:378
  24.0 2.1 %collective-permute-start.4 = (f32[16,256]{1,0:T(8,128)S(1)}, f32[16,256]{1,0:T(8,128)S(1)}, u32[]{:S(2)}, u32[]{:S(2)}) collective-permute-start(f32[16,256]{1,0:T(8,128)S(1)} %shard_map.133.refs_0_), channel_id=1, source_target_pairs={{0,1},{1,0},{2,3},{3,2},{4,5},{5,4},{6,7},{7,6},{8,9},{9,8},{10,11... | collective-permute-start | bytes 49160 | tf_op jit(solution)/shard_map/ppermute | solution.py:378
  26.1 1.7 %collective-permute-done.4.refs_1_ = f32[16,256]{1,0:T(8,128)S(1)} collective-permute-done((f32[16,256]{1,0:T(8,128)S(1)}, f32[16,256]{1,0:T(8,128)S(1)}, u32[]{:S(2)}, u32[]{:S(2)}) %collective-permute-start.4) | collective-permute-done | bytes 16416 | tf_op jit(solution)/shard_map/ppermute | solution.py:378
  28.9 1.2 %shard_map.135 = (f32[6,16,16,256]{3,2,1,0:T(8,128)S(1)}, f32[16,256]{1,0:T(8,128)S(1)}, f32[5,16,256]{2,1,0:T(8,128)S(1)}, f32[5,16,256]{2,1,0:T(8,128)S(1)}, f...) custom-call(s32[8]{0:T(128)S(1)} %copy-done.7, ...), custom_call_target="tpu_custom_call", output_to_operand_aliasing={{0}: (1, {})} | custom-call | tf_op jit(solution)/shard_map/pallas_call | solution.py:359
  30.2 1.9 %collective-permute-start.12 = (f32[5,16,256]{2,1,0:T(8,128)S(1)}, f32[5,16,256]{2,1,0:T(8,128)S(1)}, u32[]{:S(2)}, u32[]{:S(2)}) collective-permute-start(f32[5,16,256]{2,1,0:T(8,128)S(1)} %get-tuple-element.74), channel_id=1, source_target_pairs={{4,8},{8,4},{5,9},{9,5},{6,10},{10,6},{7,11},{11,7},{12,16},{16,12... | collective-permute-start | bytes 245768 | tf_op jit(solution)/shard_map/ppermute | solution.py:373
  33.4 1.4 %collective-permute-done.12.xb = f32[5,16,256]{2,1,0:T(8,128)S(1)} collective-permute-done((f32[5,16,256]{2,1,0:T(8,128)S(1)}, f32[5,16,256]{2,1,0:T(8,128)S(1)}, u32[]{:S(2)}, u32[]{:S(2)}) %collective-permute-start.12) | collective-permute-done | bytes 81952 | tf_op jit(solution)/shard_map/ppermute | solution.py:373
  34.8 2.6 %collective-permute-done.13.ya = f32[5,16,256]{2,1,0:T(8,128)S(1)} collective-permute-done((f32[5,16,256]{2,1,0:T(8,128)S(1)}, f32[5,16,256]{2,1,0:T(8,128)S(1)}, u32[]{:S(2)}, u32[]{:S(2)}) %collective-permute-start.13) | collective-permute-done | bytes 81952 | tf_op jit(solution)/shard_map/ppermute | solution.py:373
  37.7 2.5 %collective-permute-start.16 = (f32[5,16,256]{2,1,0:T(8,128)S(1)}, f32[5,16,256]{2,1,0:T(8,128)S(1)}, u32[]{:S(2)}, u32[]{:S(2)}) collective-permute-start(f32[5,16,256]{2,1,0:T(8,128)S(1)} %get-tuple-element.80), channel_id=1, source_target_pairs={{4,8},{8,4},{5,9},{9,5},{6,10},{10,6},{7,11},{11,7},{12,16},{16,12... | collective-permute-start | bytes 245768 | tf_op jit(solution)/shard_map/ppermute | solution.py:373
  42.6 2.2 %collective-permute-done.17.ya = f32[5,16,256]{2,1,0:T(8,128)S(1)} collective-permute-done((f32[5,16,256]{2,1,0:T(8,128)S(1)}, f32[5,16,256]{2,1,0:T(8,128)S(1)}, u32[]{:S(2)}, u32[]{:S(2)}) %collective-permute-start.17) | collective-permute-done | bytes 81952 | tf_op jit(solution)/shard_map/ppermute | solution.py:373
  46.1 2.9 %collective-permute-start.20 = (f32[5,16,256]{2,1,0:T(8,128)S(1)}, f32[5,16,256]{2,1,0:T(8,128)S(1)}, u32[]{:S(2)}, u32[]{:S(2)}) collective-permute-start(f32[5,16,256]{2,1,0:T(8,128)S(1)} %get-tuple-element.85), channel_id=1, source_target_pairs={{4,8},{8,4},{5,9},{9,5},{6,10},{10,6},{7,11},{11,7},{12,16},{16,12... | collective-permute-start | bytes 245768 | tf_op jit(solution)/shard_map/ppermute | solution.py:373
  51.4 2.3 %collective-permute-done.21.ya = f32[5,16,256]{2,1,0:T(8,128)S(1)} collective-permute-done((f32[5,16,256]{2,1,0:T(8,128)S(1)}, f32[5,16,256]{2,1,0:T(8,128)S(1)}, u32[]{:S(2)}, u32[]{:S(2)}) %collective-permute-start.21) | collective-permute-done | bytes 81952 | tf_op jit(solution)/shard_map/ppermute | solution.py:373
  54.1 2.6 %collective-permute-start.24 = (f32[5,16,256]{2,1,0:T(8,128)S(1)}, f32[5,16,256]{2,1,0:T(8,128)S(1)}, u32[]{:S(2)}, u32[]{:S(2)}) collective-permute-start(f32[5,16,256]{2,1,0:T(8,128)S(1)} %get-tuple-element.91), channel_id=1, source_target_pairs={{4,8},{8,4},{5,9},{9,5},{6,10},{10,6},{7,11},{11,7},{12,16},{16,12... | collective-permute-start | bytes 245768 | tf_op jit(solution)/shard_map/ppermute | solution.py:373
  58.1 1.5 %collective-permute-done.24.xb = f32[5,16,256]{2,1,0:T(8,128)S(1)} collective-permute-done((f32[5,16,256]{2,1,0:T(8,128)S(1)}, f32[5,16,256]{2,1,0:T(8,128)S(1)}, u32[]{:S(2)}, u32[]{:S(2)}) %collective-permute-start.24) | collective-permute-done | bytes 81952 | tf_op jit(solution)/shard_map/ppermute | solution.py:373
  59.6 1.6 %collective-permute-done.25.ya = f32[5,16,256]{2,1,0:T(8,128)S(1)} collective-permute-done((f32[5,16,256]{2,1,0:T(8,128)S(1)}, f32[5,16,256]{2,1,0:T(8,128)S(1)}, u32[]{:S(2)}, u32[]{:S(2)}) %collective-permute-start.25) | collective-permute-done | bytes 81952 | tf_op jit(solution)/shard_map/ppermute | solution.py:373
  62.5 3.1 %collective-permute-start.28 = (f32[5,16,256]{2,1,0:T(8,128)S(1)}, f32[5,16,256]{2,1,0:T(8,128)S(1)}, u32[]{:S(2)}, u32[]{:S(2)}) collective-permute-start(f32[5,16,256]{2,1,0:T(8,128)S(1)} %get-tuple-element.96), channel_id=1, source_target_pairs={{4,8},{8,4},{5,9},{9,5},{6,10},{10,6},{7,11},{11,7},{12,16},{16,12... | collective-permute-start | bytes 245768 | tf_op jit(solution)/shard_map/ppermute | solution.py:373
  66.8 1.2 %collective-permute-done.28.xb = f32[5,16,256]{2,1,0:T(8,128)S(1)} collective-permute-done((f32[5,16,256]{2,1,0:T(8,128)S(1)}, f32[5,16,256]{2,1,0:T(8,128)S(1)}, u32[]{:S(2)}, u32[]{:S(2)}) %collective-permute-start.28) | collective-permute-done | bytes 81952 | tf_op jit(solution)/shard_map/ppermute | solution.py:373
  68.0 2.1 %collective-permute-done.29.ya = f32[5,16,256]{2,1,0:T(8,128)S(1)} collective-permute-done((f32[5,16,256]{2,1,0:T(8,128)S(1)}, f32[5,16,256]{2,1,0:T(8,128)S(1)}, u32[]{:S(2)}, u32[]{:S(2)}) %collective-permute-start.29) | collective-permute-done | bytes 81952 | tf_op jit(solution)/shard_map/ppermute | solution.py:373
  70.5 2.9 %collective-permute-start.32 = (f32[5,16,256]{2,1,0:T(8,128)S(1)}, f32[5,16,256]{2,1,0:T(8,128)S(1)}, u32[]{:S(2)}, u32[]{:S(2)}) collective-permute-start(f32[5,16,256]{2,1,0:T(8,128)S(1)} %get-tuple-element.104), channel_id=1, source_target_pairs={{4,8},{8,4},{5,9},{9,5},{6,10},{10,6},{7,11},{11,7},{12,16},{16,12... | collective-permute-start | bytes 245768 | tf_op jit(solution)/shard_map/ppermute | solution.py:373
  74.5 1.6 %collective-permute-done.32.xb = f32[5,16,256]{2,1,0:T(8,128)S(1)} collective-permute-done((f32[5,16,256]{2,1,0:T(8,128)S(1)}, f32[5,16,256]{2,1,0:T(8,128)S(1)}, u32[]{:S(2)}, u32[]{:S(2)}) %collective-permute-start.32) | collective-permute-done | bytes 81952 | tf_op jit(solution)/shard_map/ppermute | solution.py:373
  76.2 1.6 %collective-permute-done.33.ya = f32[5,16,256]{2,1,0:T(8,128)S(1)} collective-permute-done((f32[5,16,256]{2,1,0:T(8,128)S(1)}, f32[5,16,256]{2,1,0:T(8,128)S(1)}, u32[]{:S(2)}, u32[]{:S(2)}) %collective-permute-start.33) | collective-permute-done | bytes 81952 | tf_op jit(solution)/shard_map/ppermute | solution.py:373
  78.9 3.0 %collective-permute-start.35 = (f32[16,128]{1,0:T(8,128)S(1)}, f32[16,128]{1,0:T(8,128)S(1)}, u32[]{:S(2)}, u32[]{:S(2)}) collective-permute-start(f32[16,128]{1,0:T(8,128)S(1)} %get-tuple-element.109), channel_id=1, source_target_pairs={{0,1},{1,0},{2,3},{3,2},{4,5},{5,4},{6,7},{7,6},{8,9},{9,8},{10,11... | collective-permute-start | bytes 24584 | tf_op jit(solution)/shard_map/ppermute | solution.py:378
  82.1 1.4 %collective-permute-start.37 = (f32[16,128]{1,0:T(8,128)S(1)}, f32[16,128]{1,0:T(8,128)S(1)}, u32[]{:S(2)}, u32[]{:S(2)}) collective-permute-start(f32[16,128]{1,0:T(8,128)S(1)} %get-tuple-element.111), channel_id=1, source_target_pairs={{0,3},{1,2},{2,1},{3,0},{4,7},{5,6},{6,5},{7,4},{8,11},{9,10},{10,... | collective-permute-start | bytes 24584 | tf_op jit(solution)/shard_map/ppermute | solution.py:378
  86.6 1.2 %shard_map.148 = (f32[16,64]{1,0:T(8,128)}, f32[16,64]{1,0:T(8,128)}) custom-call(s32[8]{0:T(128)S(1)} %copy-done.7, f32[16,128]{1,0:T(8,128)S(1)} %get-tuple-element.108.send_ref, f32[16,128]{1,0:T(8,128)S(1)} %collective-permute-done.35.refs_0_, f32[16,128]{1,0:T(8,128)S(1)} %collective-permute-done.36.refs_1_, f32[16,128]{1,0:T(8,128)S(1)} %collective-permute-done.37.refs_2_), custom_call_target="tpu_custom_call" | custom-call | tf_op jit(solution)/shard_map/pallas_call | solution.py:359
  (89 shorter events, 22.0 us)
Async XLA Ops:
  2.2 6.9 %collective-permute-start = (f32[5,16,256]{2,1,0:T(8,128)S(1)}, f32[5,16,256]{2,1,0:T(8,128)S(1)}, u32[]{:S(2)}, u32[]{:S(2)}) collective-permute-start(f32[5,16,256]{2,1,0:T(8,128)S(1)} %get-tuple-element.59), channel_id=1, source_target_pairs={{0,4},{4,0},{1,5},{5,1},{2,6},{6,2},{3,7},{7,3},{8,12},{12,8},{9,1... | collective-permute-start | bytes 245768 | tf_op jit(solution)/shard_map/ppermute | solution.py:373
  2.8 6.4 %collective-permute-start.1 = (f32[5,16,256]{2,1,0:T(8,128)S(1)}, f32[5,16,256]{2,1,0:T(8,128)S(1)}, u32[]{:S(2)}, u32[]{:S(2)}) collective-permute-start(f32[5,16,256]{2,1,0:T(8,128)S(1)} %get-tuple-element.60), channel_id=1, source_target_pairs={{4,8},{8,4},{5,9},{9,5},{6,10},{10,6},{7,11},{11,7},{12,16},{16,12... | collective-permute-start | bytes 245768 | tf_op jit(solution)/shard_map/ppermute | solution.py:373
  5.3 4.5 %collective-permute-start.2 = (f32[5,16,256]{2,1,0:T(8,128)S(1)}, f32[5,16,256]{2,1,0:T(8,128)S(1)}, u32[]{:S(2)}, u32[]{:S(2)}) collective-permute-start(f32[5,16,256]{2,1,0:T(8,128)S(1)} %get-tuple-element.61), channel_id=1, source_target_pairs={{0,1},{1,0},{2,3},{3,2},{4,5},{5,4},{6,7},{7,6},{8,9},{9,8},{10,11... | collective-permute-start | bytes 245768 | tf_op jit(solution)/shard_map/ppermute | solution.py:373
  10.2 18.7 %collective-permute-start.7 = (f32[5,16,256]{2,1,0:T(8,128)S(1)}, f32[5,16,256]{2,1,0:T(8,128)S(1)}, u32[]{:S(2)}, u32[]{:S(2)}) collective-permute-start(f32[5,16,256]{2,1,0:T(8,128)S(1)} %get-tuple-element.68), channel_id=1, source_target_pairs={{0,4},{4,0},{1,5},{5,1},{2,6},{6,2},{3,7},{7,3},{8,12},{12,8},{9,1... | collective-permute-start | bytes 245768 | tf_op jit(solution)/shard_map/ppermute | solution.py:373
  10.3 18.6 %collective-permute-start.8 = (f32[5,16,256]{2,1,0:T(8,128)S(1)}, f32[5,16,256]{2,1,0:T(8,128)S(1)}, u32[]{:S(2)}, u32[]{:S(2)}) collective-permute-start(f32[5,16,256]{2,1,0:T(8,128)S(1)} %get-tuple-element.69), channel_id=1, source_target_pairs={{4,8},{8,4},{5,9},{9,5},{6,10},{10,6},{7,11},{11,7},{12,16},{16,12... | collective-permute-start | bytes 245768 | tf_op jit(solution)/shard_map/ppermute | solution.py:373
  14.0 15.0 %collective-permute-start.9 = (f32[5,16,256]{2,1,0:T(8,128)S(1)}, f32[5,16,256]{2,1,0:T(8,128)S(1)}, u32[]{:S(2)}, u32[]{:S(2)}) collective-permute-start(f32[5,16,256]{2,1,0:T(8,128)S(1)} %get-tuple-element.70), channel_id=1, source_target_pairs={{0,1},{1,0},{2,3},{3,2},{4,5},{5,4},{6,7},{7,6},{8,9},{9,8},{10,11... | collective-permute-start | bytes 245768 | tf_op jit(solution)/shard_map/ppermute | solution.py:373
  14.2 14.7 %collective-permute-start.10 = (f32[5,16,256]{2,1,0:T(8,128)S(1)}, f32[5,16,256]{2,1,0:T(8,128)S(1)}, u32[]{:S(2)}, u32[]{:S(2)}) collective-permute-start(f32[5,16,256]{2,1,0:T(8,128)S(1)} %get-tuple-element.71), channel_id=1, source_target_pairs={{1,2},{2,1},{5,6},{6,5},{9,10},{10,9},{13,14},{14,13},{17,18},{18,... | collective-permute-start | bytes 245768 | tf_op jit(solution)/shard_map/ppermute | solution.py:373
  15.6 4.6 %collective-permute-start.6 = (f32[16,256]{1,0:T(8,128)S(1)}, f32[16,256]{1,0:T(8,128)S(1)}, u32[]{:S(2)}, u32[]{:S(2)}) collective-permute-start(f32[16,256]{1,0:T(8,128)S(1)} %shard_map.133.refs_0_), channel_id=1, source_target_pairs={{0,3},{1,2},{2,1},{3,0},{4,7},{5,6},{6,5},{7,4},{8,11},{9,10},{10,... | collective-permute-start | bytes 49160 | tf_op jit(solution)/shard_map/ppermute | solution.py:378
  30.2 4.5 %collective-permute-start.12 = (f32[5,16,256]{2,1,0:T(8,128)S(1)}, f32[5,16,256]{2,1,0:T(8,128)S(1)}, u32[]{:S(2)}, u32[]{:S(2)}) collective-permute-start(f32[5,16,256]{2,1,0:T(8,128)S(1)} %get-tuple-element.74), channel_id=1, source_target_pairs={{4,8},{8,4},{5,9},{9,5},{6,10},{10,6},{7,11},{11,7},{12,16},{16,12... | collective-permute-start | bytes 245768 | tf_op jit(solution)/shard_map/ppermute | solution.py:373
  32.2 5.1 %collective-permute-start.13 = (f32[5,16,256]{2,1,0:T(8,128)S(1)}, f32[5,16,256]{2,1,0:T(8,128)S(1)}, u32[]{:S(2)}, u32[]{:S(2)}) collective-permute-start(f32[5,16,256]{2,1,0:T(8,128)S(1)} %get-tuple-element.75), channel_id=1, source_target_pairs={{0,1},{1,0},{2,3},{3,2},{4,5},{5,4},{6,7},{7,6},{8,9},{9,8},{10,11... | collective-permute-start | bytes 245768 | tf_op jit(solution)/shard_map/ppermute | solution.py:373
  32.4 4.9 %collective-permute-start.14 = (f32[5,16,256]{2,1,0:T(8,128)S(1)}, f32[5,16,256]{2,1,0:T(8,128)S(1)}, u32[]{:S(2)}, u32[]{:S(2)}) collective-permute-start(f32[5,16,256]{2,1,0:T(8,128)S(1)} %get-tuple-element.76), channel_id=1, source_target_pairs={{1,2},{2,1},{5,6},{6,5},{9,10},{10,9},{13,14},{14,13},{17,18},{18,... | collective-permute-start | bytes 245768 | tf_op jit(solution)/shard_map/ppermute | solution.py:373
  37.6 4.1 %collective-permute-start.15 = (f32[5,16,256]{2,1,0:T(8,128)S(1)}, f32[5,16,256]{2,1,0:T(8,128)S(1)}, u32[]{:S(2)}, u32[]{:S(2)}) collective-permute-start(f32[5,16,256]{2,1,0:T(8,128)S(1)} %get-tuple-element.79), channel_id=1, source_target_pairs={{0,4},{4,0},{1,5},{5,1},{2,6},{6,2},{3,7},{7,3},{8,12},{12,8},{9,1... | collective-permute-start | bytes 245768 | tf_op jit(solution)/shard_map/ppermute | solution.py:373
  37.7 4.9 %collective-permute-start.16 = (f32[5,16,256]{2,1,0:T(8,128)S(1)}, f32[5,16,256]{2,1,0:T(8,128)S(1)}, u32[]{:S(2)}, u32[]{:S(2)}) collective-permute-start(f32[5,16,256]{2,1,0:T(8,128)S(1)} %get-tuple-element.80), channel_id=1, source_target_pairs={{4,8},{8,4},{5,9},{9,5},{6,10},{10,6},{7,11},{11,7},{12,16},{16,12... | collective-permute-start | bytes 245768 | tf_op jit(solution)/shard_map/ppermute | solution.py:373
  40.2 4.7 %collective-permute-start.17 = (f32[5,16,256]{2,1,0:T(8,128)S(1)}, f32[5,16,256]{2,1,0:T(8,128)S(1)}, u32[]{:S(2)}, u32[]{:S(2)}) collective-permute-start(f32[5,16,256]{2,1,0:T(8,128)S(1)} %get-tuple-element.81), channel_id=1, source_target_pairs={{0,1},{1,0},{2,3},{3,2},{4,5},{5,4},{6,7},{7,6},{8,9},{9,8},{10,11... | collective-permute-start | bytes 245768 | tf_op jit(solution)/shard_map/ppermute | solution.py:373
  40.3 4.5 %collective-permute-start.18 = (f32[5,16,256]{2,1,0:T(8,128)S(1)}, f32[5,16,256]{2,1,0:T(8,128)S(1)}, u32[]{:S(2)}, u32[]{:S(2)}) collective-permute-start(f32[5,16,256]{2,1,0:T(8,128)S(1)} %get-tuple-element.82), channel_id=1, source_target_pairs={{1,2},{2,1},{5,6},{6,5},{9,10},{10,9},{13,14},{14,13},{17,18},{18,... | collective-permute-start | bytes 245768 | tf_op jit(solution)/shard_map/ppermute | solution.py:373
  46.1 4.1 %collective-permute-start.19 = (f32[5,16,256]{2,1,0:T(8,128)S(1)}, f32[5,16,256]{2,1,0:T(8,128)S(1)}, u32[]{:S(2)}, u32[]{:S(2)}) collective-permute-start(f32[5,16,256]{2,1,0:T(8,128)S(1)} %get-tuple-element.84), channel_id=1, source_target_pairs={{0,4},{4,0},{1,5},{5,1},{2,6},{6,2},{3,7},{7,3},{8,12},{12,8},{9,1... | collective-permute-start | bytes 245768 | tf_op jit(solution)/shard_map/ppermute | solution.py:373
  46.1 5.3 %collective-permute-start.20 = (f32[5,16,256]{2,1,0:T(8,128)S(1)}, f32[5,16,256]{2,1,0:T(8,128)S(1)}, u32[]{:S(2)}, u32[]{:S(2)}) collective-permute-start(f32[5,16,256]{2,1,0:T(8,128)S(1)} %get-tuple-element.85), channel_id=1, source_target_pairs={{4,8},{8,4},{5,9},{9,5},{6,10},{10,6},{7,11},{11,7},{12,16},{16,12... | collective-permute-start | bytes 245768 | tf_op jit(solution)/shard_map/ppermute | solution.py:373
  49.0 4.7 %collective-permute-start.21 = (f32[5,16,256]{2,1,0:T(8,128)S(1)}, f32[5,16,256]{2,1,0:T(8,128)S(1)}, u32[]{:S(2)}, u32[]{:S(2)}) collective-permute-start(f32[5,16,256]{2,1,0:T(8,128)S(1)} %get-tuple-element.86), channel_id=1, source_target_pairs={{0,1},{1,0},{2,3},{3,2},{4,5},{5,4},{6,7},{7,6},{8,9},{9,8},{10,11... | collective-permute-start | bytes 245768 | tf_op jit(solution)/shard_map/ppermute | solution.py:373
  49.0 4.7 %collective-permute-start.22 = (f32[5,16,256]{2,1,0:T(8,128)S(1)}, f32[5,16,256]{2,1,0:T(8,128)S(1)}, u32[]{:S(2)}, u32[]{:S(2)}) collective-permute-start(f32[5,16,256]{2,1,0:T(8,128)S(1)} %get-tuple-element.87), channel_id=1, source_target_pairs={{1,2},{2,1},{5,6},{6,5},{9,10},{10,9},{13,14},{14,13},{17,18},{18,... | collective-permute-start | bytes 245768 | tf_op jit(solution)/shard_map/ppermute | solution.py:373
  54.1 5.5 %collective-permute-start.24 = (f32[5,16,256]{2,1,0:T(8,128)S(1)}, f32[5,16,256]{2,1,0:T(8,128)S(1)}, u32[]{:S(2)}, u32[]{:S(2)}) collective-permute-start(f32[5,16,256]{2,1,0:T(8,128)S(1)} %get-tuple-element.91), channel_id=1, source_target_pairs={{4,8},{8,4},{5,9},{9,5},{6,10},{10,6},{7,11},{11,7},{12,16},{16,12... | collective-permute-start | bytes 245768 | tf_op jit(solution)/shard_map/ppermute | solution.py:373
  56.7 4.5 %collective-permute-start.25 = (f32[5,16,256]{2,1,0:T(8,128)S(1)}, f32[5,16,256]{2,1,0:T(8,128)S(1)}, u32[]{:S(2)}, u32[]{:S(2)}) collective-permute-start(f32[5,16,256]{2,1,0:T(8,128)S(1)} %get-tuple-element.92), channel_id=1, source_target_pairs={{0,1},{1,0},{2,3},{3,2},{4,5},{5,4},{6,7},{7,6},{8,9},{9,8},{10,11... | collective-permute-start | bytes 245768 | tf_op jit(solution)/shard_map/ppermute | solution.py:373
  56.9 4.3 %collective-permute-start.26 = (f32[5,16,256]{2,1,0:T(8,128)S(1)}, f32[5,16,256]{2,1,0:T(8,128)S(1)}, u32[]{:S(2)}, u32[]{:S(2)}) collective-permute-start(f32[5,16,256]{2,1,0:T(8,128)S(1)} %get-tuple-element.93), channel_id=1, source_target_pairs={{1,2},{2,1},{5,6},{6,5},{9,10},{10,9},{13,14},{14,13},{17,18},{18,... | collective-permute-start | bytes 245768 | tf_op jit(solution)/shard_map/ppermute | solution.py:373
  62.4 4.3 %collective-permute-start.27 = (f32[5,16,256]{2,1,0:T(8,128)S(1)}, f32[5,16,256]{2,1,0:T(8,128)S(1)}, u32[]{:S(2)}, u32[]{:S(2)}) collective-permute-start(f32[5,16,256]{2,1,0:T(8,128)S(1)} %get-tuple-element.95), channel_id=1, source_target_pairs={{0,4},{4,0},{1,5},{5,1},{2,6},{6,2},{3,7},{7,3},{8,12},{12,8},{9,1... | collective-permute-start | bytes 245768 | tf_op jit(solution)/shard_map/ppermute | solution.py:373
  62.5 5.5 %collective-permute-start.28 = (f32[5,16,256]{2,1,0:T(8,128)S(1)}, f32[5,16,256]{2,1,0:T(8,128)S(1)}, u32[]{:S(2)}, u32[]{:S(2)}) collective-permute-start(f32[5,16,256]{2,1,0:T(8,128)S(1)} %get-tuple-element.96), channel_id=1, source_target_pairs={{4,8},{8,4},{5,9},{9,5},{6,10},{10,6},{7,11},{11,7},{12,16},{16,12... | collective-permute-start | bytes 245768 | tf_op jit(solution)/shard_map/ppermute | solution.py:373
  65.6 4.5 %collective-permute-start.29 = (f32[5,16,256]{2,1,0:T(8,128)S(1)}, f32[5,16,256]{2,1,0:T(8,128)S(1)}, u32[]{:S(2)}, u32[]{:S(2)}) collective-permute-start(f32[5,16,256]{2,1,0:T(8,128)S(1)} %get-tuple-element.97), channel_id=1, source_target_pairs={{0,1},{1,0},{2,3},{3,2},{4,5},{5,4},{6,7},{7,6},{8,9},{9,8},{10,11... | collective-permute-start | bytes 245768 | tf_op jit(solution)/shard_map/ppermute | solution.py:373
  65.6 4.5 %collective-permute-start.30 = (f32[5,16,256]{2,1,0:T(8,128)S(1)}, f32[5,16,256]{2,1,0:T(8,128)S(1)}, u32[]{:S(2)}, u32[]{:S(2)}) collective-permute-start(f32[5,16,256]{2,1,0:T(8,128)S(1)} %get-tuple-element.98), channel_id=1, source_target_pairs={{1,2},{2,1},{5,6},{6,5},{9,10},{10,9},{13,14},{14,13},{17,18},{18,... | collective-permute-start | bytes 245768 | tf_op jit(solution)/shard_map/ppermute | solution.py:373
  70.4 4.2 %collective-permute-start.31 = (f32[5,16,256]{2,1,0:T(8,128)S(1)}, f32[5,16,256]{2,1,0:T(8,128)S(1)}, u32[]{:S(2)}, u32[]{:S(2)}) collective-permute-start(f32[5,16,256]{2,1,0:T(8,128)S(1)} %get-tuple-element.103), channel_id=1, source_target_pairs={{0,4},{4,0},{1,5},{5,1},{2,6},{6,2},{3,7},{7,3},{8,12},{12,8},{9,1... | collective-permute-start | bytes 245768 | tf_op jit(solution)/shard_map/ppermute | solution.py:373
  70.5 5.7 %collective-permute-start.32 = (f32[5,16,256]{2,1,0:T(8,128)S(1)}, f32[5,16,256]{2,1,0:T(8,128)S(1)}, u32[]{:S(2)}, u32[]{:S(2)}) collective-permute-start(f32[5,16,256]{2,1,0:T(8,128)S(1)} %get-tuple-element.104), channel_id=1, source_target_pairs={{4,8},{8,4},{5,9},{9,5},{6,10},{10,6},{7,11},{11,7},{12,16},{16,12... | collective-permute-start | bytes 245768 | tf_op jit(solution)/shard_map/ppermute | solution.py:373
  73.3 4.4 %collective-permute-start.33 = (f32[5,16,256]{2,1,0:T(8,128)S(1)}, f32[5,16,256]{2,1,0:T(8,128)S(1)}, u32[]{:S(2)}, u32[]{:S(2)}) collective-permute-start(f32[5,16,256]{2,1,0:T(8,128)S(1)} %get-tuple-element.105), channel_id=1, source_target_pairs={{0,1},{1,0},{2,3},{3,2},{4,5},{5,4},{6,7},{7,6},{8,9},{9,8},{10,11... | collective-permute-start | bytes 245768 | tf_op jit(solution)/shard_map/ppermute | solution.py:373
  73.5 4.3 %collective-permute-start.34 = (f32[5,16,256]{2,1,0:T(8,128)S(1)}, f32[5,16,256]{2,1,0:T(8,128)S(1)}, u32[]{:S(2)}, u32[]{:S(2)}) collective-permute-start(f32[5,16,256]{2,1,0:T(8,128)S(1)} %get-tuple-element.106), channel_id=1, source_target_pairs={{1,2},{2,1},{5,6},{6,5},{9,10},{10,9},{13,14},{14,13},{17,18},{18,... | collective-permute-start | bytes 245768 | tf_op jit(solution)/shard_map/ppermute | solution.py:373
  78.9 5.7 %collective-permute-start.35 = (f32[16,128]{1,0:T(8,128)S(1)}, f32[16,128]{1,0:T(8,128)S(1)}, u32[]{:S(2)}, u32[]{:S(2)}) collective-permute-start(f32[16,128]{1,0:T(8,128)S(1)} %get-tuple-element.109), channel_id=1, source_target_pairs={{0,1},{1,0},{2,3},{3,2},{4,5},{5,4},{6,7},{7,6},{8,9},{9,8},{10,11... | collective-permute-start | bytes 24584 | tf_op jit(solution)/shard_map/ppermute | solution.py:378
  82.1 4.5 %collective-permute-start.37 = (f32[16,128]{1,0:T(8,128)S(1)}, f32[16,128]{1,0:T(8,128)S(1)}, u32[]{:S(2)}, u32[]{:S(2)}) collective-permute-start(f32[16,128]{1,0:T(8,128)S(1)} %get-tuple-element.111), channel_id=1, source_target_pairs={{0,3},{1,2},{2,1},{3,0},{4,7},{5,6},{6,5},{7,4},{8,11},{9,10},{10,... | collective-permute-start | bytes 24584 | tf_op jit(solution)/shard_map/ppermute | solution.py:378
  (18 other events, 122.6 us)

commit v2 on v1

--- a/solution.py
+++ b/solution.py
@@ -74,9 +74,27 @@
     return sum(terms[1:], terms[0])
 
 
-def velocity_body(v_ref, s_ref, b_ref, out_ref):
+def velocity_load_body(v_ref, s_ref, b_ref, out_ref, sem):
+    groups = sem.shape[0]
+    size = v_ref.shape[1] // groups
+    copies = []
+    for g in range(groups):
+        part = (slice(None), pl.ds(g * size, size))
+        copies.append(pltpu.make_async_copy(v_ref.at[part], out_ref.at[part], sem.at[g]))
+        copies[g].start()
+
+    def before(i):
+        if i % size == 0:
+            copies[i // size].wait()
+
+    velocity_body(out_ref, s_ref, b_ref, out_ref, before)
+
+
+def velocity_body(v_ref, s_ref, b_ref, out_ref, before=None):
     count = v_ref.shape[1]
     for i in range(count):
+        if before is not None:
+            before(i)
         gain = b_ref[i] * unit
         _, syy, szz, sxy, sxz, syz = (s_ref[c, i] for c in range(6))
         sxy_y, sxz_z = plane_shift(sxy, 0), plane_shift(sxz, 1)
@@ -153,7 +171,7 @@
         before, after = layers(kind)
         up += [row(axis, comp, count - before + k) for k in range(before)]
         down += [row(axis, comp, k) for k in range(after)]
-    for k in range(a_ref.shape[0]):
+    for k in range(max(len(up), len(down))):
         high = ref[up[min(k, len(up) - 1)]]
         low = ref[down[min(k, len(down) - 1)]]
         a_ref[k] = lax.select(even, high, low)
@@ -193,9 +211,15 @@
             for i, value in update.items():
                 at = row(axis, target, i)
                 out_ref[at] = out_ref[at] + (b_ref[mat(axis, i)] * unit) * value
-    if packs:
-        for axis in (0, 1):
-            pack(out_ref, axis, VELOCITY_FACE[axis], *packs[2 * axis : 2 * axis + 2])
+    for axis in (0, 1):
+        pack(out_ref, axis, VELOCITY_FACE[axis], *packs[2 * axis : 2 * axis + 2])
+
+
+def velocity_ride_body(own_ref, v_ref, b_ref, xa, xb, ya, yb, out_ref, *packs):
+    velocity_edge_body(v_ref, b_ref, xa, xb, ya, yb, out_ref, *packs)
+    last = packs[3].shape[0] - 1
+    packs[3][last - 1] = own_ref[...]
+    packs[3][last] = ya[ya.shape[0] - 1]
 
 
 def inverse_sinh(value):
@@ -224,7 +248,7 @@
 
 
 def stress_edge_body(
-    tile_ref, s_ref, lame_ref, shear_ref, b_ref, load_ref, normal_ref, rate_ref, state_ref, xa, xb, ya, yb,
+    owner_ref, s_ref, lame_ref, shear_ref, b_ref, load_ref, normal_ref, rate_ref, state_ref, xa, xb, ya, yb,
     out_ref, *rest
 ):
     for axis, a_ref, b_ref2 in ((0, xa, xb), (1, ya, yb)):
@@ -242,21 +266,21 @@
             for i, value in update.items():
                 at = row(axis, target, i)
                 out_ref[at] = out_ref[at] + (shear_ref[mat(axis, i)] * unit) * value
-    is_owner = tile_ref[lax.axis_index("strike")] == lax.axis_index("cross")
+    is_owner = owner_ref[...] > 0.5
     first = row(1, 3, 0)
     trial = out_ref[first]
     damping = 0.5 * jnp.sqrt(shear_ref[:, 0] / b_ref[:, 0])
     change, slip, evolved = friction(
         trial, damping, load_ref[...], normal_ref[...], rate_ref[...], state_ref[...]
     )
-    out_ref[first] = lax.select(is_owner, change, trial)
+    out_ref[first] = jnp.where(is_owner, change, trial)
     if len(rest[-1].shape) == 3:
         evolved_ref, *packs = rest
         evolved_ref[...] = evolved
         for axis in (0, 1):
             pack(out_ref, axis, STRESS_FACE[axis], *packs[2 * axis : 2 * axis + 2])
     else:
-        spread_out(slip, evolved, rest)
+        spread_out(jnp.where(is_owner, slip, 0.0), jnp.where(is_owner, evolved, 0.0), rest)
 
 
 def spread_out(slip, evolved, sends):
@@ -271,41 +295,32 @@
         send_ref[...] = jnp.where(place < rows, head, tail)[:, :lanes]
 
 
-def finish_body(tile_ref, send_ref, *refs):
-    *got, slip_ref, state_ref = refs
-    owner = tile_ref[lax.axis_index("strike")]
-    me = lax.axis_index("cross")
-    value = send_ref[...]
-    for r, ref in enumerate(got, 1):
-        value = lax.select(owner == (me ^ r), ref[...], value)
-    rows = slip_ref.shape[1]
-    slip_ref[...] = value[:, :rows]
-    state_ref[...] = pltpu.roll(value, rows, 1)[:, :rows]
-
-
-def own_body(*refs):
-    *parts, out_ref = refs
-    pieces = [ref[...] for ref in parts]
-    rest = out_ref.shape[1] - sum(p.shape[1] for p in pieces)
+def owner_body(tile_ref, owner_ref):
+    mine = tile_ref[lax.axis_index("strike")] == lax.axis_index("cross")
+    owner_ref[...] = jnp.full(owner_ref.shape, mine.astype(jnp.float32))
+
+
+def join(pieces, width):
+    rest = width - sum(p.shape[1] for p in pieces)
     if rest:
-        pieces.append(jnp.zeros((out_ref.shape[0], rest), out_ref.dtype))
-    out_ref[...] = jnp.concatenate(pieces, axis=1)
-
-
-def fault_body(*refs):
+        pieces.append(jnp.zeros((pieces[0].shape[0], rest), pieces[0].dtype))
+    return jnp.concatenate(pieces, axis=1)
+
+
+def fault_body(order, *refs):
     arrays = 4
     blocks, outs = refs[:-arrays], refs[-arrays:]
-    count, width = len(blocks), blocks[0].shape[1]
+    held = [block[...] for block in blocks]
+    count, width = len(held), held[0].shape[1]
     depth = outs[0].shape[1]
     rows = depth // count
-    me = lax.axis_index("cross")
-    held = [ref[...] for ref in blocks]
+    holder = order(lax.axis_index("cross"))
     place = lax.broadcasted_iota(jnp.int32, held[0].shape, 1)
     whole = [jnp.zeros_like(held[0])] * arrays
     for q in range(count):
         value = held[0]
-        for r in range(1, count):
-            value = lax.select((me ^ r) == q, held[r], value)
+        for at, block in zip(holder[1:], held[1:]):
+            value = lax.select(at == q, block, value)
         mine = (place >= q * rows) & (place < (q + 1) * rows)
         for k in range(arrays):
             shift = ((q - k) * rows) % width
@@ -315,9 +330,20 @@
         out_ref[...] = value[:, :depth]
 
 
-def pack_body(s_ref, *packs):
-    for axis in (0, 1):
-        pack(s_ref, axis, STRESS_FACE[axis], *packs[2 * axis : 2 * axis + 2])
+def pack_body(s_ref, *rest):
+    *sources, s_out, xa, xb, ya, yb, own_ref, part_ref, s_sem, part_sem = rest
+    copies = [pltpu.make_async_copy(ref, part_ref.at[k], part_sem.at[k]) for k, ref in enumerate(sources)]
+    copies += [pltpu.make_async_copy(s_ref.at[c], s_out.at[c], s_sem.at[c]) for c in range(s_ref.shape[0])]
+    for copy in copies:
+        copy.start()
+    for copy in copies:
+        copy.wait()
+    own = join([part_ref[k] for k in range(len(sources))], own_ref.shape[1])
+    own_ref[...] = own
+    for axis, a_ref, b_ref in ((0, xa, xb), (1, ya, yb)):
+        pack(s_out, axis, STRESS_FACE[axis], a_ref, b_ref)
+    if ya.shape[0] > yb.shape[0]:
+        ya[ya.shape[0] - 1] = own
 
 
 def swaps(pairs):
@@ -332,12 +358,19 @@
     strike_b = [(at(s, c), at(s + 1, c)) for s in range(1, n_strike - 1, 2) for c in range(n_cross)]
     cross_a = [(at(s, c), at(s, c + 1)) for s in range(n_strike) for c in range(0, n_cross - 1, 2)]
     cross_b = [(at(s, c), at(s, c + 1)) for s in range(n_strike) for c in range(1, n_cross - 1, 2)]
+    cross_ring = cross_b + [(at(s, 0), at(s, n_cross - 1)) for s in range(n_strike)]
     half = n_cross // 2
     for s in (0, n_strike - 1):
         strike_b += [(at(s, c), at(s, c + half)) for c in range(half)]
     for c in (0, n_cross - 1):
         cross_b += [(at(s, c), at(s + 1, c)) for s in range(0, n_strike - 1, 2)]
-    return tuple(swaps(p) for p in (strike_a, strike_b, cross_a, cross_b))
+    return tuple(swaps(p) for p in (strike_a, strike_b, cross_a, cross_b, cross_ring))
+
+
+def cycle_order(me):
+    size = lax.axis_size("cross")
+    far = lax.rem(me + jnp.where(lax.rem(me, 2) == 0, size - 1, 1), size)
+    return [me, me ^ 1, far, far ^ 1]
 
 
 def local(
@@ -345,7 +378,7 @@
 ):
     n_strike, n_cross = lax.axis_size("strike"), lax.axis_size("cross")
     axes = ("strike", "cross")
-    strike_a, strike_b, cross_a, cross_b = exchange_pairs(n_strike, n_cross)
+    strike_a, strike_b, cross_a, cross_b, cross_ring = exchange_pairs(n_strike, n_cross)
     _, nx, ny, nz = velocity.shape
     bz = prestress.shape[1]
     f32 = jnp.float32
@@ -366,8 +399,8 @@
             scratch_shapes=scratch,
         )(*ins)
 
-    def exchange(packs):
-        perms = dict(xa=strike_a, xb=strike_b, ya=cross_a, yb=cross_b)
+    def exchange(packs, wrap=False):
+        perms = dict(xa=strike_a, xb=strike_b, ya=cross_a, yb=cross_ring if wrap else cross_b)
         halos = {}
         for name, block in reversed(tuple(zip(perms, packs))):
             halos[name] = lax.ppermute(block, axes, perms[name])
@@ -377,45 +410,68 @@
         pairs = [(s * n_cross + c, s * n_cross + (c ^ r)) for s in range(n_strike) for c in range(n_cross)]
         return lax.ppermute(block, axes, pairs)
 
+    ride = n_cross == 4
     width = max(nz, 4 * bz)
-    (own,) = call(own_body, (prestress, normal_stress, rate_a, state), (vec(nx, width),))
-    packs = call(pack_body, (stress,), faces)
+    params = (prestress, normal_stress, rate_a, state)
+    outs = (like_s, *faces[:2], vec(thick + ride, nx, nz), faces[3], vec(nx, width))
+    sources = [pltpu.with_memory_space_constraint(x, pltpu.HBM) for x in (stress, *params)]
+    dma = pltpu.SemaphoreType.DMA
+    stress, *packs, own = call(
+        pack_body, sources, outs, [HBM] * 5,
+        scratch=[pltpu.VMEM((4, nx, bz), f32), dma((stress.shape[0],)), dma((4,))],
+    )
     for iteration in range(STEPS):
         first, last = iteration == 0, iteration == STEPS - 1
         halos = exchange(packs)
         if first:
-            blocks = [own] + [partner(own, r) for r in range(1, n_cross)]
-            *fault, fault_state = call(fault_body, blocks, (plane,) * 4)
-        (velocity,) = call(
-            velocity_body, (velocity, stress, buoyancy), (like_v,),
-            alias=None if first else 0,
-        )
-        velocity, *packs = call(
-            velocity_edge_body, (velocity, buoyancy, *halos), (like_v, *faces), alias=0,
-        )
-        halos = exchange(packs)
+            (owner,) = call(owner_body, (fault_tile,), (plane,), [SMEM])
+            source = pltpu.with_memory_space_constraint(velocity, pltpu.HBM)
+            (velocity,) = call(
+                velocity_load_body, (source, stress, buoyancy), (like_v,),
+                [HBM, VMEM, VMEM], scratch=[pltpu.SemaphoreType.DMA((4,))],
+            )
+        else:
+            (velocity,) = call(velocity_body, (velocity, stress, buoyancy), (like_v,), alias=0)
+        if first and ride:
+            velocity, *packs = call(
+                velocity_ride_body, (own, velocity, buoyancy, *halos),
+                (like_v, *faces[:3], vec(thick + 2, nx, nz)), alias=1,
+            )
+            near = halos[2]
+        else:
+            velocity, *packs = call(
+                velocity_edge_body, (velocity, buoyancy, *halos), (like_v, *faces), alias=0,
+            )
+        halos = exchange(packs, wrap=first and ride)
         body, outs, scratch = stress_body, (like_s,), ()
         if last:
             body, outs = stress_store_body, (like_s, Stored(vec(*velocity.shape)))
             scratch = [pltpu.SemaphoreType.DMA]
         stress, *stored = call(
             body, (stress, velocity, lame, shear), outs,
-            alias=None if first else 0, scratch=scratch,
-        )
+            alias=0, scratch=scratch,
+        )
+        if first:
+            if ride:
+                blocks, order = (own, near, halos[3]), cycle_order
+                body = lambda own, near, far, *outs: fault_body(
+                    order, own, near.at[thick], far.at[thick], far.at[thick + 1], *outs
+                )
+            else:
+                blocks = [own] + [partner(own, r) for r in range(1, n_cross)]
+                order = lambda me: [me ^ r for r in range(n_cross)]
+                body = lambda *refs: fault_body(order, *refs)
+            *fault, fault_state = call(body, blocks, (plane,) * 4)
         outs = (like_s,) + (vec(nx, 2 * bz),) * n_cross if last else (like_s, plane, *faces)
         stress, fault_state, *packs = call(
             stress_edge_body,
-            (fault_tile, stress, lame, shear, buoyancy, *fault, fault_state, *halos),
-            outs, [SMEM] + [VMEM] * 12, alias=1,
+            (owner, stress, lame, shear, buoyancy, *fault, fault_state, *halos),
+            outs, alias=1,
         )
 
     sends = [fault_state, *packs]
-    got = [partner(sends[r], r) for r in range(1, n_cross)]
-    slip_out, state_out = call(
-        finish_body, (fault_tile, sends[0], *got), (vec(nx, bz), vec(nx, bz)),
-        [SMEM] + [VMEM] * n_cross,
-    )
-    return (stored[0], stress, slip_out, state_out)
+    result = sum([partner(sends[r], r) for r in range(1, n_cross)], sends[0])
+    return (stored[0], stress, result[:, :bz], result[:, bz:])
 
 
 class Stored:

time: 88 us -> 76.4 us (0.87)
  waiting for transfers between devices: 29.8 us -> 24.6 us
  starting transfers between devices: 38.2 us -> 34.2 us
  local copies, waits for them, and re-layouts: 4.04 us -> 1.83 us
    ppermute x6 -> x3, waiting for transfers between devices: 8.85 us -> 2.02 us  [partner(): return lax.ppermute(block, axes, pairs)]
    ppermute x6 -> x3, starting transfers between devices: 9.92 us -> 4.57 us  [partner(): return lax.ppermute(block, axes, pairs)]
    unnamed x25 -> x9, local copies, waits for them, and re-layouts: 4.04 us -> 1.16 us
    ppermute x32, waiting for transfers between devices: 21 us -> 22.6 us  [exchange(): halos[name] = lax.ppermute(block, axes, perms[name])]
    ppermute x32, starting transfers between devices: 28.2 us -> 29.6 us  [exchange(): halos[name] = lax.ppermute(block, axes, perms[name])]
    pallas_call x20 -> x19, Pallas kernels: 14.8 us -> 14.7 us  [call(): pl.pallas_call(body, in_specs=[VMEM] * len(ins) if specs is None else spe...]
  transfers between devices with their start and end apart: 38 -> 35, of which waited for: 18 -> 17; matrix products, arithmetic and copies ran while one was open for 1% -> 1% of each run, Pallas kernels for 8% -> 12%
where the time goes in v2:
time: 76.4 us; the launch traced here: 76.2 us
  starting transfers between devices  34.2 us (45%)
  waiting for transfers between devices  24.6 us (32%)
  Pallas kernels  14.7 us (19%)
  local copies, waits for them, and re-layouts  1.83 us (2%)
  between operations  0.95 us (1%)
    ppermute x32, starting transfers between devices, exchange(): halos[name] = lax.ppermute(block, axes, perms[name])  29.6 us
    ppermute x32, waiting for transfers between devices, exchange(): halos[name] = lax.ppermute(block, axes, perms[name])  22.6 us
    pallas_call x19, Pallas kernels, call(): pl.pallas_call(body, in_specs=[VMEM] * len(ins) if specs is None else spe...  14.7 us
    ppermute x3, starting transfers between devices, partner(): return lax.ppermute(block, axes, pairs)  4.57 us
    ppermute x3, waiting for transfers between devices, partner(): return lax.ppermute(block, axes, pairs)  2.02 us
  transfers between devices with their start and end apart: 35, of which 17 were waited for; matrix products, arithmetic and copies ran while one was open for 1% of the time, Pallas kernels for 12%

profile of v2, /device:TPU:0, one launch (start us, length us, event | category | flops | bytes accessed | tf_op | source)
XLA Modules:
  0.0 76.2 jit_solution(15587883326171423612)
XLA Ops:
  0.6 1.6 %shard_map.130 = (f32[6,16,16,256]{3,2,1,0:T(8,128)S(1)}, f32[5,16,256]{2,1,0:T(8,128)S(1)}, f32[5,16,256]{2,1,0:T(8,128)S(1)}, f32[6,16,256]{2,1,0:T(8,128)S(1)...) custom-call(f32[6,16,16,256]{3,2,1,0:T(8,128)} %s_ref.1, f32[16,64]{1,0:T(8,128)} %rest_0_.1, f32[16,64]{1,0:T(8,128)} %rest_1_.1, ...), custom_call_target="tpu_custom_call" | custom-call | tf_op jit(solution)/shard_map/pallas_call | solution.py:392
  2.3 3.0 %collective-permute-start.2 = (f32[6,16,256]{2,1,0:T(8,128)S(1)}, f32[6,16,256]{2,1,0:T(8,128)S(1)}, u32[]{:S(2)}, u32[]{:S(2)}) collective-permute-start(f32[6,16,256]{2,1,0:T(8,128)S(1)} %get-tuple-element.63), channel_id=1, source_target_pairs={{0,1},{1,0},{2,3},{3,2},{4,5},{5,4},{6,7},{7,6},{8,9},{9,8},{10,11... | collective-permute-start | bytes 294920 | tf_op jit(solution)/shard_map/ppermute | solution.py:406
  5.3 1.5 %collective-permute-start.1 = (f32[5,16,256]{2,1,0:T(8,128)S(1)}, f32[5,16,256]{2,1,0:T(8,128)S(1)}, u32[]{:S(2)}, u32[]{:S(2)}) collective-permute-start(f32[5,16,256]{2,1,0:T(8,128)S(1)} %get-tuple-element.62), channel_id=1, source_target_pairs={{4,8},{8,4},{5,9},{9,5},{6,10},{10,6},{7,11},{11,7},{12,16},{16,12... | collective-permute-start | bytes 245768 | tf_op jit(solution)/shard_map/ppermute | solution.py:406
  7.0 2.0 %shard_map.131.v_ref = f32[3,16,16,256]{3,2,1,0:T(8,128)S(1)} custom-call(f32[3,16,16,256]{3,2,1,0:T(8,128)} %v_ref.1, f32[6,16,16,256]{3,2,1,0:T(8,128)S(1)} %get-tuple-element.59.s_ref, f32[16,16,256]{2,1,0:T(8,128)S(1)} %copy-done), custom_call_target="tpu_custom_call" | custom-call | tf_op jit(solution)/shard_map/pallas_call | solution.py:392
  10.1 1.6 %collective-permute-start.4 = (f32[7,16,256]{2,1,0:T(8,128)S(1)}, f32[7,16,256]{2,1,0:T(8,128)S(1)}, u32[]{:S(2)}, u32[]{:S(2)}) collective-permute-start(f32[7,16,256]{2,1,0:T(8,128)S(1)} %get-tuple-element.66), channel_id=1, source_target_pairs={{1,2},{2,1},{5,6},{6,5},{9,10},{10,9},{13,14},{14,13},{17,18},{18,... | collective-permute-start | bytes 344072 | tf_op jit(solution)/shard_map/ppermute | solution.py:406
  11.6 3.0 %collective-permute-start.6 = (f32[5,16,256]{2,1,0:T(8,128)S(1)}, f32[5,16,256]{2,1,0:T(8,128)S(1)}, u32[]{:S(2)}, u32[]{:S(2)}) collective-permute-start(f32[5,16,256]{2,1,0:T(8,128)S(1)} %get-tuple-element.72), channel_id=1, source_target_pairs={{4,8},{8,4},{5,9},{9,5},{6,10},{10,6},{7,11},{11,7},{12,16},{16,12... | collective-permute-start | bytes 245768 | tf_op jit(solution)/shard_map/ppermute | solution.py:406
  15.8 1.0 %shard_map.133.s_ref = f32[6,16,16,256]{3,2,1,0:T(8,128)S(1)} custom-call(f32[6,16,16,256]{3,2,1,0:T(8,128)S(1)} %get-tuple-element.59.s_ref, f32[3,16,16,256]{3,2,1,0:T(8,128)S(1)} %get-tuple-element.65.v_ref, f32[16,16,256]{2,1,0:T(8,128)S(1)} %copy-done.1, f32[16,16,256]{2,1,0:T(8,128)S(1)} %copy-done.2), custom_call_target="tpu_custom_call", output_to_operand_aliasing={{}: (0, {})} | custom-call | tf_op jit(solution)/shard_map/pallas_call | solution.py:392
  16.9 1.3 %collective-permute-done.6.xb = f32[5,16,256]{2,1,0:T(8,128)S(1)} collective-permute-done((f32[5,16,256]{2,1,0:T(8,128)S(1)}, f32[5,16,256]{2,1,0:T(8,128)S(1)}, u32[]{:S(2)}, u32[]{:S(2)}) %collective-permute-start.6) | collective-permute-done | bytes 81952 | tf_op jit(solution)/shard_map/ppermute | solution.py:406
  18.2 1.9 %collective-permute-done.7.ya = f32[5,16,256]{2,1,0:T(8,128)S(1)} collective-permute-done((f32[5,16,256]{2,1,0:T(8,128)S(1)}, f32[5,16,256]{2,1,0:T(8,128)S(1)}, u32[]{:S(2)}, u32[]{:S(2)}) %collective-permute-start.7) | collective-permute-done | bytes 81952 | tf_op jit(solution)/shard_map/ppermute | solution.py:406
  21.5 1.0 %collective-permute-start.10 = (f32[5,16,256]{2,1,0:T(8,128)S(1)}, f32[5,16,256]{2,1,0:T(8,128)S(1)}, u32[]{:S(2)}, u32[]{:S(2)}) collective-permute-start(f32[5,16,256]{2,1,0:T(8,128)S(1)} %get-tuple-element.77), channel_id=1, source_target_pairs={{0,1},{1,0},{2,3},{3,2},{4,5},{5,4},{6,7},{7,6},{8,9},{9,8},{10,11... | collective-permute-start | bytes 245768 | tf_op jit(solution)/shard_map/ppermute | solution.py:406
  23.9 1.5 %collective-permute-done.9.xb = f32[5,16,256]{2,1,0:T(8,128)S(1)} collective-permute-done((f32[5,16,256]{2,1,0:T(8,128)S(1)}, f32[5,16,256]{2,1,0:T(8,128)S(1)}, u32[]{:S(2)}, u32[]{:S(2)}) %collective-permute-start.9) | collective-permute-done | bytes 81952 | tf_op jit(solution)/shard_map/ppermute | solution.py:406
  25.4 1.2 %collective-permute-done.10.ya = f32[5,16,256]{2,1,0:T(8,128)S(1)} collective-permute-done((f32[5,16,256]{2,1,0:T(8,128)S(1)}, f32[5,16,256]{2,1,0:T(8,128)S(1)}, u32[]{:S(2)}, u32[]{:S(2)}) %collective-permute-start.10) | collective-permute-done | bytes 81952 | tf_op jit(solution)/shard_map/ppermute | solution.py:406
  27.3 3.0 %collective-permute-start.13 = (f32[5,16,256]{2,1,0:T(8,128)S(1)}, f32[5,16,256]{2,1,0:T(8,128)S(1)}, u32[]{:S(2)}, u32[]{:S(2)}) collective-permute-start(f32[5,16,256]{2,1,0:T(8,128)S(1)} %get-tuple-element.82), channel_id=1, source_target_pairs={{4,8},{8,4},{5,9},{9,5},{6,10},{10,6},{7,11},{11,7},{12,16},{16,12... | collective-permute-start | bytes 245768 | tf_op jit(solution)/shard_map/ppermute | solution.py:406
  30.3 1.2 %collective-permute-start.15 = (f32[5,16,256]{2,1,0:T(8,128)S(1)}, f32[5,16,256]{2,1,0:T(8,128)S(1)}, u32[]{:S(2)}, u32[]{:S(2)}) collective-permute-start(f32[5,16,256]{2,1,0:T(8,128)S(1)} %get-tuple-element.84), channel_id=1, source_target_pairs={{1,2},{2,1},{5,6},{6,5},{9,10},{10,9},{13,14},{14,13},{17,18},{18,... | collective-permute-start | bytes 245768 | tf_op jit(solution)/shard_map/ppermute | solution.py:406
  31.5 1.0 %shard_map.138.s_ref = f32[6,16,16,256]{3,2,1,0:T(8,128)S(1)} custom-call(f32[6,16,16,256]{3,2,1,0:T(8,128)S(1)} %get-tuple-element.74.s_ref, f32[3,16,16,256]{3,2,1,0:T(8,128)S(1)} %get-tuple-element.79.v_ref, f32[16,16,256]{2,1,0:T(8,128)S(1)} %copy-done.1, f32[16,16,256]{2,1,0:T(8,128)S(1)} %copy-done.2), custom_call_target="tpu_custom_call", output_to_operand_aliasing={{}: (0, {})} | custom-call | tf_op jit(solution)/shard_map/pallas_call | solution.py:392
  32.7 2.9 %collective-permute-done.14.ya = f32[5,16,256]{2,1,0:T(8,128)S(1)} collective-permute-done((f32[5,16,256]{2,1,0:T(8,128)S(1)}, f32[5,16,256]{2,1,0:T(8,128)S(1)}, u32[]{:S(2)}, u32[]{:S(2)}) %collective-permute-start.14) | collective-permute-done | bytes 81952 | tf_op jit(solution)/shard_map/ppermute | solution.py:406
  36.4 2.4 %collective-permute-start.17 = (f32[5,16,256]{2,1,0:T(8,128)S(1)}, f32[5,16,256]{2,1,0:T(8,128)S(1)}, u32[]{:S(2)}, u32[]{:S(2)}) collective-permute-start(f32[5,16,256]{2,1,0:T(8,128)S(1)} %get-tuple-element.87), channel_id=1, source_target_pairs={{4,8},{8,4},{5,9},{9,5},{6,10},{10,6},{7,11},{11,7},{12,16},{16,12... | collective-permute-start | bytes 245768 | tf_op jit(solution)/shard_map/ppermute | solution.py:406
  41.2 2.2 %collective-permute-done.18.ya = f32[5,16,256]{2,1,0:T(8,128)S(1)} collective-permute-done((f32[5,16,256]{2,1,0:T(8,128)S(1)}, f32[5,16,256]{2,1,0:T(8,128)S(1)}, u32[]{:S(2)}, u32[]{:S(2)}) %collective-permute-start.18) | collective-permute-done | bytes 81952 | tf_op jit(solution)/shard_map/ppermute | solution.py:406
  43.8 2.7 %collective-permute-start.21 = (f32[5,16,256]{2,1,0:T(8,128)S(1)}, f32[5,16,256]{2,1,0:T(8,128)S(1)}, u32[]{:S(2)}, u32[]{:S(2)}) collective-permute-start(f32[5,16,256]{2,1,0:T(8,128)S(1)} %get-tuple-element.93), channel_id=1, source_target_pairs={{4,8},{8,4},{5,9},{9,5},{6,10},{10,6},{7,11},{11,7},{12,16},{16,12... | collective-permute-start | bytes 245768 | tf_op jit(solution)/shard_map/ppermute | solution.py:406
  47.1 1.0 %shard_map.142.s_ref = f32[6,16,16,256]{3,2,1,0:T(8,128)S(1)} custom-call(f32[6,16,16,256]{3,2,1,0:T(8,128)S(1)} %get-tuple-element.85.s_ref, f32[3,16,16,256]{3,2,1,0:T(8,128)S(1)} %get-tuple-element.90.v_ref, f32[16,16,256]{2,1,0:T(8,128)S(1)} %copy-done.1, f32[16,16,256]{2,1,0:T(8,128)S(1)} %copy-done.2), custom_call_target="tpu_custom_call", output_to_operand_aliasing={{}: (0, {})} | custom-call | tf_op jit(solution)/shard_map/pallas_call | solution.py:392
  48.9 2.4 %collective-permute-done.22.ya = f32[5,16,256]{2,1,0:T(8,128)S(1)} collective-permute-done((f32[5,16,256]{2,1,0:T(8,128)S(1)}, f32[5,16,256]{2,1,0:T(8,128)S(1)}, u32[]{:S(2)}, u32[]{:S(2)}) %collective-permute-start.22) | collective-permute-done | bytes 81952 | tf_op jit(solution)/shard_map/ppermute | solution.py:406
  52.1 2.7 %collective-permute-start.25 = (f32[5,16,256]{2,1,0:T(8,128)S(1)}, f32[5,16,256]{2,1,0:T(8,128)S(1)}, u32[]{:S(2)}, u32[]{:S(2)}) collective-permute-start(f32[5,16,256]{2,1,0:T(8,128)S(1)} %get-tuple-element.98), channel_id=1, source_target_pairs={{4,8},{8,4},{5,9},{9,5},{6,10},{10,6},{7,11},{11,7},{12,16},{16,12... | collective-permute-start | bytes 245768 | tf_op jit(solution)/shard_map/ppermute | solution.py:406
  55.9 1.8 %collective-permute-done.25.xb = f32[5,16,256]{2,1,0:T(8,128)S(1)} collective-permute-done((f32[5,16,256]{2,1,0:T(8,128)S(1)}, f32[5,16,256]{2,1,0:T(8,128)S(1)}, u32[]{:S(2)}, u32[]{:S(2)}) %collective-permute-start.25) | collective-permute-done | bytes 81952 | tf_op jit(solution)/shard_map/ppermute | solution.py:406
  57.7 1.6 %collective-permute-done.26.ya = f32[5,16,256]{2,1,0:T(8,128)S(1)} collective-permute-done((f32[5,16,256]{2,1,0:T(8,128)S(1)}, f32[5,16,256]{2,1,0:T(8,128)S(1)}, u32[]{:S(2)}, u32[]{:S(2)}) %collective-permute-start.26) | collective-permute-done | bytes 81952 | tf_op jit(solution)/shard_map/ppermute | solution.py:406
  59.8 2.9 %collective-permute-start.29 = (f32[5,16,256]{2,1,0:T(8,128)S(1)}, f32[5,16,256]{2,1,0:T(8,128)S(1)}, u32[]{:S(2)}, u32[]{:S(2)}) collective-permute-start(f32[5,16,256]{2,1,0:T(8,128)S(1)} %get-tuple-element.106), channel_id=1, source_target_pairs={{4,8},{8,4},{5,9},{9,5},{6,10},{10,6},{7,11},{11,7},{12,16},{16,12... | collective-permute-start | bytes 245768 | tf_op jit(solution)/shard_map/ppermute | solution.py:406
  63.0 1.0 %shard_map.146 = (f32[6,16,16,256]{3,2,1,0:T(8,128)S(1)}, f32[3,16,16,256]{3,2,1,0:T(8,128)}) custom-call(f32[6,16,16,256]{3,2,1,0:T(8,128)S(1)} %get-tuple-element.96.s_ref, f32[3,16,16,256]{3,2,1,0:T(8,128)S(1)} %get-tuple-element.101.v_ref, f32[16,16,256]{2,1,0:T(8,128)S(1)} %copy-done.1, ...), custom_call_target="tpu_custom_call", output_to_operand_aliasing={{0}: (0, {})} | custom-call | tf_op jit(solution)/shard_map/pallas_call | solution.py:392
  64.0 1.6 %collective-permute-done.29.xb = f32[5,16,256]{2,1,0:T(8,128)S(1)} collective-permute-done((f32[5,16,256]{2,1,0:T(8,128)S(1)}, f32[5,16,256]{2,1,0:T(8,128)S(1)}, u32[]{:S(2)}, u32[]{:S(2)}) %collective-permute-start.29) | collective-permute-done | bytes 81952 | tf_op jit(solution)/shard_map/ppermute | solution.py:406
  65.6 1.6 %collective-permute-done.30.ya = f32[5,16,256]{2,1,0:T(8,128)S(1)} collective-permute-done((f32[5,16,256]{2,1,0:T(8,128)S(1)}, f32[5,16,256]{2,1,0:T(8,128)S(1)}, u32[]{:S(2)}, u32[]{:S(2)}) %collective-permute-start.30) | collective-permute-done | bytes 81952 | tf_op jit(solution)/shard_map/ppermute | solution.py:406
  67.8 3.0 %collective-permute-start.32 = (f32[16,128]{1,0:T(8,128)S(1)}, f32[16,128]{1,0:T(8,128)S(1)}, u32[]{:S(2)}, u32[]{:S(2)}) collective-permute-start(f32[16,128]{1,0:T(8,128)S(1)} %get-tuple-element.111), channel_id=1, source_target_pairs={{0,1},{1,0},{2,3},{3,2},{4,5},{5,4},{6,7},{7,6},{8,9},{9,8},{10,11... | collective-permute-start | bytes 24584 | tf_op jit(solution)/shard_map/ppermute | solution.py:411
  71.0 1.4 %collective-permute-start.34 = (f32[16,128]{1,0:T(8,128)S(1)}, f32[16,128]{1,0:T(8,128)S(1)}, u32[]{:S(2)}, u32[]{:S(2)}) collective-permute-start(f32[16,128]{1,0:T(8,128)S(1)} %get-tuple-element.113), channel_id=1, source_target_pairs={{0,3},{1,2},{2,1},{3,0},{4,7},{5,6},{6,5},{7,4},{8,11},{9,10},{10,... | collective-permute-start | bytes 24584 | tf_op jit(solution)/shard_map/ppermute | solution.py:411
  72.4 1.1 %copy.44 = f32[6,16,16,256]{3,2,1,0:T(8,128)} copy(f32[6,16,16,256]{3,2,1,0:T(8,128)S(1)} %get-tuple-element.117) | data formatting | bytes 3145728
  74.4 1.1 %collective-permute-done.34 = f32[16,128]{1,0:T(8,128)S(1)} collective-permute-done((f32[16,128]{1,0:T(8,128)S(1)}, f32[16,128]{1,0:T(8,128)S(1)}, u32[]{:S(2)}, u32[]{:S(2)}) %collective-permute-start.34) | collective-permute-done | bytes 8224 | tf_op jit(solution)/shard_map/ppermute | solution.py:411
  (68 shorter events, 16.3 us)
Async XLA Ops:
  2.3 7.5 %collective-permute-start.2 = (f32[6,16,256]{2,1,0:T(8,128)S(1)}, f32[6,16,256]{2,1,0:T(8,128)S(1)}, u32[]{:S(2)}, u32[]{:S(2)}) collective-permute-start(f32[6,16,256]{2,1,0:T(8,128)S(1)} %get-tuple-element.63), channel_id=1, source_target_pairs={{0,1},{1,0},{2,3},{3,2},{4,5},{5,4},{6,7},{7,6},{8,9},{9,8},{10,11... | collective-permute-start | bytes 294920 | tf_op jit(solution)/shard_map/ppermute | solution.py:406
  5.3 3.7 %collective-permute-start = (f32[5,16,256]{2,1,0:T(8,128)S(1)}, f32[5,16,256]{2,1,0:T(8,128)S(1)}, u32[]{:S(2)}, u32[]{:S(2)}) collective-permute-start(f32[5,16,256]{2,1,0:T(8,128)S(1)} %get-tuple-element.61), channel_id=1, source_target_pairs={{0,4},{4,0},{1,5},{5,1},{2,6},{6,2},{3,7},{7,3},{8,12},{12,8},{9,1... | collective-permute-start | bytes 245768 | tf_op jit(solution)/shard_map/ppermute | solution.py:406
  5.3 4.4 %collective-permute-start.1 = (f32[5,16,256]{2,1,0:T(8,128)S(1)}, f32[5,16,256]{2,1,0:T(8,128)S(1)}, u32[]{:S(2)}, u32[]{:S(2)}) collective-permute-start(f32[5,16,256]{2,1,0:T(8,128)S(1)} %get-tuple-element.62), channel_id=1, source_target_pairs={{4,8},{8,4},{5,9},{9,5},{6,10},{10,6},{7,11},{11,7},{12,16},{16,12... | collective-permute-start | bytes 245768 | tf_op jit(solution)/shard_map/ppermute | solution.py:406
  10.1 6.7 %collective-permute-start.4 = (f32[7,16,256]{2,1,0:T(8,128)S(1)}, f32[7,16,256]{2,1,0:T(8,128)S(1)}, u32[]{:S(2)}, u32[]{:S(2)}) collective-permute-start(f32[7,16,256]{2,1,0:T(8,128)S(1)} %get-tuple-element.66), channel_id=1, source_target_pairs={{1,2},{2,1},{5,6},{6,5},{9,10},{10,9},{13,14},{14,13},{17,18},{18,... | collective-permute-start | bytes 344072 | tf_op jit(solution)/shard_map/ppermute | solution.py:406
  11.6 5.2 %collective-permute-start.5 = (f32[5,16,256]{2,1,0:T(8,128)S(1)}, f32[5,16,256]{2,1,0:T(8,128)S(1)}, u32[]{:S(2)}, u32[]{:S(2)}) collective-permute-start(f32[5,16,256]{2,1,0:T(8,128)S(1)} %get-tuple-element.71), channel_id=1, source_target_pairs={{0,4},{4,0},{1,5},{5,1},{2,6},{6,2},{3,7},{7,3},{8,12},{12,8},{9,1... | collective-permute-start | bytes 245768 | tf_op jit(solution)/shard_map/ppermute | solution.py:406
  11.6 6.6 %collective-permute-start.6 = (f32[5,16,256]{2,1,0:T(8,128)S(1)}, f32[5,16,256]{2,1,0:T(8,128)S(1)}, u32[]{:S(2)}, u32[]{:S(2)}) collective-permute-start(f32[5,16,256]{2,1,0:T(8,128)S(1)} %get-tuple-element.72), channel_id=1, source_target_pairs={{4,8},{8,4},{5,9},{9,5},{6,10},{10,6},{7,11},{11,7},{12,16},{16,12... | collective-permute-start | bytes 245768 | tf_op jit(solution)/shard_map/ppermute | solution.py:406
  14.6 5.4 %collective-permute-start.7 = (f32[5,16,256]{2,1,0:T(8,128)S(1)}, f32[5,16,256]{2,1,0:T(8,128)S(1)}, u32[]{:S(2)}, u32[]{:S(2)}) collective-permute-start(f32[5,16,256]{2,1,0:T(8,128)S(1)} %get-tuple-element.73), channel_id=1, source_target_pairs={{0,1},{1,0},{2,3},{3,2},{4,5},{5,4},{6,7},{7,6},{8,9},{9,8},{10,11... | collective-permute-start | bytes 245768 | tf_op jit(solution)/shard_map/ppermute | solution.py:406
  20.8 4.5 %collective-permute-start.9 = (f32[5,16,256]{2,1,0:T(8,128)S(1)}, f32[5,16,256]{2,1,0:T(8,128)S(1)}, u32[]{:S(2)}, u32[]{:S(2)}) collective-permute-start(f32[5,16,256]{2,1,0:T(8,128)S(1)} %get-tuple-element.76), channel_id=1, source_target_pairs={{4,8},{8,4},{5,9},{9,5},{6,10},{10,6},{7,11},{11,7},{12,16},{16,12... | collective-permute-start | bytes 245768 | tf_op jit(solution)/shard_map/ppermute | solution.py:406
  21.5 5.1 %collective-permute-start.10 = (f32[5,16,256]{2,1,0:T(8,128)S(1)}, f32[5,16,256]{2,1,0:T(8,128)S(1)}, u32[]{:S(2)}, u32[]{:S(2)}) collective-permute-start(f32[5,16,256]{2,1,0:T(8,128)S(1)} %get-tuple-element.77), channel_id=1, source_target_pairs={{0,1},{1,0},{2,3},{3,2},{4,5},{5,4},{6,7},{7,6},{8,9},{9,8},{10,11... | collective-permute-start | bytes 245768 | tf_op jit(solution)/shard_map/ppermute | solution.py:406
  22.5 4.1 %collective-permute-start.11 = (f32[5,16,256]{2,1,0:T(8,128)S(1)}, f32[5,16,256]{2,1,0:T(8,128)S(1)}, u32[]{:S(2)}, u32[]{:S(2)}) collective-permute-start(f32[5,16,256]{2,1,0:T(8,128)S(1)} %get-tuple-element.78), channel_id=1, source_target_pairs={{1,2},{2,1},{5,6},{6,5},{9,10},{10,9},{13,14},{14,13},{17,18},{18,... | collective-permute-start | bytes 245768 | tf_op jit(solution)/shard_map/ppermute | solution.py:406
  26.9 5.6 %collective-permute-start.12 = (f32[5,16,256]{2,1,0:T(8,128)S(1)}, f32[5,16,256]{2,1,0:T(8,128)S(1)}, u32[]{:S(2)}, u32[]{:S(2)}) collective-permute-start(f32[5,16,256]{2,1,0:T(8,128)S(1)} %get-tuple-element.81), channel_id=1, source_target_pairs={{0,4},{4,0},{1,5},{5,1},{2,6},{6,2},{3,7},{7,3},{8,12},{12,8},{9,1... | collective-permute-start | bytes 245768 | tf_op jit(solution)/shard_map/ppermute | solution.py:406
  27.3 5.4 %collective-permute-start.13 = (f32[5,16,256]{2,1,0:T(8,128)S(1)}, f32[5,16,256]{2,1,0:T(8,128)S(1)}, u32[]{:S(2)}, u32[]{:S(2)}) collective-permute-start(f32[5,16,256]{2,1,0:T(8,128)S(1)} %get-tuple-element.82), channel_id=1, source_target_pairs={{4,8},{8,4},{5,9},{9,5},{6,10},{10,6},{7,11},{11,7},{12,16},{16,12... | collective-permute-start | bytes 245768 | tf_op jit(solution)/shard_map/ppermute | solution.py:406
  30.3 5.3 %collective-permute-start.14 = (f32[5,16,256]{2,1,0:T(8,128)S(1)}, f32[5,16,256]{2,1,0:T(8,128)S(1)}, u32[]{:S(2)}, u32[]{:S(2)}) collective-permute-start(f32[5,16,256]{2,1,0:T(8,128)S(1)} %get-tuple-element.83), channel_id=1, source_target_pairs={{0,1},{1,0},{2,3},{3,2},{4,5},{5,4},{6,7},{7,6},{8,9},{9,8},{10,11... | collective-permute-start | bytes 245768 | tf_op jit(solution)/shard_map/ppermute | solution.py:406
  30.3 5.3 %collective-permute-start.15 = (f32[5,16,256]{2,1,0:T(8,128)S(1)}, f32[5,16,256]{2,1,0:T(8,128)S(1)}, u32[]{:S(2)}, u32[]{:S(2)}) collective-permute-start(f32[5,16,256]{2,1,0:T(8,128)S(1)} %get-tuple-element.84), channel_id=1, source_target_pairs={{1,2},{2,1},{5,6},{6,5},{9,10},{10,9},{13,14},{14,13},{17,18},{18,... | collective-permute-start | bytes 245768 | tf_op jit(solution)/shard_map/ppermute | solution.py:406
  36.3 4.0 %collective-permute-start.16 = (f32[5,16,256]{2,1,0:T(8,128)S(1)}, f32[5,16,256]{2,1,0:T(8,128)S(1)}, u32[]{:S(2)}, u32[]{:S(2)}) collective-permute-start(f32[5,16,256]{2,1,0:T(8,128)S(1)} %get-tuple-element.86), channel_id=1, source_target_pairs={{0,4},{4,0},{1,5},{5,1},{2,6},{6,2},{3,7},{7,3},{8,12},{12,8},{9,1... | collective-permute-start | bytes 245768 | tf_op jit(solution)/shard_map/ppermute | solution.py:406
  36.4 4.8 %collective-permute-start.17 = (f32[5,16,256]{2,1,0:T(8,128)S(1)}, f32[5,16,256]{2,1,0:T(8,128)S(1)}, u32[]{:S(2)}, u32[]{:S(2)}) collective-permute-start(f32[5,16,256]{2,1,0:T(8,128)S(1)} %get-tuple-element.87), channel_id=1, source_target_pairs={{4,8},{8,4},{5,9},{9,5},{6,10},{10,6},{7,11},{11,7},{12,16},{16,12... | collective-permute-start | bytes 245768 | tf_op jit(solution)/shard_map/ppermute | solution.py:406
  38.8 4.6 %collective-permute-start.18 = (f32[5,16,256]{2,1,0:T(8,128)S(1)}, f32[5,16,256]{2,1,0:T(8,128)S(1)}, u32[]{:S(2)}, u32[]{:S(2)}) collective-permute-start(f32[5,16,256]{2,1,0:T(8,128)S(1)} %get-tuple-element.88), channel_id=1, source_target_pairs={{0,1},{1,0},{2,3},{3,2},{4,5},{5,4},{6,7},{7,6},{8,9},{9,8},{10,11... | collective-permute-start | bytes 245768 | tf_op jit(solution)/shard_map/ppermute | solution.py:406
  38.8 4.6 %collective-permute-start.19 = (f32[5,16,256]{2,1,0:T(8,128)S(1)}, f32[5,16,256]{2,1,0:T(8,128)S(1)}, u32[]{:S(2)}, u32[]{:S(2)}) collective-permute-start(f32[5,16,256]{2,1,0:T(8,128)S(1)} %get-tuple-element.89), channel_id=1, source_target_pairs={{1,2},{2,1},{5,6},{6,5},{9,10},{10,9},{13,14},{14,13},{17,18},{18,... | collective-permute-start | bytes 245768 | tf_op jit(solution)/shard_map/ppermute | solution.py:406
  43.7 4.4 %collective-permute-start.20 = (f32[5,16,256]{2,1,0:T(8,128)S(1)}, f32[5,16,256]{2,1,0:T(8,128)S(1)}, u32[]{:S(2)}, u32[]{:S(2)}) collective-permute-start(f32[5,16,256]{2,1,0:T(8,128)S(1)} %get-tuple-element.92), channel_id=1, source_target_pairs={{0,4},{4,0},{1,5},{5,1},{2,6},{6,2},{3,7},{7,3},{8,12},{12,8},{9,1... | collective-permute-start | bytes 245768 | tf_op jit(solution)/shard_map/ppermute | solution.py:406
  43.8 5.1 %collective-permute-start.21 = (f32[5,16,256]{2,1,0:T(8,128)S(1)}, f32[5,16,256]{2,1,0:T(8,128)S(1)}, u32[]{:S(2)}, u32[]{:S(2)}) collective-permute-start(f32[5,16,256]{2,1,0:T(8,128)S(1)} %get-tuple-element.93), channel_id=1, source_target_pairs={{4,8},{8,4},{5,9},{9,5},{6,10},{10,6},{7,11},{11,7},{12,16},{16,12... | collective-permute-start | bytes 245768 | tf_op jit(solution)/shard_map/ppermute | solution.py:406
  46.5 4.8 %collective-permute-start.22 = (f32[5,16,256]{2,1,0:T(8,128)S(1)}, f32[5,16,256]{2,1,0:T(8,128)S(1)}, u32[]{:S(2)}, u32[]{:S(2)}) collective-permute-start(f32[5,16,256]{2,1,0:T(8,128)S(1)} %get-tuple-element.94), channel_id=1, source_target_pairs={{0,1},{1,0},{2,3},{3,2},{4,5},{5,4},{6,7},{7,6},{8,9},{9,8},{10,11... | collective-permute-start | bytes 245768 | tf_op jit(solution)/shard_map/ppermute | solution.py:406
  46.7 4.6 %collective-permute-start.23 = (f32[5,16,256]{2,1,0:T(8,128)S(1)}, f32[5,16,256]{2,1,0:T(8,128)S(1)}, u32[]{:S(2)}, u32[]{:S(2)}) collective-permute-start(f32[5,16,256]{2,1,0:T(8,128)S(1)} %get-tuple-element.95), channel_id=1, source_target_pairs={{1,2},{2,1},{5,6},{6,5},{9,10},{10,9},{13,14},{14,13},{17,18},{18,... | collective-permute-start | bytes 245768 | tf_op jit(solution)/shard_map/ppermute | solution.py:406
  52.0 3.9 %collective-permute-start.24 = (f32[5,16,256]{2,1,0:T(8,128)S(1)}, f32[5,16,256]{2,1,0:T(8,128)S(1)}, u32[]{:S(2)}, u32[]{:S(2)}) collective-permute-start(f32[5,16,256]{2,1,0:T(8,128)S(1)} %get-tuple-element.97), channel_id=1, source_target_pairs={{0,4},{4,0},{1,5},{5,1},{2,6},{6,2},{3,7},{7,3},{8,12},{12,8},{9,1... | collective-permute-start | bytes 245768 | tf_op jit(solution)/shard_map/ppermute | solution.py:406
  52.1 5.6 %collective-permute-start.25 = (f32[5,16,256]{2,1,0:T(8,128)S(1)}, f32[5,16,256]{2,1,0:T(8,128)S(1)}, u32[]{:S(2)}, u32[]{:S(2)}) collective-permute-start(f32[5,16,256]{2,1,0:T(8,128)S(1)} %get-tuple-element.98), channel_id=1, source_target_pairs={{4,8},{8,4},{5,9},{9,5},{6,10},{10,6},{7,11},{11,7},{12,16},{16,12... | collective-permute-start | bytes 245768 | tf_op jit(solution)/shard_map/ppermute | solution.py:406
  54.8 4.4 %collective-permute-start.26 = (f32[5,16,256]{2,1,0:T(8,128)S(1)}, f32[5,16,256]{2,1,0:T(8,128)S(1)}, u32[]{:S(2)}, u32[]{:S(2)}) collective-permute-start(f32[5,16,256]{2,1,0:T(8,128)S(1)} %get-tuple-element.99), channel_id=1, source_target_pairs={{0,1},{1,0},{2,3},{3,2},{4,5},{5,4},{6,7},{7,6},{8,9},{9,8},{10,11... | collective-permute-start | bytes 245768 | tf_op jit(solution)/shard_map/ppermute | solution.py:406
  54.8 4.4 %collective-permute-start.27 = (f32[5,16,256]{2,1,0:T(8,128)S(1)}, f32[5,16,256]{2,1,0:T(8,128)S(1)}, u32[]{:S(2)}, u32[]{:S(2)}) collective-permute-start(f32[5,16,256]{2,1,0:T(8,128)S(1)} %get-tuple-element.100), channel_id=1, source_target_pairs={{1,2},{2,1},{5,6},{6,5},{9,10},{10,9},{13,14},{14,13},{17,18},{18,... | collective-permute-start | bytes 245768 | tf_op jit(solution)/shard_map/ppermute | solution.py:406
  59.8 4.2 %collective-permute-start.28 = (f32[5,16,256]{2,1,0:T(8,128)S(1)}, f32[5,16,256]{2,1,0:T(8,128)S(1)}, u32[]{:S(2)}, u32[]{:S(2)}) collective-permute-start(f32[5,16,256]{2,1,0:T(8,128)S(1)} %get-tuple-element.105), channel_id=1, source_target_pairs={{0,4},{4,0},{1,5},{5,1},{2,6},{6,2},{3,7},{7,3},{8,12},{12,8},{9,1... | collective-permute-start | bytes 245768 | tf_op jit(solution)/shard_map/ppermute | solution.py:406
  59.8 5.7 %collective-permute-start.29 = (f32[5,16,256]{2,1,0:T(8,128)S(1)}, f32[5,16,256]{2,1,0:T(8,128)S(1)}, u32[]{:S(2)}, u32[]{:S(2)}) collective-permute-start(f32[5,16,256]{2,1,0:T(8,128)S(1)} %get-tuple-element.106), channel_id=1, source_target_pairs={{4,8},{8,4},{5,9},{9,5},{6,10},{10,6},{7,11},{11,7},{12,16},{16,12... | collective-permute-start | bytes 245768 | tf_op jit(solution)/shard_map/ppermute | solution.py:406
  62.7 4.4 %collective-permute-start.30 = (f32[5,16,256]{2,1,0:T(8,128)S(1)}, f32[5,16,256]{2,1,0:T(8,128)S(1)}, u32[]{:S(2)}, u32[]{:S(2)}) collective-permute-start(f32[5,16,256]{2,1,0:T(8,128)S(1)} %get-tuple-element.107), channel_id=1, source_target_pairs={{0,1},{1,0},{2,3},{3,2},{4,5},{5,4},{6,7},{7,6},{8,9},{9,8},{10,11... | collective-permute-start | bytes 245768 | tf_op jit(solution)/shard_map/ppermute | solution.py:406
  62.9 4.2 %collective-permute-start.31 = (f32[5,16,256]{2,1,0:T(8,128)S(1)}, f32[5,16,256]{2,1,0:T(8,128)S(1)}, u32[]{:S(2)}, u32[]{:S(2)}) collective-permute-start(f32[5,16,256]{2,1,0:T(8,128)S(1)} %get-tuple-element.108), channel_id=1, source_target_pairs={{1,2},{2,1},{5,6},{6,5},{9,10},{10,9},{13,14},{14,13},{17,18},{18,... | collective-permute-start | bytes 245768 | tf_op jit(solution)/shard_map/ppermute | solution.py:406
  67.8 5.7 %collective-permute-start.32 = (f32[16,128]{1,0:T(8,128)S(1)}, f32[16,128]{1,0:T(8,128)S(1)}, u32[]{:S(2)}, u32[]{:S(2)}) collective-permute-start(f32[16,128]{1,0:T(8,128)S(1)} %get-tuple-element.111), channel_id=1, source_target_pairs={{0,1},{1,0},{2,3},{3,2},{4,5},{5,4},{6,7},{7,6},{8,9},{9,8},{10,11... | collective-permute-start | bytes 24584 | tf_op jit(solution)/shard_map/ppermute | solution.py:411
  71.0 4.5 %collective-permute-start.34 = (f32[16,128]{1,0:T(8,128)S(1)}, f32[16,128]{1,0:T(8,128)S(1)}, u32[]{:S(2)}, u32[]{:S(2)}) collective-permute-start(f32[16,128]{1,0:T(8,128)S(1)} %get-tuple-element.113), channel_id=1, source_target_pairs={{0,3},{1,2},{2,1},{3,0},{4,7},{5,6},{6,5},{7,4},{8,11},{9,10},{10,... | collective-permute-start | bytes 24584 | tf_op jit(solution)/shard_map/ppermute | solution.py:411
  (7 other events, 41.8 us)

commit v3 on v2

--- a/solution.py
+++ b/solution.py
@@ -1,3 +1,5 @@
+import functools
+
 import jax
 import jax.numpy as jnp
 from jax import lax
@@ -74,27 +76,37 @@
     return sum(terms[1:], terms[0])
 
 
-def velocity_load_body(v_ref, s_ref, b_ref, out_ref, sem):
+def velocity_load_body(
+    tile_ref, v_ref, s_ref, b_ref, out_ref, owner_ref, rows_ref, first_ref, sem, tile_smem, tile_sem
+):
     groups = sem.shape[0]
     size = v_ref.shape[1] // groups
-    copies = []
-    for g in range(groups):
-        part = (slice(None), pl.ds(g * size, size))
-        copies.append(pltpu.make_async_copy(v_ref.at[part], out_ref.at[part], sem.at[g]))
-        copies[g].start()
-
-    def before(i):
-        if i % size == 0:
-            copies[i // size].wait()
-
-    velocity_body(out_ref, s_ref, b_ref, out_ref, before)
-
-
-def velocity_body(v_ref, s_ref, b_ref, out_ref, before=None):
-    count = v_ref.shape[1]
+    parts = [(slice(None), pl.ds(g * size, size)) for g in range(groups)]
+    copies = [
+        pltpu.make_async_copy(v_ref.at[part], first_ref.at[part], sem.at[g])
+        for g, part in enumerate(parts)
+    ]
+    tile_copy = pltpu.make_async_copy(tile_ref, tile_smem, tile_sem)
+    for copy in (*copies, tile_copy):
+        copy.start()
+    for k, value in enumerate(edge_rows(b_ref, unit)):
+        rows_ref[k] = value
+    velocity_body(None, s_ref, b_ref, out_ref)
+    tile_copy.wait()
+    mine = tile_smem[lax.axis_index("strike")] == lax.axis_index("cross")
+    owner_ref[...] = jnp.full(owner_ref.shape, mine.astype(jnp.float32))
+    for copy, part in zip(copies, parts):
+        copy.wait()
+        out_ref[part] = out_ref[part] + first_ref[part]
+
+
+def velocity_body(v_ref, s_ref, b_ref, out_ref):
+    count = out_ref.shape[1]
+
+    def store(comp, i, more):
+        out_ref[comp, i] = more if v_ref is None else v_ref[comp, i] + more
+
     for i in range(count):
-        if before is not None:
-            before(i)
         gain = b_ref[i] * unit
         _, syy, szz, sxy, sxz, syz = (s_ref[c, i] for c in range(6))
         sxy_y, sxz_z = plane_shift(sxy, 0), plane_shift(sxz, 1)
@@ -103,19 +115,19 @@
             difference("b", sxy_y),
             difference("b", sxz_z),
         )
-        out_ref[0, i] = v_ref[0, i] + gain * force
+        store(0, i, gain * force)
         force = add(
             difference("b", strike_shift(s_ref, 3, i, count)),
             difference("f", plane_shift(syy, 0)),
             difference("b", plane_shift(syz, 1)),
         )
-        out_ref[1, i] = v_ref[1, i] + gain * force
+        store(1, i, gain * force)
         force = add(
             difference("b", strike_shift(s_ref, 4, i, count)),
             difference("b", plane_shift(syz, 0)),
             difference("f", plane_shift(szz, 1)),
         )
-        out_ref[2, i] = v_ref[2, i] + gain * force
+        store(2, i, gain * force)
 
 
 def stress_store_body(s_ref, v_ref, lame_ref, shear_ref, out_ref, store_ref, sem):
@@ -153,8 +165,13 @@
     return (comp, i) if axis == 0 else (comp, slice(None), i)
 
 
-def mat(axis, i):
-    return (i,) if axis == 0 else (slice(None), i)
+def slot(i, count):
+    return i if i < 2 else i - count + 4
+
+
+def edge_rows(ref, scale):
+    count = ref.shape[1]
+    return [ref[:, i] * scale for i in (0, 1, count - 2, count - 1)]
 
 
 def side(axis):
@@ -163,19 +180,33 @@
     return lax.rem(pos, 2) == 0, pos > 0, pos < size - 1
 
 
-def pack(ref, axis, spec, a_ref, b_ref):
+def pack_steps(ref, axis, spec, a_ref, b_ref, rows=None):
     even, _, _ = side(axis)
     count = ref.shape[1 + axis]
     up, down = [], []
     for comp, kind in spec:
         before, after = layers(kind)
-        up += [row(axis, comp, count - before + k) for k in range(before)]
-        down += [row(axis, comp, k) for k in range(after)]
-    for k in range(max(len(up), len(down))):
-        high = ref[up[min(k, len(up) - 1)]]
-        low = ref[down[min(k, len(down) - 1)]]
+        up += [(comp, count - before + k) for k in range(before)]
+        down += [(comp, k) for k in range(after)]
+
+    def read(comp, i):
+        if rows is not None:
+            return rows[comp, i]
+        return ref[row(axis, comp, i)]
+
+    def step(k, first, second):
+        high, low = read(*first), read(*second)
         a_ref[k] = lax.select(even, high, low)
         b_ref[k] = lax.select(even, low, high)
+
+    for k in range(max(len(up), len(down))):
+        first, second = up[min(k, len(up) - 1)], down[min(k, len(down) - 1)]
+        yield (first, second), functools.partial(step, k, first, second)
+
+
+def pack(*args):
+    for _, step in pack_steps(*args):
+        step()
 
 
 def halo_terms(axis, spec, count, a_ref, b_ref):
@@ -202,21 +233,30 @@
     return terms
 
 
-def velocity_edge_body(v_ref, b_ref, xa, xb, ya, yb, out_ref, *packs):
-    for axis, a_ref, b_ref2 in ((0, xa, xb), (1, ya, yb)):
-        count = v_ref.shape[1 + axis]
-        terms = halo_terms(axis, STRESS_FACE[axis], count, a_ref, b_ref2)
-        targets = (1, 2, 0) if axis == 0 else (0, 2, 1)
-        for target, update in zip(targets, terms):
-            for i, value in update.items():
-                at = row(axis, target, i)
-                out_ref[at] = out_ref[at] + (b_ref[mat(axis, i)] * unit) * value
-    for axis in (0, 1):
-        pack(out_ref, axis, VELOCITY_FACE[axis], *packs[2 * axis : 2 * axis + 2])
-
-
-def velocity_ride_body(own_ref, v_ref, b_ref, xa, xb, ya, yb, out_ref, *packs):
-    velocity_edge_body(v_ref, b_ref, xa, xb, ya, yb, out_ref, *packs)
+def grow(ref, at, more):
+    value = ref[at] + more
+    ref[at] = value
+    return value
+
+
+def velocity_edge_body(v_ref, b_ref, b_rows, xa, xb, ya, yb, out_ref, *packs):
+    count = v_ref.shape[1]
+    terms = halo_terms(0, STRESS_FACE[0], count, xa, xb)
+    for target, update in zip((1, 2, 0), terms):
+        for i, value in update.items():
+            grow(out_ref, row(0, target, i), (b_ref[i] * unit) * value)
+    count = v_ref.shape[2]
+    terms = halo_terms(1, STRESS_FACE[1], count, ya, yb)
+    rows = {}
+    for target, update in zip((0, 2, 1), terms):
+        for i, value in update.items():
+            rows[target, i] = grow(out_ref, row(1, target, i), b_rows[slot(i, count)] * value)
+    pack(out_ref, 1, VELOCITY_FACE[1], *packs[2:], rows)
+    pack(out_ref, 0, VELOCITY_FACE[0], *packs[:2])
+
+
+def velocity_ride_body(own_ref, v_ref, b_ref, b_rows, xa, xb, ya, yb, out_ref, *packs):
+    velocity_edge_body(v_ref, b_ref, b_rows, xa, xb, ya, yb, out_ref, *packs)
     last = packs[3].shape[0] - 1
     packs[3][last - 1] = own_ref[...]
     packs[3][last] = ya[ya.shape[0] - 1]
@@ -234,51 +274,85 @@
     strength = rate_a * normal_stress
     drag = damping * width
     scaled = inverse_sinh(total / drag)
+    yield
     for _ in range(NEWTON):
         grow, decay = 0.5 * jnp.exp(scaled), 0.5 * jnp.exp(-scaled)
         residual = strength * scaled + drag * (grow - decay) - total
         slope = strength + drag * (grow + decay)
         scaled = scaled - residual / slope
+        yield
     slip = width * (0.5 * jnp.exp(scaled) - 0.5 * jnp.exp(-scaled))
     traction = total - damping * slip
     evolved = state + evolve_rate * (
         jnp.exp((base_friction - state) / evolve_b) - jnp.abs(slip) / ref_rate
     )
-    return (traction - prestress, slip, evolved)
+    yield (traction - prestress, slip, evolved)
 
 
 def stress_edge_body(
-    owner_ref, s_ref, lame_ref, shear_ref, b_ref, load_ref, normal_ref, rate_ref, state_ref, xa, xb, ya, yb,
-    out_ref, *rest
+    owner_ref, s_ref, lame_ref, shear_ref, material_rows, damping_ref, load_ref, normal_ref,
+    rate_ref, state_ref, xa, xb, ya, yb, out_ref, *rest
 ):
-    for axis, a_ref, b_ref2 in ((0, xa, xb), (1, ya, yb)):
-        count = s_ref.shape[1 + axis]
-        terms = halo_terms(axis, VELOCITY_FACE[axis], count, a_ref, b_ref2)
-        for i, value in terms[0].items():
-            lam, mu = lame_ref[mat(axis, i)] * unit, shear_ref[mat(axis, i)] * unit
-            spread = lam * value
-            for comp in range(3):
-                at = row(axis, comp, i)
-                more = spread + 2.0 * mu * value if comp == axis else spread
-                out_ref[at] = out_ref[at] + more
-        targets = (3, 4) if axis == 0 else (3, 5)
-        for target, update in zip(targets, terms[1:]):
-            for i, value in update.items():
-                at = row(axis, target, i)
-                out_ref[at] = out_ref[at] + (shear_ref[mat(axis, i)] * unit) * value
+    rows = {}
+    counts = s_ref.shape[1:3]
+    terms = [
+        halo_terms(axis, VELOCITY_FACE[axis], counts[axis], a_ref, b_ref)
+        for axis, a_ref, b_ref in ((0, xa, xb), (1, ya, yb))
+    ]
+
+    def material(axis, kind, i):
+        if axis == 0:
+            return (lame_ref, shear_ref)[kind][i] * unit
+        return material_rows[4 * kind + slot(i, counts[axis])]
+
+    def correct(axis, comp, i, more):
+        value = grow(out_ref, row(axis, comp, i), more)
+        if axis == 1:
+            rows[comp, i] = value
+
+    def tangent(axis, comp, i, value):
+        correct(axis, comp, i, material(axis, 1, i) * value)
+
+    def normal(axis, i, value):
+        spread = material(axis, 0, i) * value
+        for comp in range(3):
+            more = spread + 2.0 * material(axis, 1, i) * value if comp == axis else spread
+            correct(axis, comp, i, more)
+
+    for i, value in terms[0][1].items():
+        tangent(0, 3, i, value)
+    tangent(1, 3, 0, terms[1][1].pop(0))
+    trial = rows[3, 0]
+    solve = friction(
+        trial, damping_ref[...], load_ref[...], normal_ref[...], rate_ref[...], state_ref[...]
+    )
+    work = [functools.partial(tangent, 1, 3, i, value) for i, value in terms[1][1].items()]
+    for axis, comp in ((0, 4), (1, 5)):
+        work += [functools.partial(tangent, axis, comp, i, value) for i, value in terms[axis][2].items()]
+    for axis in (0, 1):
+        work += [functools.partial(normal, axis, i, value) for i, value in terms[axis][0].items()]
+    after = []
+    packs = rest[1:] if len(rest[-1].shape) == 3 else ()
+    if packs:
+        for axis, held in ((1, rows), (0, None)):
+            for reads, step in pack_steps(
+                out_ref, axis, STRESS_FACE[axis], *packs[2 * axis : 2 * axis + 2], held
+            ):
+                late = any(comp == 3 and (axis == 0 or i == 0) for comp, i in reads)
+                (after if late else work).append(step)
+    stages = NEWTON + 1
+    for stage in range(stages):
+        next(solve)
+        for step in work[stage * len(work) // stages : (stage + 1) * len(work) // stages]:
+            step()
+    change, slip, evolved = next(solve)
     is_owner = owner_ref[...] > 0.5
-    first = row(1, 3, 0)
-    trial = out_ref[first]
-    damping = 0.5 * jnp.sqrt(shear_ref[:, 0] / b_ref[:, 0])
-    change, slip, evolved = friction(
-        trial, damping, load_ref[...], normal_ref[...], rate_ref[...], state_ref[...]
-    )
-    out_ref[first] = jnp.where(is_owner, change, trial)
-    if len(rest[-1].shape) == 3:
-        evolved_ref, *packs = rest
-        evolved_ref[...] = evolved
-        for axis in (0, 1):
-            pack(out_ref, axis, STRESS_FACE[axis], *packs[2 * axis : 2 * axis + 2])
+    rows[3, 0] = jnp.where(is_owner, change, trial)
+    out_ref[row(1, 3, 0)] = rows[3, 0]
+    for step in after:
+        step()
+    if packs:
+        rest[0][...] = evolved
     else:
         spread_out(jnp.where(is_owner, slip, 0.0), jnp.where(is_owner, evolved, 0.0), rest)
 
@@ -295,9 +369,10 @@
         send_ref[...] = jnp.where(place < rows, head, tail)[:, :lanes]
 
 
-def owner_body(tile_ref, owner_ref):
-    mine = tile_ref[lax.axis_index("strike")] == lax.axis_index("cross")
-    owner_ref[...] = jnp.full(owner_ref.shape, mine.astype(jnp.float32))
+def stress_rows_body(b_ref, lame_ref, shear_ref, rows_ref, damping_ref):
+    for k, value in enumerate(edge_rows(lame_ref, unit) + edge_rows(shear_ref, unit)):
+        rows_ref[k] = value
+    damping_ref[...] = 0.5 * jnp.sqrt(shear_ref[:, 0] / b_ref[:, 0])
 
 
 def join(pieces, width):
@@ -424,25 +499,29 @@
         first, last = iteration == 0, iteration == STEPS - 1
         halos = exchange(packs)
         if first:
-            (owner,) = call(owner_body, (fault_tile,), (plane,), [SMEM])
-            source = pltpu.with_memory_space_constraint(velocity, pltpu.HBM)
-            (velocity,) = call(
-                velocity_load_body, (source, stress, buoyancy), (like_v,),
-                [HBM, VMEM, VMEM], scratch=[pltpu.SemaphoreType.DMA((4,))],
+            sources = [pltpu.with_memory_space_constraint(x, pltpu.HBM) for x in (fault_tile, velocity)]
+            velocity, owner, b_rows = call(
+                velocity_load_body, (*sources, stress, buoyancy),
+                (like_v, plane, vec(4, nx, nz)), [HBM, HBM, VMEM, VMEM],
+                scratch=[
+                    pltpu.VMEM(velocity.shape, f32), dma((4,)), pltpu.SMEM(fault_tile.shape, jnp.int32), dma
+                ],
             )
         else:
             (velocity,) = call(velocity_body, (velocity, stress, buoyancy), (like_v,), alias=0)
         if first and ride:
             velocity, *packs = call(
-                velocity_ride_body, (own, velocity, buoyancy, *halos),
+                velocity_ride_body, (own, velocity, buoyancy, b_rows, *halos),
                 (like_v, *faces[:3], vec(thick + 2, nx, nz)), alias=1,
             )
             near = halos[2]
         else:
             velocity, *packs = call(
-                velocity_edge_body, (velocity, buoyancy, *halos), (like_v, *faces), alias=0,
+                velocity_edge_body, (velocity, buoyancy, b_rows, *halos), (like_v, *faces), alias=0,
             )
         halos = exchange(packs, wrap=first and ride)
+        if first:
+            rows, damping = call(stress_rows_body, (buoyancy, lame, shear), (vec(8, nx, nz), plane))
         body, outs, scratch = stress_body, (like_s,), ()
         if last:
             body, outs = stress_store_body, (like_s, Stored(vec(*velocity.shape)))
@@ -465,7 +544,7 @@
         outs = (like_s,) + (vec(nx, 2 * bz),) * n_cross if last else (like_s, plane, *faces)
         stress, fault_state, *packs = call(
             stress_edge_body,
-            (owner, stress, lame, shear, buoyancy, *fault, fault_state, *halos),
+            (owner, stress, lame, shear, rows, damping, *fault, fault_state, *halos),
             outs, alias=1,
         )
 

time: 76.4 us -> 74.8 us (0.979)
  Pallas kernels: 14.7 us -> 12.5 us
    pallas_call x19, Pallas kernels: 14.7 us -> 12.5 us  [call(): pl.pallas_call(body, in_specs=[VMEM] * len(ins) if specs is None else spe...]
  transfers between devices with their start and end apart: 35 -> 35, of which waited for: 17 -> 17; matrix products, arithmetic and copies ran while one was open for 1% -> 2% of each run, Pallas kernels for 12% -> 11%
where the time goes in v3:
time: 74.8 us; the launch traced here: 74.6 us
  starting transfers between devices  34.2 us (46%)
  waiting for transfers between devices  25.2 us (34%)
  Pallas kernels  12.5 us (17%)
  local copies, waits for them, and re-layouts  1.83 us (2%)
  between operations  0.9 us (1%)
    ppermute x32, starting transfers between devices, exchange(): halos[name] = lax.ppermute(block, axes, perms[name])  29.6 us
    ppermute x32, waiting for transfers between devices, exchange(): halos[name] = lax.ppermute(block, axes, perms[name])  23.2 us
    pallas_call x19, Pallas kernels, call(): pl.pallas_call(body, in_specs=[VMEM] * len(ins) if specs is None else spe...  12.5 us
    ppermute x3, starting transfers between devices, partner(): return lax.ppermute(block, axes, pairs)  4.57 us
    ppermute x3, waiting for transfers between devices, partner(): return lax.ppermute(block, axes, pairs)  2.02 us
  transfers between devices with their start and end apart: 35, of which 17 were waited for; matrix products, arithmetic and copies ran while one was open for 2% of the time, Pallas kernels for 11%

profile of v3, /device:TPU:0, one launch (start us, length us, event | category | flops | bytes accessed | tf_op | source)
XLA Modules:
  0.0 74.6 jit_solution(17190917026385466371)
XLA Ops:
  0.6 1.6 %shard_map.129 = (f32[6,16,16,256]{3,2,1,0:T(8,128)S(1)}, f32[5,16,256]{2,1,0:T(8,128)S(1)}, f32[5,16,256]{2,1,0:T(8,128)S(1)}, f32[6,16,256]{2,1,0:T(8,128)S(1)...) custom-call(f32[6,16,16,256]{3,2,1,0:T(8,128)} %s_ref.1, f32[16,64]{1,0:T(8,128)} %rest_0_.1, f32[16,64]{1,0:T(8,128)} %rest_1_.1, ...), custom_call_target="tpu_custom_call" | custom-call | tf_op jit(solution)/shard_map/pallas_call | solution.py:467
  2.3 3.0 %collective-permute-start.2 = (f32[6,16,256]{2,1,0:T(8,128)S(1)}, f32[6,16,256]{2,1,0:T(8,128)S(1)}, u32[]{:S(2)}, u32[]{:S(2)}) collective-permute-start(f32[6,16,256]{2,1,0:T(8,128)S(1)} %get-tuple-element.71), channel_id=1, source_target_pairs={{0,1},{1,0},{2,3},{3,2},{4,5},{5,4},{6,7},{7,6},{8,9},{9,8},{10,11... | collective-permute-start | bytes 294920 | tf_op jit(solution)/shard_map/ppermute | solution.py:481
  5.3 1.5 %collective-permute-start.1 = (f32[5,16,256]{2,1,0:T(8,128)S(1)}, f32[5,16,256]{2,1,0:T(8,128)S(1)}, u32[]{:S(2)}, u32[]{:S(2)}) collective-permute-start(f32[5,16,256]{2,1,0:T(8,128)S(1)} %get-tuple-element.70), channel_id=1, source_target_pairs={{4,8},{8,4},{5,9},{9,5},{6,10},{10,6},{7,11},{11,7},{12,16},{16,12... | collective-permute-start | bytes 245768 | tf_op jit(solution)/shard_map/ppermute | solution.py:481
  7.0 1.9 %shard_map.130 = (f32[3,16,16,256]{3,2,1,0:T(8,128)S(1)}, f32[16,256]{1,0:T(8,128)S(1)}, f32[4,16,256]{2,1,0:T(8,128)S(1)}) custom-call(s32[8]{0:T(128)} %tile_ref.1, f32[3,16,16,256]{3,2,1,0:T(8,128)} %v_ref.1, f32[6,16,16,256]{3,2,1,0:T(8,128)S(1)} %get-tuple-element.64.s_ref, f32[16,16,256]{2,1,0:T(8,128)S(1)} %copy-done.2), custom_call_target="tpu_custom_call" | custom-call | tf_op jit(solution)/shard_map/pallas_call | solution.py:467
  10.0 1.6 %collective-permute-start.4 = (f32[7,16,256]{2,1,0:T(8,128)S(1)}, f32[7,16,256]{2,1,0:T(8,128)S(1)}, u32[]{:S(2)}, u32[]{:S(2)}) collective-permute-start(f32[7,16,256]{2,1,0:T(8,128)S(1)} %get-tuple-element.76), channel_id=1, source_target_pairs={{1,2},{2,1},{5,6},{6,5},{9,10},{10,9},{13,14},{14,13},{17,18},{18,... | collective-permute-start | bytes 344072 | tf_op jit(solution)/shard_map/ppermute | solution.py:481
  11.5 3.0 %collective-permute-start.6 = (f32[5,16,256]{2,1,0:T(8,128)S(1)}, f32[5,16,256]{2,1,0:T(8,128)S(1)}, u32[]{:S(2)}, u32[]{:S(2)}) collective-permute-start(f32[5,16,256]{2,1,0:T(8,128)S(1)} %get-tuple-element.82), channel_id=1, source_target_pairs={{4,8},{8,4},{5,9},{9,5},{6,10},{10,6},{7,11},{11,7},{12,16},{16,12... | collective-permute-start | bytes 245768 | tf_op jit(solution)/shard_map/ppermute | solution.py:481
  15.2 1.0 %shard_map.132.s_ref = f32[6,16,16,256]{3,2,1,0:T(8,128)S(1)} custom-call(f32[6,16,16,256]{3,2,1,0:T(8,128)S(1)} %get-tuple-element.64.s_ref, f32[3,16,16,256]{3,2,1,0:T(8,128)S(1)} %get-tuple-element.73.v_ref, f32[16,16,256]{2,1,0:T(8,128)S(1)} %copy-done, f32[16,16,256]{2,1,0:T(8,128)S(1)} %copy-done.1), custom_call_target="tpu_custom_call", output_to_operand_aliasing={{}: (0, {})} | custom-call | tf_op jit(solution)/shard_map/pallas_call | solution.py:467
  16.3 1.8 %collective-permute-done.6.xb = f32[5,16,256]{2,1,0:T(8,128)S(1)} collective-permute-done((f32[5,16,256]{2,1,0:T(8,128)S(1)}, f32[5,16,256]{2,1,0:T(8,128)S(1)}, u32[]{:S(2)}, u32[]{:S(2)}) %collective-permute-start.6) | collective-permute-done | bytes 81952 | tf_op jit(solution)/shard_map/ppermute | solution.py:481
  18.1 1.9 %collective-permute-done.7.ya = f32[5,16,256]{2,1,0:T(8,128)S(1)} collective-permute-done((f32[5,16,256]{2,1,0:T(8,128)S(1)}, f32[5,16,256]{2,1,0:T(8,128)S(1)}, u32[]{:S(2)}, u32[]{:S(2)}) %collective-permute-start.7) | collective-permute-done | bytes 81952 | tf_op jit(solution)/shard_map/ppermute | solution.py:481
  21.1 1.0 %collective-permute-start.10 = (f32[5,16,256]{2,1,0:T(8,128)S(1)}, f32[5,16,256]{2,1,0:T(8,128)S(1)}, u32[]{:S(2)}, u32[]{:S(2)}) collective-permute-start(f32[5,16,256]{2,1,0:T(8,128)S(1)} %get-tuple-element.87), channel_id=1, source_target_pairs={{0,1},{1,0},{2,3},{3,2},{4,5},{5,4},{6,7},{7,6},{8,9},{9,8},{10,11... | collective-permute-start | bytes 245768 | tf_op jit(solution)/shard_map/ppermute | solution.py:481
  23.5 1.5 %collective-permute-done.9.xb = f32[5,16,256]{2,1,0:T(8,128)S(1)} collective-permute-done((f32[5,16,256]{2,1,0:T(8,128)S(1)}, f32[5,16,256]{2,1,0:T(8,128)S(1)}, u32[]{:S(2)}, u32[]{:S(2)}) %collective-permute-start.9) | collective-permute-done | bytes 81952 | tf_op jit(solution)/shard_map/ppermute | solution.py:481
  25.0 1.2 %collective-permute-done.10.ya = f32[5,16,256]{2,1,0:T(8,128)S(1)} collective-permute-done((f32[5,16,256]{2,1,0:T(8,128)S(1)}, f32[5,16,256]{2,1,0:T(8,128)S(1)}, u32[]{:S(2)}, u32[]{:S(2)}) %collective-permute-start.10) | collective-permute-done | bytes 81952 | tf_op jit(solution)/shard_map/ppermute | solution.py:481
  26.7 3.0 %collective-permute-start.13 = (f32[5,16,256]{2,1,0:T(8,128)S(1)}, f32[5,16,256]{2,1,0:T(8,128)S(1)}, u32[]{:S(2)}, u32[]{:S(2)}) collective-permute-start(f32[5,16,256]{2,1,0:T(8,128)S(1)} %get-tuple-element.92), channel_id=1, source_target_pairs={{4,8},{8,4},{5,9},{9,5},{6,10},{10,6},{7,11},{11,7},{12,16},{16,12... | collective-permute-start | bytes 245768 | tf_op jit(solution)/shard_map/ppermute | solution.py:481
  29.8 1.2 %collective-permute-start.15 = (f32[5,16,256]{2,1,0:T(8,128)S(1)}, f32[5,16,256]{2,1,0:T(8,128)S(1)}, u32[]{:S(2)}, u32[]{:S(2)}) collective-permute-start(f32[5,16,256]{2,1,0:T(8,128)S(1)} %get-tuple-element.94), channel_id=1, source_target_pairs={{1,2},{2,1},{5,6},{6,5},{9,10},{10,9},{13,14},{14,13},{17,18},{18,... | collective-permute-start | bytes 245768 | tf_op jit(solution)/shard_map/ppermute | solution.py:481
  31.0 1.0 %shard_map.138.s_ref = f32[6,16,16,256]{3,2,1,0:T(8,128)S(1)} custom-call(f32[6,16,16,256]{3,2,1,0:T(8,128)S(1)} %get-tuple-element.84.s_ref, f32[3,16,16,256]{3,2,1,0:T(8,128)S(1)} %get-tuple-element.89.v_ref, f32[16,16,256]{2,1,0:T(8,128)S(1)} %copy-done, f32[16,16,256]{2,1,0:T(8,128)S(1)} %copy-done.1), custom_call_target="tpu_custom_call", output_to_operand_aliasing={{}: (0, {})} | custom-call | tf_op jit(solution)/shard_map/pallas_call | solution.py:467
  32.2 2.9 %collective-permute-done.14.ya = f32[5,16,256]{2,1,0:T(8,128)S(1)} collective-permute-done((f32[5,16,256]{2,1,0:T(8,128)S(1)}, f32[5,16,256]{2,1,0:T(8,128)S(1)}, u32[]{:S(2)}, u32[]{:S(2)}) %collective-permute-start.14) | collective-permute-done | bytes 81952 | tf_op jit(solution)/shard_map/ppermute | solution.py:481
  35.6 2.4 %collective-permute-start.17 = (f32[5,16,256]{2,1,0:T(8,128)S(1)}, f32[5,16,256]{2,1,0:T(8,128)S(1)}, u32[]{:S(2)}, u32[]{:S(2)}) collective-permute-start(f32[5,16,256]{2,1,0:T(8,128)S(1)} %get-tuple-element.97), channel_id=1, source_target_pairs={{4,8},{8,4},{5,9},{9,5},{6,10},{10,6},{7,11},{11,7},{12,16},{16,12... | collective-permute-start | bytes 245768 | tf_op jit(solution)/shard_map/ppermute | solution.py:481
  40.4 2.2 %collective-permute-done.18.ya = f32[5,16,256]{2,1,0:T(8,128)S(1)} collective-permute-done((f32[5,16,256]{2,1,0:T(8,128)S(1)}, f32[5,16,256]{2,1,0:T(8,128)S(1)}, u32[]{:S(2)}, u32[]{:S(2)}) %collective-permute-start.18) | collective-permute-done | bytes 81952 | tf_op jit(solution)/shard_map/ppermute | solution.py:481
  42.8 2.7 %collective-permute-start.21 = (f32[5,16,256]{2,1,0:T(8,128)S(1)}, f32[5,16,256]{2,1,0:T(8,128)S(1)}, u32[]{:S(2)}, u32[]{:S(2)}) collective-permute-start(f32[5,16,256]{2,1,0:T(8,128)S(1)} %get-tuple-element.103), channel_id=1, source_target_pairs={{4,8},{8,4},{5,9},{9,5},{6,10},{10,6},{7,11},{11,7},{12,16},{16,12... | collective-permute-start | bytes 245768 | tf_op jit(solution)/shard_map/ppermute | solution.py:481
  46.1 1.0 %shard_map.142.s_ref = f32[6,16,16,256]{3,2,1,0:T(8,128)S(1)} custom-call(f32[6,16,16,256]{3,2,1,0:T(8,128)S(1)} %get-tuple-element.95.s_ref, f32[3,16,16,256]{3,2,1,0:T(8,128)S(1)} %get-tuple-element.100.v_ref, f32[16,16,256]{2,1,0:T(8,128)S(1)} %copy-done, f32[16,16,256]{2,1,0:T(8,128)S(1)} %copy-done.1), custom_call_target="tpu_custom_call", output_to_operand_aliasing={{}: (0, {})} | custom-call | tf_op jit(solution)/shard_map/pallas_call | solution.py:467
  48.0 2.4 %collective-permute-done.22.ya = f32[5,16,256]{2,1,0:T(8,128)S(1)} collective-permute-done((f32[5,16,256]{2,1,0:T(8,128)S(1)}, f32[5,16,256]{2,1,0:T(8,128)S(1)}, u32[]{:S(2)}, u32[]{:S(2)}) %collective-permute-start.22) | collective-permute-done | bytes 81952 | tf_op jit(solution)/shard_map/ppermute | solution.py:481
  50.9 2.7 %collective-permute-start.25 = (f32[5,16,256]{2,1,0:T(8,128)S(1)}, f32[5,16,256]{2,1,0:T(8,128)S(1)}, u32[]{:S(2)}, u32[]{:S(2)}) collective-permute-start(f32[5,16,256]{2,1,0:T(8,128)S(1)} %get-tuple-element.108), channel_id=1, source_target_pairs={{4,8},{8,4},{5,9},{9,5},{6,10},{10,6},{7,11},{11,7},{12,16},{16,12... | collective-permute-start | bytes 245768 | tf_op jit(solution)/shard_map/ppermute | solution.py:481
  54.7 1.8 %collective-permute-done.25.xb = f32[5,16,256]{2,1,0:T(8,128)S(1)} collective-permute-done((f32[5,16,256]{2,1,0:T(8,128)S(1)}, f32[5,16,256]{2,1,0:T(8,128)S(1)}, u32[]{:S(2)}, u32[]{:S(2)}) %collective-permute-start.25) | collective-permute-done | bytes 81952 | tf_op jit(solution)/shard_map/ppermute | solution.py:481
  56.5 1.6 %collective-permute-done.26.ya = f32[5,16,256]{2,1,0:T(8,128)S(1)} collective-permute-done((f32[5,16,256]{2,1,0:T(8,128)S(1)}, f32[5,16,256]{2,1,0:T(8,128)S(1)}, u32[]{:S(2)}, u32[]{:S(2)}) %collective-permute-start.26) | collective-permute-done | bytes 81952 | tf_op jit(solution)/shard_map/ppermute | solution.py:481
  58.3 2.9 %collective-permute-start.29 = (f32[5,16,256]{2,1,0:T(8,128)S(1)}, f32[5,16,256]{2,1,0:T(8,128)S(1)}, u32[]{:S(2)}, u32[]{:S(2)}) collective-permute-start(f32[5,16,256]{2,1,0:T(8,128)S(1)} %get-tuple-element.116), channel_id=1, source_target_pairs={{4,8},{8,4},{5,9},{9,5},{6,10},{10,6},{7,11},{11,7},{12,16},{16,12... | collective-permute-start | bytes 245768 | tf_op jit(solution)/shard_map/ppermute | solution.py:481
  61.5 1.0 %shard_map.146 = (f32[6,16,16,256]{3,2,1,0:T(8,128)S(1)}, f32[3,16,16,256]{3,2,1,0:T(8,128)}) custom-call(f32[6,16,16,256]{3,2,1,0:T(8,128)S(1)} %get-tuple-element.106.s_ref, f32[3,16,16,256]{3,2,1,0:T(8,128)S(1)} %get-tuple-element.111.v_ref, f32[16,16,256]{2,1,0:T(8,128)S(1)} %copy-done, f32[16,16,256]{2,1,0:T(8,128)S(1)} %copy-done.1), custom_call_target="tpu_custom_call", output_to_operand_aliasing={{0}: (0, {})} | custom-call | tf_op jit(solution)/shard_map/pallas_call | solution.py:467
  62.5 1.6 %collective-permute-done.29.xb = f32[5,16,256]{2,1,0:T(8,128)S(1)} collective-permute-done((f32[5,16,256]{2,1,0:T(8,128)S(1)}, f32[5,16,256]{2,1,0:T(8,128)S(1)}, u32[]{:S(2)}, u32[]{:S(2)}) %collective-permute-start.29) | collective-permute-done | bytes 81952 | tf_op jit(solution)/shard_map/ppermute | solution.py:481
  64.1 1.6 %collective-permute-done.30.ya = f32[5,16,256]{2,1,0:T(8,128)S(1)} collective-permute-done((f32[5,16,256]{2,1,0:T(8,128)S(1)}, f32[5,16,256]{2,1,0:T(8,128)S(1)}, u32[]{:S(2)}, u32[]{:S(2)}) %collective-permute-start.30) | collective-permute-done | bytes 81952 | tf_op jit(solution)/shard_map/ppermute | solution.py:481
  66.2 3.0 %collective-permute-start.32 = (f32[16,128]{1,0:T(8,128)S(1)}, f32[16,128]{1,0:T(8,128)S(1)}, u32[]{:S(2)}, u32[]{:S(2)}) collective-permute-start(f32[16,128]{1,0:T(8,128)S(1)} %get-tuple-element.121), channel_id=1, source_target_pairs={{0,1},{1,0},{2,3},{3,2},{4,5},{5,4},{6,7},{7,6},{8,9},{9,8},{10,11... | collective-permute-start | bytes 24584 | tf_op jit(solution)/shard_map/ppermute | solution.py:486
  69.4 1.4 %collective-permute-start.34 = (f32[16,128]{1,0:T(8,128)S(1)}, f32[16,128]{1,0:T(8,128)S(1)}, u32[]{:S(2)}, u32[]{:S(2)}) collective-permute-start(f32[16,128]{1,0:T(8,128)S(1)} %get-tuple-element.123), channel_id=1, source_target_pairs={{0,3},{1,2},{2,1},{3,0},{4,7},{5,6},{6,5},{7,4},{8,11},{9,10},{10,... | collective-permute-start | bytes 24584 | tf_op jit(solution)/shard_map/ppermute | solution.py:486
  70.8 1.1 %copy.44 = f32[6,16,16,256]{3,2,1,0:T(8,128)} copy(f32[6,16,16,256]{3,2,1,0:T(8,128)S(1)} %get-tuple-element.127) | data formatting | bytes 3145728
  72.8 1.1 %collective-permute-done.34 = f32[16,128]{1,0:T(8,128)S(1)} collective-permute-done((f32[16,128]{1,0:T(8,128)S(1)}, f32[16,128]{1,0:T(8,128)S(1)}, u32[]{:S(2)}, u32[]{:S(2)}) %collective-permute-start.34) | collective-permute-done | bytes 8224 | tf_op jit(solution)/shard_map/ppermute | solution.py:486
  (66 shorter events, 14.4 us)
Async XLA Ops:
  2.3 7.5 %collective-permute-start.2 = (f32[6,16,256]{2,1,0:T(8,128)S(1)}, f32[6,16,256]{2,1,0:T(8,128)S(1)}, u32[]{:S(2)}, u32[]{:S(2)}) collective-permute-start(f32[6,16,256]{2,1,0:T(8,128)S(1)} %get-tuple-element.71), channel_id=1, source_target_pairs={{0,1},{1,0},{2,3},{3,2},{4,5},{5,4},{6,7},{7,6},{8,9},{9,8},{10,11... | collective-permute-start | bytes 294920 | tf_op jit(solution)/shard_map/ppermute | solution.py:481
  5.3 4.4 %collective-permute-start.1 = (f32[5,16,256]{2,1,0:T(8,128)S(1)}, f32[5,16,256]{2,1,0:T(8,128)S(1)}, u32[]{:S(2)}, u32[]{:S(2)}) collective-permute-start(f32[5,16,256]{2,1,0:T(8,128)S(1)} %get-tuple-element.70), channel_id=1, source_target_pairs={{4,8},{8,4},{5,9},{9,5},{6,10},{10,6},{7,11},{11,7},{12,16},{16,12... | collective-permute-start | bytes 245768 | tf_op jit(solution)/shard_map/ppermute | solution.py:481
  10.0 6.2 %collective-permute-start.4 = (f32[7,16,256]{2,1,0:T(8,128)S(1)}, f32[7,16,256]{2,1,0:T(8,128)S(1)}, u32[]{:S(2)}, u32[]{:S(2)}) collective-permute-start(f32[7,16,256]{2,1,0:T(8,128)S(1)} %get-tuple-element.76), channel_id=1, source_target_pairs={{1,2},{2,1},{5,6},{6,5},{9,10},{10,9},{13,14},{14,13},{17,18},{18,... | collective-permute-start | bytes 344072 | tf_op jit(solution)/shard_map/ppermute | solution.py:481
  11.5 4.8 %collective-permute-start.5 = (f32[5,16,256]{2,1,0:T(8,128)S(1)}, f32[5,16,256]{2,1,0:T(8,128)S(1)}, u32[]{:S(2)}, u32[]{:S(2)}) collective-permute-start(f32[5,16,256]{2,1,0:T(8,128)S(1)} %get-tuple-element.81), channel_id=1, source_target_pairs={{0,4},{4,0},{1,5},{5,1},{2,6},{6,2},{3,7},{7,3},{8,12},{12,8},{9,1... | collective-permute-start | bytes 245768 | tf_op jit(solution)/shard_map/ppermute | solution.py:481
  11.5 6.6 %collective-permute-start.6 = (f32[5,16,256]{2,1,0:T(8,128)S(1)}, f32[5,16,256]{2,1,0:T(8,128)S(1)}, u32[]{:S(2)}, u32[]{:S(2)}) collective-permute-start(f32[5,16,256]{2,1,0:T(8,128)S(1)} %get-tuple-element.82), channel_id=1, source_target_pairs={{4,8},{8,4},{5,9},{9,5},{6,10},{10,6},{7,11},{11,7},{12,16},{16,12... | collective-permute-start | bytes 245768 | tf_op jit(solution)/shard_map/ppermute | solution.py:481
  14.5 5.4 %collective-permute-start.7 = (f32[5,16,256]{2,1,0:T(8,128)S(1)}, f32[5,16,256]{2,1,0:T(8,128)S(1)}, u32[]{:S(2)}, u32[]{:S(2)}) collective-permute-start(f32[5,16,256]{2,1,0:T(8,128)S(1)} %get-tuple-element.83), channel_id=1, source_target_pairs={{0,1},{1,0},{2,3},{3,2},{4,5},{5,4},{6,7},{7,6},{8,9},{9,8},{10,11... | collective-permute-start | bytes 245768 | tf_op jit(solution)/shard_map/ppermute | solution.py:481
  20.4 4.5 %collective-permute-start.9 = (f32[5,16,256]{2,1,0:T(8,128)S(1)}, f32[5,16,256]{2,1,0:T(8,128)S(1)}, u32[]{:S(2)}, u32[]{:S(2)}) collective-permute-start(f32[5,16,256]{2,1,0:T(8,128)S(1)} %get-tuple-element.86), channel_id=1, source_target_pairs={{4,8},{8,4},{5,9},{9,5},{6,10},{10,6},{7,11},{11,7},{12,16},{16,12... | collective-permute-start | bytes 245768 | tf_op jit(solution)/shard_map/ppermute | solution.py:481
  21.1 5.1 %collective-permute-start.10 = (f32[5,16,256]{2,1,0:T(8,128)S(1)}, f32[5,16,256]{2,1,0:T(8,128)S(1)}, u32[]{:S(2)}, u32[]{:S(2)}) collective-permute-start(f32[5,16,256]{2,1,0:T(8,128)S(1)} %get-tuple-element.87), channel_id=1, source_target_pairs={{0,1},{1,0},{2,3},{3,2},{4,5},{5,4},{6,7},{7,6},{8,9},{9,8},{10,11... | collective-permute-start | bytes 245768 | tf_op jit(solution)/shard_map/ppermute | solution.py:481
  22.1 4.1 %collective-permute-start.11 = (f32[5,16,256]{2,1,0:T(8,128)S(1)}, f32[5,16,256]{2,1,0:T(8,128)S(1)}, u32[]{:S(2)}, u32[]{:S(2)}) collective-permute-start(f32[5,16,256]{2,1,0:T(8,128)S(1)} %get-tuple-element.88), channel_id=1, source_target_pairs={{1,2},{2,1},{5,6},{6,5},{9,10},{10,9},{13,14},{14,13},{17,18},{18,... | collective-permute-start | bytes 245768 | tf_op jit(solution)/shard_map/ppermute | solution.py:481
  26.4 5.6 %collective-permute-start.12 = (f32[5,16,256]{2,1,0:T(8,128)S(1)}, f32[5,16,256]{2,1,0:T(8,128)S(1)}, u32[]{:S(2)}, u32[]{:S(2)}) collective-permute-start(f32[5,16,256]{2,1,0:T(8,128)S(1)} %get-tuple-element.91), channel_id=1, source_target_pairs={{0,4},{4,0},{1,5},{5,1},{2,6},{6,2},{3,7},{7,3},{8,12},{12,8},{9,1... | collective-permute-start | bytes 245768 | tf_op jit(solution)/shard_map/ppermute | solution.py:481
  26.7 5.4 %collective-permute-start.13 = (f32[5,16,256]{2,1,0:T(8,128)S(1)}, f32[5,16,256]{2,1,0:T(8,128)S(1)}, u32[]{:S(2)}, u32[]{:S(2)}) collective-permute-start(f32[5,16,256]{2,1,0:T(8,128)S(1)} %get-tuple-element.92), channel_id=1, source_target_pairs={{4,8},{8,4},{5,9},{9,5},{6,10},{10,6},{7,11},{11,7},{12,16},{16,12... | collective-permute-start | bytes 245768 | tf_op jit(solution)/shard_map/ppermute | solution.py:481
  29.8 5.3 %collective-permute-start.14 = (f32[5,16,256]{2,1,0:T(8,128)S(1)}, f32[5,16,256]{2,1,0:T(8,128)S(1)}, u32[]{:S(2)}, u32[]{:S(2)}) collective-permute-start(f32[5,16,256]{2,1,0:T(8,128)S(1)} %get-tuple-element.93), channel_id=1, source_target_pairs={{0,1},{1,0},{2,3},{3,2},{4,5},{5,4},{6,7},{7,6},{8,9},{9,8},{10,11... | collective-permute-start | bytes 245768 | tf_op jit(solution)/shard_map/ppermute | solution.py:481
  29.8 5.3 %collective-permute-start.15 = (f32[5,16,256]{2,1,0:T(8,128)S(1)}, f32[5,16,256]{2,1,0:T(8,128)S(1)}, u32[]{:S(2)}, u32[]{:S(2)}) collective-permute-start(f32[5,16,256]{2,1,0:T(8,128)S(1)} %get-tuple-element.94), channel_id=1, source_target_pairs={{1,2},{2,1},{5,6},{6,5},{9,10},{10,9},{13,14},{14,13},{17,18},{18,... | collective-permute-start | bytes 245768 | tf_op jit(solution)/shard_map/ppermute | solution.py:481
  35.5 4.1 %collective-permute-start.16 = (f32[5,16,256]{2,1,0:T(8,128)S(1)}, f32[5,16,256]{2,1,0:T(8,128)S(1)}, u32[]{:S(2)}, u32[]{:S(2)}) collective-permute-start(f32[5,16,256]{2,1,0:T(8,128)S(1)} %get-tuple-element.96), channel_id=1, source_target_pairs={{0,4},{4,0},{1,5},{5,1},{2,6},{6,2},{3,7},{7,3},{8,12},{12,8},{9,1... | collective-permute-start | bytes 245768 | tf_op jit(solution)/shard_map/ppermute | solution.py:481
  35.6 4.8 %collective-permute-start.17 = (f32[5,16,256]{2,1,0:T(8,128)S(1)}, f32[5,16,256]{2,1,0:T(8,128)S(1)}, u32[]{:S(2)}, u32[]{:S(2)}) collective-permute-start(f32[5,16,256]{2,1,0:T(8,128)S(1)} %get-tuple-element.97), channel_id=1, source_target_pairs={{4,8},{8,4},{5,9},{9,5},{6,10},{10,6},{7,11},{11,7},{12,16},{16,12... | collective-permute-start | bytes 245768 | tf_op jit(solution)/shard_map/ppermute | solution.py:481
  38.0 4.6 %collective-permute-start.18 = (f32[5,16,256]{2,1,0:T(8,128)S(1)}, f32[5,16,256]{2,1,0:T(8,128)S(1)}, u32[]{:S(2)}, u32[]{:S(2)}) collective-permute-start(f32[5,16,256]{2,1,0:T(8,128)S(1)} %get-tuple-element.98), channel_id=1, source_target_pairs={{0,1},{1,0},{2,3},{3,2},{4,5},{5,4},{6,7},{7,6},{8,9},{9,8},{10,11... | collective-permute-start | bytes 245768 | tf_op jit(solution)/shard_map/ppermute | solution.py:481
  38.0 4.6 %collective-permute-start.19 = (f32[5,16,256]{2,1,0:T(8,128)S(1)}, f32[5,16,256]{2,1,0:T(8,128)S(1)}, u32[]{:S(2)}, u32[]{:S(2)}) collective-permute-start(f32[5,16,256]{2,1,0:T(8,128)S(1)} %get-tuple-element.99), channel_id=1, source_target_pairs={{1,2},{2,1},{5,6},{6,5},{9,10},{10,9},{13,14},{14,13},{17,18},{18,... | collective-permute-start | bytes 245768 | tf_op jit(solution)/shard_map/ppermute | solution.py:481
  42.8 4.4 %collective-permute-start.20 = (f32[5,16,256]{2,1,0:T(8,128)S(1)}, f32[5,16,256]{2,1,0:T(8,128)S(1)}, u32[]{:S(2)}, u32[]{:S(2)}) collective-permute-start(f32[5,16,256]{2,1,0:T(8,128)S(1)} %get-tuple-element.102), channel_id=1, source_target_pairs={{0,4},{4,0},{1,5},{5,1},{2,6},{6,2},{3,7},{7,3},{8,12},{12,8},{9,1... | collective-permute-start | bytes 245768 | tf_op jit(solution)/shard_map/ppermute | solution.py:481
  42.8 5.1 %collective-permute-start.21 = (f32[5,16,256]{2,1,0:T(8,128)S(1)}, f32[5,16,256]{2,1,0:T(8,128)S(1)}, u32[]{:S(2)}, u32[]{:S(2)}) collective-permute-start(f32[5,16,256]{2,1,0:T(8,128)S(1)} %get-tuple-element.103), channel_id=1, source_target_pairs={{4,8},{8,4},{5,9},{9,5},{6,10},{10,6},{7,11},{11,7},{12,16},{16,12... | collective-permute-start | bytes 245768 | tf_op jit(solution)/shard_map/ppermute | solution.py:481
  45.6 4.8 %collective-permute-start.22 = (f32[5,16,256]{2,1,0:T(8,128)S(1)}, f32[5,16,256]{2,1,0:T(8,128)S(1)}, u32[]{:S(2)}, u32[]{:S(2)}) collective-permute-start(f32[5,16,256]{2,1,0:T(8,128)S(1)} %get-tuple-element.104), channel_id=1, source_target_pairs={{0,1},{1,0},{2,3},{3,2},{4,5},{5,4},{6,7},{7,6},{8,9},{9,8},{10,11... | collective-permute-start | bytes 245768 | tf_op jit(solution)/shard_map/ppermute | solution.py:481
  45.8 4.6 %collective-permute-start.23 = (f32[5,16,256]{2,1,0:T(8,128)S(1)}, f32[5,16,256]{2,1,0:T(8,128)S(1)}, u32[]{:S(2)}, u32[]{:S(2)}) collective-permute-start(f32[5,16,256]{2,1,0:T(8,128)S(1)} %get-tuple-element.105), channel_id=1, source_target_pairs={{1,2},{2,1},{5,6},{6,5},{9,10},{10,9},{13,14},{14,13},{17,18},{18,... | collective-permute-start | bytes 245768 | tf_op jit(solution)/shard_map/ppermute | solution.py:481
  50.8 3.9 %collective-permute-start.24 = (f32[5,16,256]{2,1,0:T(8,128)S(1)}, f32[5,16,256]{2,1,0:T(8,128)S(1)}, u32[]{:S(2)}, u32[]{:S(2)}) collective-permute-start(f32[5,16,256]{2,1,0:T(8,128)S(1)} %get-tuple-element.107), channel_id=1, source_target_pairs={{0,4},{4,0},{1,5},{5,1},{2,6},{6,2},{3,7},{7,3},{8,12},{12,8},{9,1... | collective-permute-start | bytes 245768 | tf_op jit(solution)/shard_map/ppermute | solution.py:481
  50.9 5.6 %collective-permute-start.25 = (f32[5,16,256]{2,1,0:T(8,128)S(1)}, f32[5,16,256]{2,1,0:T(8,128)S(1)}, u32[]{:S(2)}, u32[]{:S(2)}) collective-permute-start(f32[5,16,256]{2,1,0:T(8,128)S(1)} %get-tuple-element.108), channel_id=1, source_target_pairs={{4,8},{8,4},{5,9},{9,5},{6,10},{10,6},{7,11},{11,7},{12,16},{16,12... | collective-permute-start | bytes 245768 | tf_op jit(solution)/shard_map/ppermute | solution.py:481
  53.6 4.4 %collective-permute-start.26 = (f32[5,16,256]{2,1,0:T(8,128)S(1)}, f32[5,16,256]{2,1,0:T(8,128)S(1)}, u32[]{:S(2)}, u32[]{:S(2)}) collective-permute-start(f32[5,16,256]{2,1,0:T(8,128)S(1)} %get-tuple-element.109), channel_id=1, source_target_pairs={{0,1},{1,0},{2,3},{3,2},{4,5},{5,4},{6,7},{7,6},{8,9},{9,8},{10,11... | collective-permute-start | bytes 245768 | tf_op jit(solution)/shard_map/ppermute | solution.py:481
  53.6 4.4 %collective-permute-start.27 = (f32[5,16,256]{2,1,0:T(8,128)S(1)}, f32[5,16,256]{2,1,0:T(8,128)S(1)}, u32[]{:S(2)}, u32[]{:S(2)}) collective-permute-start(f32[5,16,256]{2,1,0:T(8,128)S(1)} %get-tuple-element.110), channel_id=1, source_target_pairs={{1,2},{2,1},{5,6},{6,5},{9,10},{10,9},{13,14},{14,13},{17,18},{18,... | collective-permute-start | bytes 245768 | tf_op jit(solution)/shard_map/ppermute | solution.py:481
  58.2 4.2 %collective-permute-start.28 = (f32[5,16,256]{2,1,0:T(8,128)S(1)}, f32[5,16,256]{2,1,0:T(8,128)S(1)}, u32[]{:S(2)}, u32[]{:S(2)}) collective-permute-start(f32[5,16,256]{2,1,0:T(8,128)S(1)} %get-tuple-element.115), channel_id=1, source_target_pairs={{0,4},{4,0},{1,5},{5,1},{2,6},{6,2},{3,7},{7,3},{8,12},{12,8},{9,1... | collective-permute-start | bytes 245768 | tf_op jit(solution)/shard_map/ppermute | solution.py:481
  58.3 5.7 %collective-permute-start.29 = (f32[5,16,256]{2,1,0:T(8,128)S(1)}, f32[5,16,256]{2,1,0:T(8,128)S(1)}, u32[]{:S(2)}, u32[]{:S(2)}) collective-permute-start(f32[5,16,256]{2,1,0:T(8,128)S(1)} %get-tuple-element.116), channel_id=1, source_target_pairs={{4,8},{8,4},{5,9},{9,5},{6,10},{10,6},{7,11},{11,7},{12,16},{16,12... | collective-permute-start | bytes 245768 | tf_op jit(solution)/shard_map/ppermute | solution.py:481
  61.2 4.4 %collective-permute-start.30 = (f32[5,16,256]{2,1,0:T(8,128)S(1)}, f32[5,16,256]{2,1,0:T(8,128)S(1)}, u32[]{:S(2)}, u32[]{:S(2)}) collective-permute-start(f32[5,16,256]{2,1,0:T(8,128)S(1)} %get-tuple-element.117), channel_id=1, source_target_pairs={{0,1},{1,0},{2,3},{3,2},{4,5},{5,4},{6,7},{7,6},{8,9},{9,8},{10,11... | collective-permute-start | bytes 245768 | tf_op jit(solution)/shard_map/ppermute | solution.py:481
  61.4 4.2 %collective-permute-start.31 = (f32[5,16,256]{2,1,0:T(8,128)S(1)}, f32[5,16,256]{2,1,0:T(8,128)S(1)}, u32[]{:S(2)}, u32[]{:S(2)}) collective-permute-start(f32[5,16,256]{2,1,0:T(8,128)S(1)} %get-tuple-element.118), channel_id=1, source_target_pairs={{1,2},{2,1},{5,6},{6,5},{9,10},{10,9},{13,14},{14,13},{17,18},{18,... | collective-permute-start | bytes 245768 | tf_op jit(solution)/shard_map/ppermute | solution.py:481
  66.2 5.7 %collective-permute-start.32 = (f32[16,128]{1,0:T(8,128)S(1)}, f32[16,128]{1,0:T(8,128)S(1)}, u32[]{:S(2)}, u32[]{:S(2)}) collective-permute-start(f32[16,128]{1,0:T(8,128)S(1)} %get-tuple-element.121), channel_id=1, source_target_pairs={{0,1},{1,0},{2,3},{3,2},{4,5},{5,4},{6,7},{7,6},{8,9},{9,8},{10,11... | collective-permute-start | bytes 24584 | tf_op jit(solution)/shard_map/ppermute | solution.py:486
  69.2 3.7 %collective-permute-start.33 = (f32[16,128]{1,0:T(8,128)S(1)}, f32[16,128]{1,0:T(8,128)S(1)}, u32[]{:S(2)}, u32[]{:S(2)}) collective-permute-start(f32[16,128]{1,0:T(8,128)S(1)} %get-tuple-element.122), channel_id=1, source_target_pairs={{0,2},{1,3},{2,0},{3,1},{4,6},{5,7},{6,4},{7,5},{8,10},{9,11},{10,... | collective-permute-start | bytes 24584 | tf_op jit(solution)/shard_map/ppermute | solution.py:486
  69.4 4.5 %collective-permute-start.34 = (f32[16,128]{1,0:T(8,128)S(1)}, f32[16,128]{1,0:T(8,128)S(1)}, u32[]{:S(2)}, u32[]{:S(2)}) collective-permute-start(f32[16,128]{1,0:T(8,128)S(1)} %get-tuple-element.123), channel_id=1, source_target_pairs={{0,3},{1,2},{2,1},{3,0},{4,7},{5,6},{6,5},{7,4},{8,11},{9,10},{10,... | collective-permute-start | bytes 24584 | tf_op jit(solution)/shard_map/ppermute | solution.py:486
  (6 other events, 32.1 us)

commit v4 on v3

--- a/solution.py
+++ b/solution.py
@@ -407,18 +407,31 @@
 
 def pack_body(s_ref, *rest):
     *sources, s_out, xa, xb, ya, yb, own_ref, part_ref, s_sem, part_sem = rest
-    copies = [pltpu.make_async_copy(ref, part_ref.at[k], part_sem.at[k]) for k, ref in enumerate(sources)]
-    copies += [pltpu.make_async_copy(s_ref.at[c], s_out.at[c], s_sem.at[c]) for c in range(s_ref.shape[0])]
-    for copy in copies:
+    parts = [pltpu.make_async_copy(ref, part_ref.at[k], part_sem.at[k]) for k, ref in enumerate(sources)]
+    loads = [pltpu.make_async_copy(s_ref.at[c], s_out.at[c], s_sem.at[c]) for c in range(s_ref.shape[0])]
+    across, along = ([comp for comp, _ in STRESS_FACE[axis]] for axis in (1, 0))
+    along = [comp for comp in along if comp not in across]
+    others = [comp for comp in range(len(loads)) if comp not in across + along]
+    for comp in across + along:
+        loads[comp].start()
+    for copy in parts:
         copy.start()
-    for copy in copies:
+    for comp in others:
+        loads[comp].start()
+    for comp in across:
+        loads[comp].wait()
+    pack(s_out, 1, STRESS_FACE[1], ya, yb)
+    for comp in along:
+        loads[comp].wait()
+    pack(s_out, 0, STRESS_FACE[0], xa, xb)
+    for copy in parts:
         copy.wait()
     own = join([part_ref[k] for k in range(len(sources))], own_ref.shape[1])
     own_ref[...] = own
-    for axis, a_ref, b_ref in ((0, xa, xb), (1, ya, yb)):
-        pack(s_out, axis, STRESS_FACE[axis], a_ref, b_ref)
     if ya.shape[0] > yb.shape[0]:
         ya[ya.shape[0] - 1] = own
+    for comp in others:
+        loads[comp].wait()
 
 
 def swaps(pairs):
@@ -504,7 +517,7 @@
                 velocity_load_body, (*sources, stress, buoyancy),
                 (like_v, plane, vec(4, nx, nz)), [HBM, HBM, VMEM, VMEM],
                 scratch=[
-                    pltpu.VMEM(velocity.shape, f32), dma((4,)), pltpu.SMEM(fault_tile.shape, jnp.int32), dma
+                    pltpu.VMEM(velocity.shape, f32), dma((8,)), pltpu.SMEM(fault_tile.shape, jnp.int32), dma
                 ],
             )
         else:

time: 74.8 us -> 74.7 us (level)
  no operation moved by 1% of the time
where the time goes in v4:
time: 74.7 us; the launch traced here: 74.5 us
  starting transfers between devices  34.2 us (46%)
  waiting for transfers between devices  25.1 us (34%)
  Pallas kernels  12.4 us (17%)
  local copies, waits for them, and re-layouts  1.83 us (2%)
  between operations  0.9 us (1%)
    ppermute x32, starting transfers between devices, exchange(): halos[name] = lax.ppermute(block, axes, perms[name])  29.6 us
    ppermute x32, waiting for transfers between devices, exchange(): halos[name] = lax.ppermute(block, axes, perms[name])  23.1 us
    pallas_call x19, Pallas kernels, call(): pl.pallas_call(body, in_specs=[VMEM] * len(ins) if specs is None else spe...  12.4 us
    ppermute x3, starting transfers between devices, partner(): return lax.ppermute(block, axes, pairs)  4.57 us
    ppermute x3, waiting for transfers between devices, partner(): return lax.ppermute(block, axes, pairs)  2.02 us
  transfers between devices with their start and end apart: 35, of which 17 were waited for; matrix products, arithmetic and copies ran while one was open for 2% of the time, Pallas kernels for 11%

profile of v4, /device:TPU:0, one launch (start us, length us, event | category | flops | bytes accessed | tf_op | source)
XLA Modules:
  0.0 74.5 jit_solution(12355268122743656141)
XLA Ops:
  0.6 1.5 %shard_map.129 = (f32[6,16,16,256]{3,2,1,0:T(8,128)S(1)}, f32[5,16,256]{2,1,0:T(8,128)S(1)}, f32[5,16,256]{2,1,0:T(8,128)S(1)}, f32[6,16,256]{2,1,0:T(8,128)S(1)...) custom-call(f32[6,16,16,256]{3,2,1,0:T(8,128)} %s_ref.1, f32[16,64]{1,0:T(8,128)} %rest_0_.1, f32[16,64]{1,0:T(8,128)} %rest_1_.1, ...), custom_call_target="tpu_custom_call" | custom-call | tf_op jit(solution)/shard_map/pallas_call | solution.py:480
  2.2 3.0 %collective-permute-start.2 = (f32[6,16,256]{2,1,0:T(8,128)S(1)}, f32[6,16,256]{2,1,0:T(8,128)S(1)}, u32[]{:S(2)}, u32[]{:S(2)}) collective-permute-start(f32[6,16,256]{2,1,0:T(8,128)S(1)} %get-tuple-element.71), channel_id=1, source_target_pairs={{0,1},{1,0},{2,3},{3,2},{4,5},{5,4},{6,7},{7,6},{8,9},{9,8},{10,11... | collective-permute-start | bytes 294920 | tf_op jit(solution)/shard_map/ppermute | solution.py:494
  5.2 1.5 %collective-permute-start.1 = (f32[5,16,256]{2,1,0:T(8,128)S(1)}, f32[5,16,256]{2,1,0:T(8,128)S(1)}, u32[]{:S(2)}, u32[]{:S(2)}) collective-permute-start(f32[5,16,256]{2,1,0:T(8,128)S(1)} %get-tuple-element.70), channel_id=1, source_target_pairs={{4,8},{8,4},{5,9},{9,5},{6,10},{10,6},{7,11},{11,7},{12,16},{16,12... | collective-permute-start | bytes 245768 | tf_op jit(solution)/shard_map/ppermute | solution.py:494
  6.9 1.9 %shard_map.130 = (f32[3,16,16,256]{3,2,1,0:T(8,128)S(1)}, f32[16,256]{1,0:T(8,128)S(1)}, f32[4,16,256]{2,1,0:T(8,128)S(1)}) custom-call(s32[8]{0:T(128)} %tile_ref.1, f32[3,16,16,256]{3,2,1,0:T(8,128)} %v_ref.1, f32[6,16,16,256]{3,2,1,0:T(8,128)S(1)} %get-tuple-element.64.s_ref, f32[16,16,256]{2,1,0:T(8,128)S(1)} %copy-done.2), custom_call_target="tpu_custom_call" | custom-call | tf_op jit(solution)/shard_map/pallas_call | solution.py:480
  9.9 1.6 %collective-permute-start.4 = (f32[7,16,256]{2,1,0:T(8,128)S(1)}, f32[7,16,256]{2,1,0:T(8,128)S(1)}, u32[]{:S(2)}, u32[]{:S(2)}) collective-permute-start(f32[7,16,256]{2,1,0:T(8,128)S(1)} %get-tuple-element.76), channel_id=1, source_target_pairs={{1,2},{2,1},{5,6},{6,5},{9,10},{10,9},{13,14},{14,13},{17,18},{18,... | collective-permute-start | bytes 344072 | tf_op jit(solution)/shard_map/ppermute | solution.py:494
  11.4 3.0 %collective-permute-start.6 = (f32[5,16,256]{2,1,0:T(8,128)S(1)}, f32[5,16,256]{2,1,0:T(8,128)S(1)}, u32[]{:S(2)}, u32[]{:S(2)}) collective-permute-start(f32[5,16,256]{2,1,0:T(8,128)S(1)} %get-tuple-element.82), channel_id=1, source_target_pairs={{4,8},{8,4},{5,9},{9,5},{6,10},{10,6},{7,11},{11,7},{12,16},{16,12... | collective-permute-start | bytes 245768 | tf_op jit(solution)/shard_map/ppermute | solution.py:494
  15.1 1.0 %shard_map.132.s_ref = f32[6,16,16,256]{3,2,1,0:T(8,128)S(1)} custom-call(f32[6,16,16,256]{3,2,1,0:T(8,128)S(1)} %get-tuple-element.64.s_ref, f32[3,16,16,256]{3,2,1,0:T(8,128)S(1)} %get-tuple-element.73.v_ref, f32[16,16,256]{2,1,0:T(8,128)S(1)} %copy-done, f32[16,16,256]{2,1,0:T(8,128)S(1)} %copy-done.1), custom_call_target="tpu_custom_call", output_to_operand_aliasing={{}: (0, {})} | custom-call | tf_op jit(solution)/shard_map/pallas_call | solution.py:480
  16.2 1.8 %collective-permute-done.6.xb = f32[5,16,256]{2,1,0:T(8,128)S(1)} collective-permute-done((f32[5,16,256]{2,1,0:T(8,128)S(1)}, f32[5,16,256]{2,1,0:T(8,128)S(1)}, u32[]{:S(2)}, u32[]{:S(2)}) %collective-permute-start.6) | collective-permute-done | bytes 81952 | tf_op jit(solution)/shard_map/ppermute | solution.py:494
  18.0 1.9 %collective-permute-done.7.ya = f32[5,16,256]{2,1,0:T(8,128)S(1)} collective-permute-done((f32[5,16,256]{2,1,0:T(8,128)S(1)}, f32[5,16,256]{2,1,0:T(8,128)S(1)}, u32[]{:S(2)}, u32[]{:S(2)}) %collective-permute-start.7) | collective-permute-done | bytes 81952 | tf_op jit(solution)/shard_map/ppermute | solution.py:494
  21.0 1.0 %collective-permute-start.10 = (f32[5,16,256]{2,1,0:T(8,128)S(1)}, f32[5,16,256]{2,1,0:T(8,128)S(1)}, u32[]{:S(2)}, u32[]{:S(2)}) collective-permute-start(f32[5,16,256]{2,1,0:T(8,128)S(1)} %get-tuple-element.87), channel_id=1, source_target_pairs={{0,1},{1,0},{2,3},{3,2},{4,5},{5,4},{6,7},{7,6},{8,9},{9,8},{10,11... | collective-permute-start | bytes 245768 | tf_op jit(solution)/shard_map/ppermute | solution.py:494
  23.4 1.5 %collective-permute-done.9.xb = f32[5,16,256]{2,1,0:T(8,128)S(1)} collective-permute-done((f32[5,16,256]{2,1,0:T(8,128)S(1)}, f32[5,16,256]{2,1,0:T(8,128)S(1)}, u32[]{:S(2)}, u32[]{:S(2)}) %collective-permute-start.9) | collective-permute-done | bytes 81952 | tf_op jit(solution)/shard_map/ppermute | solution.py:494
  24.9 1.2 %collective-permute-done.10.ya = f32[5,16,256]{2,1,0:T(8,128)S(1)} collective-permute-done((f32[5,16,256]{2,1,0:T(8,128)S(1)}, f32[5,16,256]{2,1,0:T(8,128)S(1)}, u32[]{:S(2)}, u32[]{:S(2)}) %collective-permute-start.10) | collective-permute-done | bytes 81952 | tf_op jit(solution)/shard_map/ppermute | solution.py:494
  26.7 3.0 %collective-permute-start.13 = (f32[5,16,256]{2,1,0:T(8,128)S(1)}, f32[5,16,256]{2,1,0:T(8,128)S(1)}, u32[]{:S(2)}, u32[]{:S(2)}) collective-permute-start(f32[5,16,256]{2,1,0:T(8,128)S(1)} %get-tuple-element.92), channel_id=1, source_target_pairs={{4,8},{8,4},{5,9},{9,5},{6,10},{10,6},{7,11},{11,7},{12,16},{16,12... | collective-permute-start | bytes 245768 | tf_op jit(solution)/shard_map/ppermute | solution.py:494
  29.7 1.2 %collective-permute-start.15 = (f32[5,16,256]{2,1,0:T(8,128)S(1)}, f32[5,16,256]{2,1,0:T(8,128)S(1)}, u32[]{:S(2)}, u32[]{:S(2)}) collective-permute-start(f32[5,16,256]{2,1,0:T(8,128)S(1)} %get-tuple-element.94), channel_id=1, source_target_pairs={{1,2},{2,1},{5,6},{6,5},{9,10},{10,9},{13,14},{14,13},{17,18},{18,... | collective-permute-start | bytes 245768 | tf_op jit(solution)/shard_map/ppermute | solution.py:494
  30.9 1.0 %shard_map.138.s_ref = f32[6,16,16,256]{3,2,1,0:T(8,128)S(1)} custom-call(f32[6,16,16,256]{3,2,1,0:T(8,128)S(1)} %get-tuple-element.84.s_ref, f32[3,16,16,256]{3,2,1,0:T(8,128)S(1)} %get-tuple-element.89.v_ref, f32[16,16,256]{2,1,0:T(8,128)S(1)} %copy-done, f32[16,16,256]{2,1,0:T(8,128)S(1)} %copy-done.1), custom_call_target="tpu_custom_call", output_to_operand_aliasing={{}: (0, {})} | custom-call | tf_op jit(solution)/shard_map/pallas_call | solution.py:480
  32.1 2.9 %collective-permute-done.14.ya = f32[5,16,256]{2,1,0:T(8,128)S(1)} collective-permute-done((f32[5,16,256]{2,1,0:T(8,128)S(1)}, f32[5,16,256]{2,1,0:T(8,128)S(1)}, u32[]{:S(2)}, u32[]{:S(2)}) %collective-permute-start.14) | collective-permute-done | bytes 81952 | tf_op jit(solution)/shard_map/ppermute | solution.py:494
  35.5 2.4 %collective-permute-start.17 = (f32[5,16,256]{2,1,0:T(8,128)S(1)}, f32[5,16,256]{2,1,0:T(8,128)S(1)}, u32[]{:S(2)}, u32[]{:S(2)}) collective-permute-start(f32[5,16,256]{2,1,0:T(8,128)S(1)} %get-tuple-element.97), channel_id=1, source_target_pairs={{4,8},{8,4},{5,9},{9,5},{6,10},{10,6},{7,11},{11,7},{12,16},{16,12... | collective-permute-start | bytes 245768 | tf_op jit(solution)/shard_map/ppermute | solution.py:494
  40.3 2.2 %collective-permute-done.18.ya = f32[5,16,256]{2,1,0:T(8,128)S(1)} collective-permute-done((f32[5,16,256]{2,1,0:T(8,128)S(1)}, f32[5,16,256]{2,1,0:T(8,128)S(1)}, u32[]{:S(2)}, u32[]{:S(2)}) %collective-permute-start.18) | collective-permute-done | bytes 81952 | tf_op jit(solution)/shard_map/ppermute | solution.py:494
  42.8 2.7 %collective-permute-start.21 = (f32[5,16,256]{2,1,0:T(8,128)S(1)}, f32[5,16,256]{2,1,0:T(8,128)S(1)}, u32[]{:S(2)}, u32[]{:S(2)}) collective-permute-start(f32[5,16,256]{2,1,0:T(8,128)S(1)} %get-tuple-element.103), channel_id=1, source_target_pairs={{4,8},{8,4},{5,9},{9,5},{6,10},{10,6},{7,11},{11,7},{12,16},{16,12... | collective-permute-start | bytes 245768 | tf_op jit(solution)/shard_map/ppermute | solution.py:494
  46.1 1.0 %shard_map.142.s_ref = f32[6,16,16,256]{3,2,1,0:T(8,128)S(1)} custom-call(f32[6,16,16,256]{3,2,1,0:T(8,128)S(1)} %get-tuple-element.95.s_ref, f32[3,16,16,256]{3,2,1,0:T(8,128)S(1)} %get-tuple-element.100.v_ref, f32[16,16,256]{2,1,0:T(8,128)S(1)} %copy-done, f32[16,16,256]{2,1,0:T(8,128)S(1)} %copy-done.1), custom_call_target="tpu_custom_call", output_to_operand_aliasing={{}: (0, {})} | custom-call | tf_op jit(solution)/shard_map/pallas_call | solution.py:480
  47.9 2.4 %collective-permute-done.22.ya = f32[5,16,256]{2,1,0:T(8,128)S(1)} collective-permute-done((f32[5,16,256]{2,1,0:T(8,128)S(1)}, f32[5,16,256]{2,1,0:T(8,128)S(1)}, u32[]{:S(2)}, u32[]{:S(2)}) %collective-permute-start.22) | collective-permute-done | bytes 81952 | tf_op jit(solution)/shard_map/ppermute | solution.py:494
  50.8 2.7 %collective-permute-start.25 = (f32[5,16,256]{2,1,0:T(8,128)S(1)}, f32[5,16,256]{2,1,0:T(8,128)S(1)}, u32[]{:S(2)}, u32[]{:S(2)}) collective-permute-start(f32[5,16,256]{2,1,0:T(8,128)S(1)} %get-tuple-element.108), channel_id=1, source_target_pairs={{4,8},{8,4},{5,9},{9,5},{6,10},{10,6},{7,11},{11,7},{12,16},{16,12... | collective-permute-start | bytes 245768 | tf_op jit(solution)/shard_map/ppermute | solution.py:494
  54.6 1.8 %collective-permute-done.25.xb = f32[5,16,256]{2,1,0:T(8,128)S(1)} collective-permute-done((f32[5,16,256]{2,1,0:T(8,128)S(1)}, f32[5,16,256]{2,1,0:T(8,128)S(1)}, u32[]{:S(2)}, u32[]{:S(2)}) %collective-permute-start.25) | collective-permute-done | bytes 81952 | tf_op jit(solution)/shard_map/ppermute | solution.py:494
  56.4 1.6 %collective-permute-done.26.ya = f32[5,16,256]{2,1,0:T(8,128)S(1)} collective-permute-done((f32[5,16,256]{2,1,0:T(8,128)S(1)}, f32[5,16,256]{2,1,0:T(8,128)S(1)}, u32[]{:S(2)}, u32[]{:S(2)}) %collective-permute-start.26) | collective-permute-done | bytes 81952 | tf_op jit(solution)/shard_map/ppermute | solution.py:494
  58.2 2.9 %collective-permute-start.29 = (f32[5,16,256]{2,1,0:T(8,128)S(1)}, f32[5,16,256]{2,1,0:T(8,128)S(1)}, u32[]{:S(2)}, u32[]{:S(2)}) collective-permute-start(f32[5,16,256]{2,1,0:T(8,128)S(1)} %get-tuple-element.116), channel_id=1, source_target_pairs={{4,8},{8,4},{5,9},{9,5},{6,10},{10,6},{7,11},{11,7},{12,16},{16,12... | collective-permute-start | bytes 245768 | tf_op jit(solution)/shard_map/ppermute | solution.py:494
  61.4 1.0 %shard_map.146 = (f32[6,16,16,256]{3,2,1,0:T(8,128)S(1)}, f32[3,16,16,256]{3,2,1,0:T(8,128)}) custom-call(f32[6,16,16,256]{3,2,1,0:T(8,128)S(1)} %get-tuple-element.106.s_ref, f32[3,16,16,256]{3,2,1,0:T(8,128)S(1)} %get-tuple-element.111.v_ref, f32[16,16,256]{2,1,0:T(8,128)S(1)} %copy-done, f32[16,16,256]{2,1,0:T(8,128)S(1)} %copy-done.1), custom_call_target="tpu_custom_call", output_to_operand_aliasing={{0}: (0, {})} | custom-call | tf_op jit(solution)/shard_map/pallas_call | solution.py:480
  62.4 1.6 %collective-permute-done.29.xb = f32[5,16,256]{2,1,0:T(8,128)S(1)} collective-permute-done((f32[5,16,256]{2,1,0:T(8,128)S(1)}, f32[5,16,256]{2,1,0:T(8,128)S(1)}, u32[]{:S(2)}, u32[]{:S(2)}) %collective-permute-start.29) | collective-permute-done | bytes 81952 | tf_op jit(solution)/shard_map/ppermute | solution.py:494
  64.0 1.6 %collective-permute-done.30.ya = f32[5,16,256]{2,1,0:T(8,128)S(1)} collective-permute-done((f32[5,16,256]{2,1,0:T(8,128)S(1)}, f32[5,16,256]{2,1,0:T(8,128)S(1)}, u32[]{:S(2)}, u32[]{:S(2)}) %collective-permute-start.30) | collective-permute-done | bytes 81952 | tf_op jit(solution)/shard_map/ppermute | solution.py:494
  66.1 3.0 %collective-permute-start.32 = (f32[16,128]{1,0:T(8,128)S(1)}, f32[16,128]{1,0:T(8,128)S(1)}, u32[]{:S(2)}, u32[]{:S(2)}) collective-permute-start(f32[16,128]{1,0:T(8,128)S(1)} %get-tuple-element.121), channel_id=1, source_target_pairs={{0,1},{1,0},{2,3},{3,2},{4,5},{5,4},{6,7},{7,6},{8,9},{9,8},{10,11... | collective-permute-start | bytes 24584 | tf_op jit(solution)/shard_map/ppermute | solution.py:499
  69.3 1.4 %collective-permute-start.34 = (f32[16,128]{1,0:T(8,128)S(1)}, f32[16,128]{1,0:T(8,128)S(1)}, u32[]{:S(2)}, u32[]{:S(2)}) collective-permute-start(f32[16,128]{1,0:T(8,128)S(1)} %get-tuple-element.123), channel_id=1, source_target_pairs={{0,3},{1,2},{2,1},{3,0},{4,7},{5,6},{6,5},{7,4},{8,11},{9,10},{10,... | collective-permute-start | bytes 24584 | tf_op jit(solution)/shard_map/ppermute | solution.py:499
  70.7 1.1 %copy.44 = f32[6,16,16,256]{3,2,1,0:T(8,128)} copy(f32[6,16,16,256]{3,2,1,0:T(8,128)S(1)} %get-tuple-element.127) | data formatting | bytes 3145728
  72.7 1.1 %collective-permute-done.34 = f32[16,128]{1,0:T(8,128)S(1)} collective-permute-done((f32[16,128]{1,0:T(8,128)S(1)}, f32[16,128]{1,0:T(8,128)S(1)}, u32[]{:S(2)}, u32[]{:S(2)}) %collective-permute-start.34) | collective-permute-done | bytes 8224 | tf_op jit(solution)/shard_map/ppermute | solution.py:499
  (66 shorter events, 14.3 us)
Async XLA Ops:
  2.2 7.5 %collective-permute-start.2 = (f32[6,16,256]{2,1,0:T(8,128)S(1)}, f32[6,16,256]{2,1,0:T(8,128)S(1)}, u32[]{:S(2)}, u32[]{:S(2)}) collective-permute-start(f32[6,16,256]{2,1,0:T(8,128)S(1)} %get-tuple-element.71), channel_id=1, source_target_pairs={{0,1},{1,0},{2,3},{3,2},{4,5},{5,4},{6,7},{7,6},{8,9},{9,8},{10,11... | collective-permute-start | bytes 294920 | tf_op jit(solution)/shard_map/ppermute | solution.py:494
  5.2 4.4 %collective-permute-start.1 = (f32[5,16,256]{2,1,0:T(8,128)S(1)}, f32[5,16,256]{2,1,0:T(8,128)S(1)}, u32[]{:S(2)}, u32[]{:S(2)}) collective-permute-start(f32[5,16,256]{2,1,0:T(8,128)S(1)} %get-tuple-element.70), channel_id=1, source_target_pairs={{4,8},{8,4},{5,9},{9,5},{6,10},{10,6},{7,11},{11,7},{12,16},{16,12... | collective-permute-start | bytes 245768 | tf_op jit(solution)/shard_map/ppermute | solution.py:494
  9.9 6.2 %collective-permute-start.4 = (f32[7,16,256]{2,1,0:T(8,128)S(1)}, f32[7,16,256]{2,1,0:T(8,128)S(1)}, u32[]{:S(2)}, u32[]{:S(2)}) collective-permute-start(f32[7,16,256]{2,1,0:T(8,128)S(1)} %get-tuple-element.76), channel_id=1, source_target_pairs={{1,2},{2,1},{5,6},{6,5},{9,10},{10,9},{13,14},{14,13},{17,18},{18,... | collective-permute-start | bytes 344072 | tf_op jit(solution)/shard_map/ppermute | solution.py:494
  11.4 4.8 %collective-permute-start.5 = (f32[5,16,256]{2,1,0:T(8,128)S(1)}, f32[5,16,256]{2,1,0:T(8,128)S(1)}, u32[]{:S(2)}, u32[]{:S(2)}) collective-permute-start(f32[5,16,256]{2,1,0:T(8,128)S(1)} %get-tuple-element.81), channel_id=1, source_target_pairs={{0,4},{4,0},{1,5},{5,1},{2,6},{6,2},{3,7},{7,3},{8,12},{12,8},{9,1... | collective-permute-start | bytes 245768 | tf_op jit(solution)/shard_map/ppermute | solution.py:494
  11.4 6.6 %collective-permute-start.6 = (f32[5,16,256]{2,1,0:T(8,128)S(1)}, f32[5,16,256]{2,1,0:T(8,128)S(1)}, u32[]{:S(2)}, u32[]{:S(2)}) collective-permute-start(f32[5,16,256]{2,1,0:T(8,128)S(1)} %get-tuple-element.82), channel_id=1, source_target_pairs={{4,8},{8,4},{5,9},{9,5},{6,10},{10,6},{7,11},{11,7},{12,16},{16,12... | collective-permute-start | bytes 245768 | tf_op jit(solution)/shard_map/ppermute | solution.py:494
  14.4 5.4 %collective-permute-start.7 = (f32[5,16,256]{2,1,0:T(8,128)S(1)}, f32[5,16,256]{2,1,0:T(8,128)S(1)}, u32[]{:S(2)}, u32[]{:S(2)}) collective-permute-start(f32[5,16,256]{2,1,0:T(8,128)S(1)} %get-tuple-element.83), channel_id=1, source_target_pairs={{0,1},{1,0},{2,3},{3,2},{4,5},{5,4},{6,7},{7,6},{8,9},{9,8},{10,11... | collective-permute-start | bytes 245768 | tf_op jit(solution)/shard_map/ppermute | solution.py:494
  20.4 4.5 %collective-permute-start.9 = (f32[5,16,256]{2,1,0:T(8,128)S(1)}, f32[5,16,256]{2,1,0:T(8,128)S(1)}, u32[]{:S(2)}, u32[]{:S(2)}) collective-permute-start(f32[5,16,256]{2,1,0:T(8,128)S(1)} %get-tuple-element.86), channel_id=1, source_target_pairs={{4,8},{8,4},{5,9},{9,5},{6,10},{10,6},{7,11},{11,7},{12,16},{16,12... | collective-permute-start | bytes 245768 | tf_op jit(solution)/shard_map/ppermute | solution.py:494
  21.0 5.1 %collective-permute-start.10 = (f32[5,16,256]{2,1,0:T(8,128)S(1)}, f32[5,16,256]{2,1,0:T(8,128)S(1)}, u32[]{:S(2)}, u32[]{:S(2)}) collective-permute-start(f32[5,16,256]{2,1,0:T(8,128)S(1)} %get-tuple-element.87), channel_id=1, source_target_pairs={{0,1},{1,0},{2,3},{3,2},{4,5},{5,4},{6,7},{7,6},{8,9},{9,8},{10,11... | collective-permute-start | bytes 245768 | tf_op jit(solution)/shard_map/ppermute | solution.py:494
  22.0 4.1 %collective-permute-start.11 = (f32[5,16,256]{2,1,0:T(8,128)S(1)}, f32[5,16,256]{2,1,0:T(8,128)S(1)}, u32[]{:S(2)}, u32[]{:S(2)}) collective-permute-start(f32[5,16,256]{2,1,0:T(8,128)S(1)} %get-tuple-element.88), channel_id=1, source_target_pairs={{1,2},{2,1},{5,6},{6,5},{9,10},{10,9},{13,14},{14,13},{17,18},{18,... | collective-permute-start | bytes 245768 | tf_op jit(solution)/shard_map/ppermute | solution.py:494
  26.3 5.6 %collective-permute-start.12 = (f32[5,16,256]{2,1,0:T(8,128)S(1)}, f32[5,16,256]{2,1,0:T(8,128)S(1)}, u32[]{:S(2)}, u32[]{:S(2)}) collective-permute-start(f32[5,16,256]{2,1,0:T(8,128)S(1)} %get-tuple-element.91), channel_id=1, source_target_pairs={{0,4},{4,0},{1,5},{5,1},{2,6},{6,2},{3,7},{7,3},{8,12},{12,8},{9,1... | collective-permute-start | bytes 245768 | tf_op jit(solution)/shard_map/ppermute | solution.py:494
  26.7 5.4 %collective-permute-start.13 = (f32[5,16,256]{2,1,0:T(8,128)S(1)}, f32[5,16,256]{2,1,0:T(8,128)S(1)}, u32[]{:S(2)}, u32[]{:S(2)}) collective-permute-start(f32[5,16,256]{2,1,0:T(8,128)S(1)} %get-tuple-element.92), channel_id=1, source_target_pairs={{4,8},{8,4},{5,9},{9,5},{6,10},{10,6},{7,11},{11,7},{12,16},{16,12... | collective-permute-start | bytes 245768 | tf_op jit(solution)/shard_map/ppermute | solution.py:494
  29.7 5.3 %collective-permute-start.14 = (f32[5,16,256]{2,1,0:T(8,128)S(1)}, f32[5,16,256]{2,1,0:T(8,128)S(1)}, u32[]{:S(2)}, u32[]{:S(2)}) collective-permute-start(f32[5,16,256]{2,1,0:T(8,128)S(1)} %get-tuple-element.93), channel_id=1, source_target_pairs={{0,1},{1,0},{2,3},{3,2},{4,5},{5,4},{6,7},{7,6},{8,9},{9,8},{10,11... | collective-permute-start | bytes 245768 | tf_op jit(solution)/shard_map/ppermute | solution.py:494
  29.7 5.3 %collective-permute-start.15 = (f32[5,16,256]{2,1,0:T(8,128)S(1)}, f32[5,16,256]{2,1,0:T(8,128)S(1)}, u32[]{:S(2)}, u32[]{:S(2)}) collective-permute-start(f32[5,16,256]{2,1,0:T(8,128)S(1)} %get-tuple-element.94), channel_id=1, source_target_pairs={{1,2},{2,1},{5,6},{6,5},{9,10},{10,9},{13,14},{14,13},{17,18},{18,... | collective-permute-start | bytes 245768 | tf_op jit(solution)/shard_map/ppermute | solution.py:494
  35.4 4.1 %collective-permute-start.16 = (f32[5,16,256]{2,1,0:T(8,128)S(1)}, f32[5,16,256]{2,1,0:T(8,128)S(1)}, u32[]{:S(2)}, u32[]{:S(2)}) collective-permute-start(f32[5,16,256]{2,1,0:T(8,128)S(1)} %get-tuple-element.96), channel_id=1, source_target_pairs={{0,4},{4,0},{1,5},{5,1},{2,6},{6,2},{3,7},{7,3},{8,12},{12,8},{9,1... | collective-permute-start | bytes 245768 | tf_op jit(solution)/shard_map/ppermute | solution.py:494
  35.5 4.8 %collective-permute-start.17 = (f32[5,16,256]{2,1,0:T(8,128)S(1)}, f32[5,16,256]{2,1,0:T(8,128)S(1)}, u32[]{:S(2)}, u32[]{:S(2)}) collective-permute-start(f32[5,16,256]{2,1,0:T(8,128)S(1)} %get-tuple-element.97), channel_id=1, source_target_pairs={{4,8},{8,4},{5,9},{9,5},{6,10},{10,6},{7,11},{11,7},{12,16},{16,12... | collective-permute-start | bytes 245768 | tf_op jit(solution)/shard_map/ppermute | solution.py:494
  37.9 4.6 %collective-permute-start.18 = (f32[5,16,256]{2,1,0:T(8,128)S(1)}, f32[5,16,256]{2,1,0:T(8,128)S(1)}, u32[]{:S(2)}, u32[]{:S(2)}) collective-permute-start(f32[5,16,256]{2,1,0:T(8,128)S(1)} %get-tuple-element.98), channel_id=1, source_target_pairs={{0,1},{1,0},{2,3},{3,2},{4,5},{5,4},{6,7},{7,6},{8,9},{9,8},{10,11... | collective-permute-start | bytes 245768 | tf_op jit(solution)/shard_map/ppermute | solution.py:494
  37.9 4.6 %collective-permute-start.19 = (f32[5,16,256]{2,1,0:T(8,128)S(1)}, f32[5,16,256]{2,1,0:T(8,128)S(1)}, u32[]{:S(2)}, u32[]{:S(2)}) collective-permute-start(f32[5,16,256]{2,1,0:T(8,128)S(1)} %get-tuple-element.99), channel_id=1, source_target_pairs={{1,2},{2,1},{5,6},{6,5},{9,10},{10,9},{13,14},{14,13},{17,18},{18,... | collective-permute-start | bytes 245768 | tf_op jit(solution)/shard_map/ppermute | solution.py:494
  42.7 4.4 %collective-permute-start.20 = (f32[5,16,256]{2,1,0:T(8,128)S(1)}, f32[5,16,256]{2,1,0:T(8,128)S(1)}, u32[]{:S(2)}, u32[]{:S(2)}) collective-permute-start(f32[5,16,256]{2,1,0:T(8,128)S(1)} %get-tuple-element.102), channel_id=1, source_target_pairs={{0,4},{4,0},{1,5},{5,1},{2,6},{6,2},{3,7},{7,3},{8,12},{12,8},{9,1... | collective-permute-start | bytes 245768 | tf_op jit(solution)/shard_map/ppermute | solution.py:494
  42.8 5.1 %collective-permute-start.21 = (f32[5,16,256]{2,1,0:T(8,128)S(1)}, f32[5,16,256]{2,1,0:T(8,128)S(1)}, u32[]{:S(2)}, u32[]{:S(2)}) collective-permute-start(f32[5,16,256]{2,1,0:T(8,128)S(1)} %get-tuple-element.103), channel_id=1, source_target_pairs={{4,8},{8,4},{5,9},{9,5},{6,10},{10,6},{7,11},{11,7},{12,16},{16,12... | collective-permute-start | bytes 245768 | tf_op jit(solution)/shard_map/ppermute | solution.py:494
  45.5 4.8 %collective-permute-start.22 = (f32[5,16,256]{2,1,0:T(8,128)S(1)}, f32[5,16,256]{2,1,0:T(8,128)S(1)}, u32[]{:S(2)}, u32[]{:S(2)}) collective-permute-start(f32[5,16,256]{2,1,0:T(8,128)S(1)} %get-tuple-element.104), channel_id=1, source_target_pairs={{0,1},{1,0},{2,3},{3,2},{4,5},{5,4},{6,7},{7,6},{8,9},{9,8},{10,11... | collective-permute-start | bytes 245768 | tf_op jit(solution)/shard_map/ppermute | solution.py:494
  45.7 4.6 %collective-permute-start.23 = (f32[5,16,256]{2,1,0:T(8,128)S(1)}, f32[5,16,256]{2,1,0:T(8,128)S(1)}, u32[]{:S(2)}, u32[]{:S(2)}) collective-permute-start(f32[5,16,256]{2,1,0:T(8,128)S(1)} %get-tuple-element.105), channel_id=1, source_target_pairs={{1,2},{2,1},{5,6},{6,5},{9,10},{10,9},{13,14},{14,13},{17,18},{18,... | collective-permute-start | bytes 245768 | tf_op jit(solution)/shard_map/ppermute | solution.py:494
  50.7 3.9 %collective-permute-start.24 = (f32[5,16,256]{2,1,0:T(8,128)S(1)}, f32[5,16,256]{2,1,0:T(8,128)S(1)}, u32[]{:S(2)}, u32[]{:S(2)}) collective-permute-start(f32[5,16,256]{2,1,0:T(8,128)S(1)} %get-tuple-element.107), channel_id=1, source_target_pairs={{0,4},{4,0},{1,5},{5,1},{2,6},{6,2},{3,7},{7,3},{8,12},{12,8},{9,1... | collective-permute-start | bytes 245768 | tf_op jit(solution)/shard_map/ppermute | solution.py:494
  50.8 5.6 %collective-permute-start.25 = (f32[5,16,256]{2,1,0:T(8,128)S(1)}, f32[5,16,256]{2,1,0:T(8,128)S(1)}, u32[]{:S(2)}, u32[]{:S(2)}) collective-permute-start(f32[5,16,256]{2,1,0:T(8,128)S(1)} %get-tuple-element.108), channel_id=1, source_target_pairs={{4,8},{8,4},{5,9},{9,5},{6,10},{10,6},{7,11},{11,7},{12,16},{16,12... | collective-permute-start | bytes 245768 | tf_op jit(solution)/shard_map/ppermute | solution.py:494
  53.5 4.4 %collective-permute-start.26 = (f32[5,16,256]{2,1,0:T(8,128)S(1)}, f32[5,16,256]{2,1,0:T(8,128)S(1)}, u32[]{:S(2)}, u32[]{:S(2)}) collective-permute-start(f32[5,16,256]{2,1,0:T(8,128)S(1)} %get-tuple-element.109), channel_id=1, source_target_pairs={{0,1},{1,0},{2,3},{3,2},{4,5},{5,4},{6,7},{7,6},{8,9},{9,8},{10,11... | collective-permute-start | bytes 245768 | tf_op jit(solution)/shard_map/ppermute | solution.py:494
  53.5 4.4 %collective-permute-start.27 = (f32[5,16,256]{2,1,0:T(8,128)S(1)}, f32[5,16,256]{2,1,0:T(8,128)S(1)}, u32[]{:S(2)}, u32[]{:S(2)}) collective-permute-start(f32[5,16,256]{2,1,0:T(8,128)S(1)} %get-tuple-element.110), channel_id=1, source_target_pairs={{1,2},{2,1},{5,6},{6,5},{9,10},{10,9},{13,14},{14,13},{17,18},{18,... | collective-permute-start | bytes 245768 | tf_op jit(solution)/shard_map/ppermute | solution.py:494
  58.1 4.2 %collective-permute-start.28 = (f32[5,16,256]{2,1,0:T(8,128)S(1)}, f32[5,16,256]{2,1,0:T(8,128)S(1)}, u32[]{:S(2)}, u32[]{:S(2)}) collective-permute-start(f32[5,16,256]{2,1,0:T(8,128)S(1)} %get-tuple-element.115), channel_id=1, source_target_pairs={{0,4},{4,0},{1,5},{5,1},{2,6},{6,2},{3,7},{7,3},{8,12},{12,8},{9,1... | collective-permute-start | bytes 245768 | tf_op jit(solution)/shard_map/ppermute | solution.py:494
  58.2 5.7 %collective-permute-start.29 = (f32[5,16,256]{2,1,0:T(8,128)S(1)}, f32[5,16,256]{2,1,0:T(8,128)S(1)}, u32[]{:S(2)}, u32[]{:S(2)}) collective-permute-start(f32[5,16,256]{2,1,0:T(8,128)S(1)} %get-tuple-element.116), channel_id=1, source_target_pairs={{4,8},{8,4},{5,9},{9,5},{6,10},{10,6},{7,11},{11,7},{12,16},{16,12... | collective-permute-start | bytes 245768 | tf_op jit(solution)/shard_map/ppermute | solution.py:494
  61.1 4.4 %collective-permute-start.30 = (f32[5,16,256]{2,1,0:T(8,128)S(1)}, f32[5,16,256]{2,1,0:T(8,128)S(1)}, u32[]{:S(2)}, u32[]{:S(2)}) collective-permute-start(f32[5,16,256]{2,1,0:T(8,128)S(1)} %get-tuple-element.117), channel_id=1, source_target_pairs={{0,1},{1,0},{2,3},{3,2},{4,5},{5,4},{6,7},{7,6},{8,9},{9,8},{10,11... | collective-permute-start | bytes 245768 | tf_op jit(solution)/shard_map/ppermute | solution.py:494
  61.3 4.2 %collective-permute-start.31 = (f32[5,16,256]{2,1,0:T(8,128)S(1)}, f32[5,16,256]{2,1,0:T(8,128)S(1)}, u32[]{:S(2)}, u32[]{:S(2)}) collective-permute-start(f32[5,16,256]{2,1,0:T(8,128)S(1)} %get-tuple-element.118), channel_id=1, source_target_pairs={{1,2},{2,1},{5,6},{6,5},{9,10},{10,9},{13,14},{14,13},{17,18},{18,... | collective-permute-start | bytes 245768 | tf_op jit(solution)/shard_map/ppermute | solution.py:494
  66.1 5.7 %collective-permute-start.32 = (f32[16,128]{1,0:T(8,128)S(1)}, f32[16,128]{1,0:T(8,128)S(1)}, u32[]{:S(2)}, u32[]{:S(2)}) collective-permute-start(f32[16,128]{1,0:T(8,128)S(1)} %get-tuple-element.121), channel_id=1, source_target_pairs={{0,1},{1,0},{2,3},{3,2},{4,5},{5,4},{6,7},{7,6},{8,9},{9,8},{10,11... | collective-permute-start | bytes 24584 | tf_op jit(solution)/shard_map/ppermute | solution.py:499
  69.1 3.7 %collective-permute-start.33 = (f32[16,128]{1,0:T(8,128)S(1)}, f32[16,128]{1,0:T(8,128)S(1)}, u32[]{:S(2)}, u32[]{:S(2)}) collective-permute-start(f32[16,128]{1,0:T(8,128)S(1)} %get-tuple-element.122), channel_id=1, source_target_pairs={{0,2},{1,3},{2,0},{3,1},{4,6},{5,7},{6,4},{7,5},{8,10},{9,11},{10,... | collective-permute-start | bytes 24584 | tf_op jit(solution)/shard_map/ppermute | solution.py:499
  69.3 4.5 %collective-permute-start.34 = (f32[16,128]{1,0:T(8,128)S(1)}, f32[16,128]{1,0:T(8,128)S(1)}, u32[]{:S(2)}, u32[]{:S(2)}) collective-permute-start(f32[16,128]{1,0:T(8,128)S(1)} %get-tuple-element.123), channel_id=1, source_target_pairs={{0,3},{1,2},{2,1},{3,0},{4,7},{5,6},{6,5},{7,4},{8,11},{9,10},{10,... | collective-permute-start | bytes 24584 | tf_op jit(solution)/shard_map/ppermute | solution.py:499
  (6 other events, 32.1 us)
